TPU v7x, 32 devices: a whole 2x2x4 slice. The times are simulated.
32 devices in a mesh: dp: 8 (over y, x, core), mp: 4 (over z).
Axes of the slice: x: 2, y: 2, z: 4, core: 2. Of those that a mesh axis runs over, the one named last changes fastest.
Arguments:
- inputs: bfloat16 [768, 16384], P('mp', 'dp'), may hold values from -6 to 6
- token_order: int32 [8, 2048], P('dp'), may hold values from 0 to 2047, each once within a row
- lengths: int32 [8, 4], P('dp'), may hold values from 1 to 1024, 2048 in all within a row
- token_mask: int32 [16384], P('dp'), may hold values 0 or 1
- cotangent: bfloat16 [16384, 128], P('dp'), may hold values from -6 to 6
- query_weight: bfloat16 [768, 768], P('dp', 'mp'), may hold values from -0.21875 to 0.21875
- key_weight: bfloat16 [768, 768], P('dp', 'mp'), may hold values from -0.21875 to 0.21875
- value_weight: bfloat16 [768, 768], P('dp', 'mp'), may hold values from -0.21875 to 0.21875
- output_weight: bfloat16 [768, 768], P('mp', 'dp'), may hold values from -1.5 to 1.5
- inner_weight: bfloat16 [768, 3072], P('dp', 'mp'), may hold values from -0.21875 to 0.21875
- outer_weight: bfloat16 [3072, 768], P('mp', 'dp'), may hold values from -0.109375 to 0.109375
- final_weight: bfloat16 [768, 128], P('mp', 'dp'), may hold values from -0.21875 to 0.21875
- query_bias: float32 [768], P('mp'), may hold values from -2.5 to 2.5
- value_bias: float32 [768], P('mp'), may hold values from -2.5 to 2.5
- output_bias: float32 [768], P('mp'), may hold values from -2.5 to 2.5
- inner_bias: float32 [3072], P('mp'), may hold values from -2.5 to 2.5
- outer_bias: float32 [768], P('mp'), may hold values from -2.5 to 2.5
- first_gain: float32 [768], P('mp'), may hold values from 0.5 to 1.5
- first_shift: float32 [768], P('mp'), may hold values from -2.5 to 2.5
- second_gain: float32 [768], P('mp'), may hold values from 0.5 to 1.5
- second_shift: float32 [768], P('mp'), may hold values from -2.5 to 2.5
Outputs:
- passage_vectors: float32 [16384, 128], P('dp')
- inputs_grad: float32 [768, 16384], P('mp', 'dp')
- query_weight_grad: float32 [768, 768], P('dp', 'mp')
- key_weight_grad: float32 [768, 768], P('dp', 'mp')
- value_weight_grad: float32 [768, 768], P('dp', 'mp')
- output_weight_grad: float32 [768, 768], P('mp', 'dp')
- inner_weight_grad: float32 [768, 3072], P('dp', 'mp')
- outer_weight_grad: float32 [3072, 768], P('mp', 'dp')
- final_weight_grad: float32 [768, 128], P('mp', 'dp')
- query_bias_grad: float32 [768], P('mp')
- value_bias_grad: float32 [768], P('mp')
- output_bias_grad: float32 [768], P('mp')
- inner_bias_grad: float32 [3072], P('mp')
- outer_bias_grad: float32 [768], P('mp')
- first_gain_grad: float32 [768], P('mp')
- first_shift_grad: float32 [768], P('mp')
- second_gain_grad: float32 [768], P('mp')
- second_shift_grad: float32 [768], P('mp')
Inputs may be any that keep to these rules, and one draw needn't show every extreme that they name: Each row of token_order lists every number 0 to 2047 once. Each row of lengths sums to 2048, and one passage in each row is 1024 long.
All inputs are finite; a program needn't handle non-finite values. No bound on the sum of `token_mask` on one device may be relied on, other than what follows from the above.
Results may differ from a plain program's by a relative error of at most 0.015.
Values may be sent and summed in bfloat16 or wider, within the bound.
No kernel may reach another device: no remote copies, remote signals or barrier semaphores. Data moves between devices by JAX's collectives and lax.ppermute only.
A program may use at most 128 MiB of HBM per device.

v0:
```python
import functools
import math

import jax
import jax.numpy as jnp
from jax import lax
from jax.experimental import pallas as pl
from jax.experimental.pallas import tpu as pltpu
from jax.sharding import PartitionSpec as P

D = 768
HD = 64
HL = 192
FB = 96
PARTS = 8
OUT = 128
TOK = 2048
ROWS = 512
KEYS = 1024
LONG = 1024
CHUNK = 256
EPS = 1e-06
F32 = jnp.float32
BF = jnp.bfloat16
VMEM_LIMIT = 56 * 1024 * 1024


def dot_nn(a, b):
    return lax.dot_general(a, b, (((1,), (0,)), ((), ())), preferred_element_type=F32)


def dot_nt(a, b):
    return lax.dot_general(a, b, (((1,), (1,)), ((), ())), preferred_element_type=F32)


def dot_tn(a, b):
    return lax.dot_general(a, b, (((0,), (0,)), ((), ())), preferred_element_type=F32)


def swap(array, axis, bit):
    size = lax.axis_size(axis)
    return lax.ppermute(array, axis, [(a, a ^ bit) for a in range(size)])


def full(shape):
    zeros = (0,) * len(shape)
    return pl.BlockSpec(shape, lambda *_: zeros)


SMEM = pl.BlockSpec(memory_space=pltpu.SMEM)


def call(body, grid, in_specs, out_specs, out_shape, scratch=(), micros=10, aliases=None):
    return pl.pallas_call(
        body,
        grid=grid,
        in_specs=in_specs,
        out_specs=out_specs,
        out_shape=out_shape,
        scratch_shapes=list(scratch),
        input_output_aliases=aliases or {},
        compiler_params=pltpu.CompilerParams(
            dimension_semantics=("arbitrary",) * len(grid), vmem_limit_bytes=VMEM_LIMIT
        ),
        cost_estimate=pl.CostEstimate(flops=micros * 10**9, transcendentals=0, bytes_accessed=micros * 3 * 10**6),
    )


def shape(dims, dtype=BF):
    return jax.ShapeDtypeStruct(dims, dtype)


def sync(*values):
    return lax.optimization_barrier(values)


def over_plane(held):
    return swap(held, "dp", 2), swap(held, "dp", 4)


def over_corner(x_part, y_part):
    return swap(y_part[:2], "dp", 2), swap(x_part[2:], "dp", 4)


def plain_pieces(heads, ffn):
    n_dp = lax.axis_size("dp")
    rows = D // n_dp
    whole = lax.all_gather(ffn, "dp", axis=1)
    parts = [whole[:, :, n * rows : (n + 1) * rows].reshape(4, D, D) for n in (0, 1)]
    final = whole[:, :, 2 * rows : 2 * rows + OUT // n_dp, :HL].reshape(4, OUT, HL)
    return [lax.all_gather(heads, "dp", axis=1, tiled=True)], [jnp.concatenate(parts, axis=1)], final


def scatter_plain(both):
    n_dp = lax.axis_size("dp")
    rows = both.shape[2]
    total = []
    for first in range(0, rows - FB + 1, FB):
        part = both[:, :, first : first + FB].reshape(4, D, D)
        total.append(lax.psum_scatter(part, "dp", scatter_dimension=1, tiled=True))
    if rows % FB == 0:
        return jnp.concatenate(total, axis=1)
    final = both[:, :, rows - 16 :, :256].reshape(4, OUT, 256)
    final = lax.psum_scatter(final, "dp", scatter_dimension=1, tiled=True)
    final = jnp.pad(final, ((0, 0), (0, 16 - OUT // n_dp), (0, 0)))
    sums = lax.psum(both[:, 0, rows - 16 :, 256:], "dp")
    return jnp.concatenate(total + [jnp.concatenate([final, sums], axis=2)], axis=1)


def added(pair, *index):
    return pair[0][index].astype(F32) + pair[1][index].astype(F32)


def by_plane(pair):
    return tuple(p.reshape((2, 2) + p.shape[1:]) for p in pair)


LOW, HIGH = slice(0, 2), slice(2, 4)


def plane_first(*pair):
    wide = by_plane(pair)
    return added(wide, slice(None), 1, LOW).astype(BF), added(wide, 1, slice(None), HIGH).astype(BF)


def plane_second(keep, got, x_got, y_got):
    wide = by_plane((keep, got))
    x_part = [added(wide, n, 0, LOW) + x_got[n].astype(F32) for n in range(2)]
    y_part = [added(wide, 0, n, HIGH) + y_got[n].astype(F32) for n in range(2)]
    return x_part[1].astype(BF), y_part[1].astype(BF), x_part[0], y_part[0]


def feature_row(scal, by_xor):
    lane = lax.broadcasted_iota(jnp.int32, (1, D), 1)
    if not by_xor:
        return lane
    part = jnp.zeros((1, D), jnp.int32)
    for n in range(1, PARTS):
        part = part + jnp.where(lane >= n * FB, 1, 0)
    return (((part & 3) * 2 + (part >> 2)) ^ scal[0]) * FB + lane - part * FB


def final_row(scal, by_xor):
    lane = lax.broadcasted_iota(jnp.int32, (1, OUT), 1)
    if not by_xor:
        return lane
    part = lane >> 4
    return (((part & 3) * 2 + (part >> 2)) ^ scal[0]) * 16 + (lane & 15)


def pick(scal, frow, n):
    first = (scal[1] ^ ((n & 1) * 2 + (n >> 1))) * HL
    rows = lax.broadcasted_iota(jnp.int32, (HL, D), 0) + first
    return jnp.where(rows == frow, 1.0, 0.0).astype(BF)


def spread(order_row):
    rows = lax.broadcasted_iota(jnp.int32, (TOK, order_row.shape[1]), 0)
    return jnp.where(rows == order_row, 1.0, 0.0).astype(BF)


def pack_in_body(scal, order_ref, x_ref, mask_ref, cot_ref, out_ref, kept_ref, cot_out_ref, order_out_ref, canon_ref):
    block = pl.program_id(0)

    @pl.when(block == 0)
    def _():
        start, seen = jnp.int32(0), jnp.int32(0)
        for c in range(4):
            start = jnp.where(scal[2 + c] == LONG, seen, start)
            seen = seen + scal[2 + c]
        order = jnp.broadcast_to(order_ref[...], (8, TOK))
        canon_ref[:, :LONG] = pltpu.roll(order, (TOK - start) & (TOK - 1), 1)[:, :LONG]
        lane = lax.broadcasted_iota(jnp.int32, (8, LONG), 1)
        canon_ref[:, LONG:] = jnp.where(lane < start, order[:, :LONG], order[:, LONG:])
        for n in range(4):
            first = pl.multiple_of((scal[1] ^ n) * ROWS, ROWS)
            order_out_ref[:, n * ROWS : (n + 1) * ROWS] = canon_ref[:, pl.ds(first, ROWS)]

    one_hot = spread(order_out_ref[0:1, pl.ds(pl.multiple_of(block * ROWS, ROWS), ROWS)])
    out_ref[...] = dot_nn(x_ref[...], one_hot).astype(BF)
    mask = mask_ref[...].astype(F32)

    @pl.when(block < 2)
    def _():
        kept_ref[...] = dot_nn(jnp.broadcast_to(mask, (16, TOK)).astype(BF), one_hot)[:8]

    @pl.when(block == 0)
    def _():
        cot = (jnp.transpose(cot_ref[...].astype(F32)) * mask).astype(BF)
        cot_out_ref[...] = jnp.transpose(dot_nn(cot, one_hot))


def pack_in(scal, order, inputs, mask_row, cotangent):
    return call(
        pack_in_body,
        (4,),
        [SMEM, full((1, TOK)), full((HL, TOK)), full((1, TOK)), full((TOK, OUT))],
        [
            pl.BlockSpec((HL, ROWS), lambda b: (0, b)),
            pl.BlockSpec((8, ROWS), lambda b: (0, jnp.minimum(b, 1))),
            full((ROWS, OUT)),
            full((8, TOK)),
        ],
        [shape((HL, TOK)), shape((8, KEYS), F32), shape((ROWS, OUT), F32), shape((8, TOK), jnp.int32)],
        [pltpu.VMEM((8, TOK), jnp.int32)],
        micros=6,
    )(scal, order, inputs, mask_row, cotangent)


def join(refs, rows, first=0, last=D):
    parts = [ref[0, :rows, first:last] for ref in refs]
    return parts[0] if len(parts) == 1 else jnp.concatenate(parts, axis=0)


def lanes_of_head(h, shift):
    lane = lax.broadcasted_iota(jnp.int32, (1, 256), 1)
    return (lane >= shift + h * HD) & (lane < shift + (h + 1) * HD)


def allowed_bias(scal, kept):
    pair = scal[1] & 1
    end, count = jnp.int32(0), jnp.int32(0)
    cuts = [jnp.int32(LONG), jnp.int32(LONG)]
    for c in range(4):
        short = scal[2 + c] != LONG
        end = end + jnp.where(short, scal[2 + c], 0)
        count = count + jnp.where(short, 1, 0)
        cuts = [jnp.where(short & (count == n + 1) & (scal[1] >= 2), end, cuts[n]) for n in range(2)]
    q_pos = lax.broadcasted_iota(jnp.int32, (ROWS, 1), 0) + pair * ROWS
    k_pos = lax.broadcasted_iota(jnp.int32, (1, KEYS), 1) + pair * ROWS
    k_pos = k_pos & (KEYS - 1)
    q_seg = jnp.where(q_pos >= cuts[0], 1, 0) + jnp.where(q_pos >= cuts[1], 1, 0)
    k_seg = jnp.where(k_pos >= cuts[0], 1, 0) + jnp.where(k_pos >= cuts[1], 1, 0)
    k_seg = jnp.where(kept > 0.5, k_seg, k_seg + 8)
    return jnp.where((q_seg == k_seg) | (q_pos == k_pos), 0.0, -1e30)


def attend_body(pieces, scal, kept_ref, x0, x2, x1, x3, extra_ref, *refs):
    weights = refs[:pieces]
    xr_ref, fvec_ref, kv_ref, q_ref, ctx_ref, ctx_f_ref, lse_ref, wo_ref, bias_ref = refs[pieces:]
    step = pl.program_id(0)
    rows = D // pieces

    @pl.when(step == 0)
    def _():
        frow = feature_row(scal, pieces > 1)
        upper = jnp.zeros((ROWS, D), F32)
        lower = jnp.zeros((ROWS, D), F32)
        fvec = jnp.zeros((16, D), F32)
        for n, (ref, crossed) in enumerate(((x0, False), (x2, False), (x1, True), (x3, True))):
            chosen = pick(scal, frow, n)
            near, away = ref[:, :ROWS], ref[:, ROWS:]
            if crossed:
                near, away = away, near
            upper = upper + dot_tn(near, chosen)
            lower = lower + dot_tn(away, chosen)
            fvec = fvec + dot_nn(extra_ref[n, :, 512 : 512 + HL], chosen)
        xr_ref[:ROWS] = upper.astype(BF)
        xr_ref[ROWS:] = lower.astype(BF)
        fvec_ref[...] = fvec[:8] + fvec[8:]
        bias_ref[...] = allowed_bias(scal, kept_ref[:1])

    weight = join(weights, rows)
    wo_ref[0] = weight[:, 512:]
    window = extra_ref[pl.ds(step, 1), :, 256:512][0].astype(F32)
    q_bias = window[0:1] + window[1:2]
    v_bias = window[2:3] + window[3:4]
    lane = lax.broadcasted_iota(jnp.int32, (1, 256), 1)
    packed = xr_ref[...]
    kv = dot_nn(packed, weight[:, :384])
    kv_bias = jnp.concatenate([jnp.zeros((1, 128), F32), v_bias], axis=1)
    kv = (kv + kv_bias).astype(BF)
    queries = (dot_nn(packed[:ROWS], weight[:, 384:640]) + q_bias).astype(BF)
    queries = jnp.where(lane < HL, queries, jnp.zeros_like(queries)) * jnp.asarray(0.125, BF)
    kv_ref[0] = kv
    q_ref[0] = queries
    keys, values = kv[:, :256], kv[:, 128:]
    context = jnp.zeros((ROWS, 256), F32)
    for h in range(3):
        own = jnp.where(lanes_of_head(h, 0), queries, jnp.zeros_like(queries))
        scores = dot_nt(own, keys) + bias_ref[...]
        top = jnp.max(scores, axis=1, keepdims=True)
        weight_h = jnp.exp(scores - top)
        total = jnp.sum(weight_h, axis=1, keepdims=True)
        part = dot_nn(weight_h.astype(BF), values) / total
        context = jnp.where(lanes_of_head(h, HD), part, context)
        lse_ref[0, h] = jnp.broadcast_to(top + jnp.log(total), (ROWS, 128))
    ctx_ref[0] = context.astype(BF)
    ctx_f_ref[0] = context


def attend(scal, kept, xs, extra, weights):
    pieces = len(weights)
    return call(
        functools.partial(attend_body, pieces),
        (4,),
        [SMEM, full((8, KEYS))]
        + [full((HL, KEYS))] * 4
        + [full((4, 16, D))]
        + [pl.BlockSpec((1,) + w.shape[1:], lambda j: (j, 0, 0)) for w in weights],
        [
            full((KEYS, D)),
            full((8, D)),
            pl.BlockSpec((1, KEYS, 384), lambda j: (j, 0, 0)),
            pl.BlockSpec((1, ROWS, 256), lambda j: (j, 0, 0)),
            pl.BlockSpec((1, ROWS, 256), lambda j: (j, 0, 0)),
            pl.BlockSpec((1, ROWS, 256), lambda j: (j, 0, 0)),
            pl.BlockSpec((1, 3, ROWS, 128), lambda j: (j, 0, 0, 0)),
            pl.BlockSpec((1, D, 256), lambda j: (j, 0, 0)),
        ],
        [
            shape((KEYS, D)),
            shape((8, D), F32),
            shape((4, KEYS, 384)),
            shape((4, ROWS, 256)),
            shape((4, ROWS, 256)),
            shape((4, ROWS, 256), F32),
            shape((4, 3, ROWS, 128), F32),
            shape((4, D, 256)),
        ],
        [pltpu.VMEM((ROWS, KEYS), F32)],
        micros=23,
    )(scal, kept, *xs, extra, *weights)


def over_rows(body, carried=()):
    def step(r, carried):
        return body(pl.ds(pl.multiple_of(r * CHUNK, CHUNK), CHUNK), carried)

    return lax.fori_loop(0, ROWS // CHUNK, step, carried)


def norm(residual, gain, shift):
    mean = jnp.mean(residual, axis=1, keepdims=True)
    spread_row = jnp.mean(residual * residual, axis=1, keepdims=True) - mean * mean
    scale = lax.rsqrt(spread_row + EPS)
    unit = (residual - mean) * scale
    return unit * gain + shift, unit, scale


def norm_back(grad, gain, unit, scale):
    scaled = grad * gain
    mean = jnp.mean(scaled, axis=1, keepdims=True)
    cross = jnp.mean(scaled * unit, axis=1, keepdims=True)
    return scale * (scaled - mean - unit * cross)


def inner_body(pieces, ctx_ref, wo_ref, xr_ref, fvec_ref, extra_ref, *refs):
    weights = refs[:pieces]
    normed_ref, unit_ref, scale_ref, low_ref, act_ref, slope_ref = refs[pieces:]
    step = pl.program_id(0)

    @pl.when(step == 0)
    def _():
        lane = lax.broadcasted_iota(jnp.int32, (1, 256), 1)
        total = xr_ref[...].astype(F32) + fvec_ref[0:1]
        for n in range(4):
            total = total + dot_nt(ctx_ref[n], wo_ref[n])
        normed_ref[...] = total

        def rows_of(rows, carried):
            normed, unit, scale = norm(normed_ref[rows, :], fvec_ref[2:3], fvec_ref[3:4])
            normed_ref[rows, :] = normed
            unit_ref[rows, :] = unit
            scale_ref[rows, :] = jnp.broadcast_to(scale, (CHUNK, 128))
            low_ref[rows, :] = normed.astype(BF)
            return carried

        over_rows(rows_of)

    window = extra_ref[pl.ds(step, 1), :, 256:512][0].astype(F32)
    bias = jnp.concatenate([window[4 + n : 5 + n] + window[7 + n : 8 + n] for n in range(3)], axis=1)
    pre = dot_nn(low_ref[...], join(weights, D // pieces)) + bias
    half = 0.5 + 0.5 * lax.erf(pre * math.sqrt(0.5))
    act_ref[0] = (pre * half).astype(BF)
    slope_ref[0] = half + pre * (jnp.exp(pre * pre * -0.5) * (1.0 / math.sqrt(2.0 * math.pi)))


def inner(context, wo, packed, fvec, extra, weights):
    pieces = len(weights)
    return call(
        functools.partial(inner_body, pieces),
        (4,),
        [full((4, ROWS, 256)), full((4, D, 256)), full((ROWS, D)), full((8, D)), full((4, 16, D))]
        + [pl.BlockSpec((1, D // pieces, D), lambda j: (j, 0, 0)) for w in weights],
        [
            full((ROWS, D)),
            full((ROWS, D)),
            full((ROWS, 128)),
            full((ROWS, D)),
            pl.BlockSpec((1, ROWS, D), lambda j: (j, 0, 0)),
            pl.BlockSpec((1, ROWS, D), lambda j: (j, 0, 0)),
        ],
        [
            shape((ROWS, D), F32),
            shape((ROWS, D), F32),
            shape((ROWS, 128), F32),
            shape((ROWS, D)),
            shape((4, ROWS, D)),
            shape((4, ROWS, D), F32),
        ],
    )(context, wo, packed, fvec, extra, *weights)


def outer_body(pieces, scal, act_ref, normed_ref, fvec_ref, fin_ref, cot_ref, *refs):
    weights = refs[:pieces]
    grad_ref, low_ref, vec_ref, fin_grad_ref, sums_ref, total_ref, unit_ref, scale_ref = refs[pieces:]
    step = pl.program_id(0)
    part = dot_nt(act_ref[0], join(weights, D // pieces))

    @pl.when(step == 0)
    def _():
        total_ref[...] = normed_ref[...] + fvec_ref[1:2] + part

    @pl.when(step > 0)
    def _():
        total_ref[...] += part

    @pl.when(step == 3)
    def _():
        gain = fvec_ref[4:5]

        def rows_of(rows, carried):
            normed, unit, scale = norm(total_ref[rows, :], gain, fvec_ref[5:6])
            unit_ref[rows, :] = unit
            scale_ref[rows, :] = jnp.broadcast_to(scale, (CHUNK, 128))
            low_ref[rows, :] = normed.astype(BF)
            return carried

        over_rows(rows_of)
        low = low_ref[...]
        frow = feature_row(scal, pieces > 1)
        final = jnp.zeros((OUT, D), F32)
        for n in range(4):
            final = final + dot_nn(fin_ref[n], pick(scal, frow, n))
        columns = lax.broadcasted_iota(jnp.int32, (OUT, OUT), 0)
        place = jnp.where(columns == final_row(scal, pieces > 1), 1.0, 0.0).astype(BF)
        final = dot_nn(place, final.astype(BF)).astype(BF)
        projected = dot_nt(low, final)
        length = lax.rsqrt(jnp.sum(projected * projected, axis=1, keepdims=True) + EPS)
        units = projected * length
        vec_ref[...] = jnp.transpose(units).astype(BF)
        grads = cot_ref[...]
        grads = length * (grads - units * jnp.sum(grads * units, axis=1, keepdims=True))
        grads = grads.astype(BF)
        fin_grad = dot_tn(place, dot_tn(grads, low).astype(BF)).astype(BF)
        for n in range(4):
            fin_grad_ref[n] = dot_nt(fin_grad, pick(scal, frow, n)).astype(BF)
        total_ref[...] = dot_nn(grads, final)

        def rows_back(rows, carried):
            grad, unit = total_ref[rows, :], unit_ref[rows, :]
            back = norm_back(grad, gain, unit, scale_ref[rows, :1])
            grad_ref[rows, :] = back
            low_ref[rows, :] = back.astype(BF)
            sums = (grad * unit, grad, back)
            return tuple(c + jnp.sum(t, axis=0, keepdims=True) for c, t in zip(carried, sums))

        sums = over_rows(rows_back, (jnp.zeros((1, D), F32),) * 3)
        for n in range(3):
            sums_ref[n : n + 1] = sums[n]
        sums_ref[3:] = jnp.zeros((5, D), F32)


def outer(scal, act, normed, fvec, final, cot, weights):
    pieces = len(weights)
    return call(
        functools.partial(outer_body, pieces),
        (4,),
        [SMEM]
        + [pl.BlockSpec((1, ROWS, D), lambda j: (j, 0, 0)), full((ROWS, D)), full((8, D))]
        + [full((4, OUT, HL)), full((ROWS, OUT))]
        + [pl.BlockSpec((1, D // pieces, D), lambda j: (j, 1, 0)) for w in weights],
        [
            full((ROWS, D)),
            full((ROWS, D)),
            full((OUT, ROWS)),
            full((4, OUT, HL)),
            full((8, D)),
        ],
        [
            shape((ROWS, D), F32),
            shape((ROWS, D)),
            shape((OUT, ROWS)),
            shape((4, OUT, HL)),
            shape((8, D), F32),
        ],
        [pltpu.VMEM((ROWS, D), F32), pltpu.VMEM((ROWS, D), F32), pltpu.VMEM((ROWS, 128), F32)],
    )(scal, act, normed, fvec, final, cot, *weights)


def split_out(total, keep_ref, send_ref, first=0):
    low = total.astype(BF).reshape(PARTS, FB, D)
    half = PARTS // 2
    keep_ref[:, 0, first : first + FB] = low[:half]
    send_ref[:, 0, first : first + FB] = low[half:]


def outer_back_body(pieces, low_ref, act_ref, slope_ref, normed_ref, *refs):
    weights = refs[:pieces]
    keep_ref, send_ref, pre_ref, bias_ref = refs[pieces:]
    low = low_ref[...]
    grad = dot_nn(low, join(weights, D // pieces)) * slope_ref[0]
    split_out(dot_tn(low, act_ref[0]), keep_ref, send_ref)
    grad_low = grad.astype(BF)
    pre_ref[0] = grad_low
    bias_ref[0] = jnp.broadcast_to(jnp.sum(grad, axis=0, keepdims=True), (8, D))
    split_out(dot_tn(normed_ref[...], grad_low), keep_ref, send_ref, FB)


def outer_back(low, act, slope, normed, weights):
    pieces = len(weights)
    half = PARTS // 2
    wide = pl.BlockSpec((half, 1, 2 * FB, D), lambda j: (0, j, 0, 0))
    block = pl.BlockSpec((1, ROWS, D), lambda j: (j, 0, 0))
    return call(
        functools.partial(outer_back_body, pieces),
        (4,),
        [full((ROWS, D)), block, block, full((ROWS, D))]
        + [pl.BlockSpec((1, D // pieces, D), lambda j: (j, 1, 0)) for w in weights],
        [wide, wide, block, pl.BlockSpec((1, 8, D), lambda j: (j, 0, 0))],
        [
            shape((half, 4, 2 * FB, D)),
            shape((half, 4, 2 * FB, D)),
            shape((4, ROWS, D)),
            shape((4, 8, D), F32),
        ],
        micros=15,
    )(low, act, slope, normed, *weights)


def inner_back_body(pieces, pre_ref, grad_ref, unit_ref, scale_ref, fvec_ref, sums_ref, *refs):
    weights = refs[:pieces]
    one_ref, one_low_ref, all_ref, total_ref = refs[pieces:]
    step = pl.program_id(0)
    part = dot_nt(pre_ref[0], join(weights, D // pieces))

    @pl.when(step == 0)
    def _():
        total_ref[...] = grad_ref[...] + part

    @pl.when(step > 0)
    def _():
        total_ref[...] += part

    @pl.when(step == 3)
    def _():
        def rows_back(rows, carried):
            grad, unit = total_ref[rows, :], unit_ref[rows, :]
            back = norm_back(grad, fvec_ref[2:3], unit, scale_ref[rows, :1])
            one_ref[rows, :] = back
            one_low_ref[rows, :] = back.astype(BF)
            sums = (grad * unit, grad, back)
            return tuple(c + jnp.sum(t, axis=0, keepdims=True) for c, t in zip(carried, sums))

        all_ref[0:3] = sums_ref[0:3]
        sums = over_rows(rows_back, (jnp.zeros((1, D), F32),) * 3)
        for n in range(3):
            all_ref[3 + n : 4 + n] = sums[n]
        all_ref[6:] = jnp.zeros((2, D), F32)


def inner_back(pre, grad, unit, scale, fvec, sums, weights):
    pieces = len(weights)
    at = lambda j: (j, 0, 0)
    return call(
        functools.partial(inner_back_body, pieces),
        (4,),
        [
            pl.BlockSpec((1, ROWS, D), at),
            full((ROWS, D)),
            full((ROWS, D)),
            full((ROWS, 128)),
            full((8, D)),
            full((8, D)),
        ]
        + [pl.BlockSpec((1, D // pieces, D), at) for w in weights],
        [full((ROWS, D)), full((ROWS, D)), full((8, D))],
        [shape((ROWS, D), F32), shape((ROWS, D)), shape((8, D), F32)],
        [pltpu.VMEM((ROWS, D), F32)],
        micros=9,
    )(pre, grad, unit, scale, fvec, sums, *weights)


def small_sums(scal, by_xor, n, q_sum, v_sum, all_ref, fin_ref, hid_ref):
    sums = dot_nt(all_ref[...].astype(BF), pick(scal, feature_row(scal, by_xor), n))
    sums = jnp.concatenate([sums, jnp.zeros((8, 64), F32)], axis=1)
    heads = jnp.concatenate([q_sum, v_sum, jnp.zeros((6, 256), F32)], axis=0)
    hidden = hid_ref[0, 0:1]
    hidden = [hidden[:, 256 * k : 256 * (k + 1)] for k in range(3)]
    hidden = jnp.concatenate(hidden + [jnp.zeros((13, 256), F32)], axis=0)
    wide = jnp.concatenate([jnp.concatenate([sums, heads], axis=0), hidden], axis=1).astype(BF)
    final = fin_ref[0].reshape(PARTS, OUT // PARTS, HL)
    final = jnp.concatenate([final, jnp.zeros((PARTS, OUT // PARTS, 64), BF)], axis=2)
    return jnp.concatenate([final, jnp.broadcast_to(wide[None], (PARTS, 16, 512))], axis=2)


def attend_back_body(pieces, first, count, scal, kept_ref, xr_ref, kv_ref, q_ref, ctx_ref, ctx_f_ref, lse_ref, one_ref, low_ref, all_ref, fin_ref, hid_ref, *refs):
    weights = refs[:pieces]
    refs = refs[pieces + (2 if first else 0) :]
    keep_ref, send_ref = refs[:2]
    bias_ref, total_ref = refs[-2:]
    step = pl.program_id(0)

    @pl.when(step == 0)
    def _():
        bias_ref[...] = allowed_bias(scal, kept_ref[:1])
        total_ref[:ROWS] = one_ref[:ROWS]
        total_ref[ROWS:] = one_ref[ROWS:] if first else jnp.zeros((ROWS, D), F32)

    weight = join(weights, D // pieces)
    low = low_ref[...]
    lane = lax.broadcasted_iota(jnp.int32, (1, 256), 1)
    grad_ctx = dot_nn(low, weight[:, 512:])
    grad_ctx = jnp.where(lane >= HD, grad_ctx, 0.0).astype(BF)
    keys, values = kv_ref[0, :, :256], kv_ref[0, :, 128:]
    queries = q_ref[0]
    products = grad_ctx.astype(F32) * ctx_f_ref[0]
    dq = jnp.zeros((ROWS, 256), F32)
    dk = jnp.zeros((KEYS, 256), F32)
    dv = jnp.zeros((KEYS, 256), F32)
    zero = jnp.zeros_like(queries)
    for h in range(3):
        own = jnp.where(lanes_of_head(h, 0), queries, zero)
        own_grad = jnp.where(lanes_of_head(h, HD), grad_ctx, zero)
        row_dot = jnp.sum(jnp.where(lanes_of_head(h, HD), products, 0.0), axis=1, keepdims=True)
        scores = dot_nt(own, keys) + bias_ref[...]
        prob = jnp.exp(scores - lse_ref[0, h][:, :1])
        dv = dv + dot_tn(prob.astype(BF), own_grad)
        grad_scores = (prob * (dot_nt(own_grad, values) - row_dot)).astype(BF)
        dq = jnp.where(lanes_of_head(h, 0), dot_nn(grad_scores, keys), dq)
        dk = dk + dot_tn(grad_scores, own)
    dq = dq * 0.125
    gap = jnp.zeros((KEYS, 128), F32)
    dkv = jnp.concatenate([dk, gap], axis=1) + jnp.concatenate([gap, dv], axis=1)
    q_sum = jnp.sum(dq, axis=0, keepdims=True)
    v_sum = jnp.sum(dv, axis=0, keepdims=True)
    dkv = dkv.astype(BF)
    dq = dq.astype(BF)
    packed = xr_ref[...]
    low_kv = dot_tn(packed, dkv)
    from_q = dot_tn(packed[:ROWS], dq)
    from_o = dot_tn(low, ctx_ref[0])
    gap = jnp.zeros((D, 128), F32)
    from_qo = jnp.concatenate([from_q, gap], axis=1) + jnp.concatenate([gap, from_o], axis=1)
    split_out(jnp.concatenate([low_kv, from_qo], axis=1), keep_ref, send_ref)
    extra = small_sums(scal, pieces > 1, first + step, q_sum, v_sum, all_ref, fin_ref, hid_ref)
    keep_ref[:, 0, FB:] = extra[: PARTS // 2]
    send_ref[:, 0, FB:] = extra[PARTS // 2 :]
    total_ref[...] += dot_nt(dkv, weight[:, :384])
    total_ref[:ROWS] += dot_nt(dq, weight[:, 384:640])

    @pl.when(step == count - 1)
    def _():
        if first + count < 4:
            refs[2][...] = total_ref[...]
            return
        x0_ref, x2_ref, x1_ref, x3_ref = refs[2:6]
        grads = total_ref[...].astype(BF)
        frow = feature_row(scal, pieces > 1)
        x0_ref[...] = dot_nt(pick(scal, frow, 0), grads)
        x2_ref[...] = dot_nt(pick(scal, frow, 1), grads)
        for n, ref in ((2, x1_ref), (3, x3_ref)):
            part = dot_nt(pick(scal, frow, n), grads).astype(BF)
            ref[:, :ROWS] = part[:, ROWS:]
            ref[:, ROWS:] = part[:, :ROWS]


def attend_back(scal, kept, packed, kv, queries, context, context_f, lse, one, low, small, weights, first, count, held):
    pieces = len(weights)
    half = PARTS // 2
    at = lambda j: (j + first, 0, 0)
    wide = pl.BlockSpec((half, 1, FB + 16, D), lambda j: (0, j + first, 0, 0))
    n_in = 13 + pieces
    last = first + count == 4
    return call(
        functools.partial(attend_back_body, pieces, first, count),
        (count,),
        [
            SMEM,
            full((8, KEYS)),
            full((KEYS, D)),
            pl.BlockSpec((1, KEYS, 384), at),
            pl.BlockSpec((1, ROWS, 256), at),
            pl.BlockSpec((1, ROWS, 256), at),
            pl.BlockSpec((1, ROWS, 256), at),
            pl.BlockSpec((1, 3, ROWS, 128), lambda j: (j + first, 0, 0, 0)),
            full(one.shape),
            full((ROWS, D)),
            full((8, D)),
            pl.BlockSpec((1, OUT, HL), at),
            pl.BlockSpec((1, 8, D), at),
        ]
        + [pl.BlockSpec((1,) + w.shape[1:], at) for w in weights]
        + [pl.BlockSpec(memory_space=pl.ANY)] * len(held),
        [wide, wide] + ([full((HL, KEYS))] * 4 if last else [full((KEYS, D))]),
        [shape((half, 4, FB + 16, D)), shape((half, 4, FB + 16, D))]
        + ([shape((HL, KEYS), F32)] * 2 + [shape((HL, KEYS))] * 2 if last else [shape((KEYS, D), F32)]),
        [pltpu.VMEM((ROWS, KEYS), F32), pltpu.VMEM((KEYS, D), F32)],
        micros=9 * count,
        aliases={n_in + n: n for n in range(len(held))},
    )(scal, kept, packed, kv, queries, context, context_f, lse, one, low, *small, *weights, *held)


def pack_vec_body(order_ref, mask_ref, vec_ref, out_ref, total_ref):
    step = pl.program_id(0)
    part = dot_nt(vec_ref[0], spread(order_ref[:1]))

    @pl.when(step == 0)
    def _():
        total_ref[...] = part

    @pl.when(step > 0)
    def _():
        total_ref[...] += part

    @pl.when(step == 3)
    def _():
        out_ref[...] = jnp.transpose(total_ref[...] * mask_ref[...].astype(F32))


def pack_vec(order, mask_row, vecs):
    return call(
        pack_vec_body,
        (4,),
        [
            pl.BlockSpec((8, ROWS), lambda b: (0, b)),
            full((1, TOK)),
            pl.BlockSpec((1, OUT, ROWS), lambda b: (b, 0, 0)),
        ],
        full((TOK, OUT)),
        shape((TOK, OUT), F32),
        [pltpu.VMEM((OUT, TOK), F32)],
        micros=5,
    )(order, mask_row, vecs)


def pack_x_body(order_ref, x0_ref, x1_ref, far_ref, out_ref):
    step = pl.program_id(0)
    near = (x0_ref[...] + x1_ref[...].astype(F32)).astype(BF)
    part = dot_nt(jnp.where(step < 2, near, far_ref[...]), spread(order_ref[:1]))

    @pl.when(step == 0)
    def _():
        out_ref[...] = part

    @pl.when(step > 0)
    def _():
        out_ref[...] += part


def pack_x(order, *parts):
    return call(
        pack_x_body,
        (4,),
        [pl.BlockSpec((8, ROWS), lambda b: (0, b))]
        + [pl.BlockSpec((HL, ROWS), lambda b: (0, b & 1)) for _ in parts],
        full((HL, TOK)),
        shape((HL, TOK), F32),
        micros=5,
    )(order, *parts)


def halves(vector):
    high = vector.astype(BF)
    return high, (vector - high.astype(F32)).astype(BF)


def pack_weights_body(k_ref, v_ref, q_ref, o_ref, in_ref, out_ref, fin_ref, qb, vb, inb, ob, outb, g1, s1, g2, s2, heads_ref, ffn_ref):
    turned = lambda ref: jnp.transpose(ref[...].astype(F32)).astype(BF)
    heads_ref[:FB] = jnp.concatenate([k_ref[...], v_ref[...], q_ref[...], turned(o_ref)], axis=1)
    ffn_ref[:FB] = in_ref[...]
    ffn_ref[FB : 2 * FB] = out_ref[...]
    qb, vb, inb, ob, outb, g1, s1, g2, s2 = (ref[...].reshape(1, ref.shape[0]) for ref in (qb, vb, inb, ob, outb, g1, s1, g2, s2))
    gap = jnp.zeros((1, 64), F32)
    window = []
    for value in (jnp.concatenate([qb, gap], axis=1), jnp.concatenate([gap, vb], axis=1)):
        window += list(halves(value))
    hidden = [halves(inb[:, n * 256 : (n + 1) * 256]) for n in range(3)]
    window += [high for high, _ in hidden] + [low for _, low in hidden]
    window = jnp.concatenate(window + [jnp.zeros((6, 256), BF)], axis=0)
    features = [halves(jnp.concatenate([value, gap], axis=1)) for value in (ob, outb, g1, s1, g2, s2)]
    pad = [jnp.zeros((2, 256), BF)]
    features = jnp.concatenate([high for high, _ in features] + pad + [low for _, low in features] + pad, axis=0)
    final = jnp.concatenate([fin_ref[...], jnp.zeros((16, 64), BF)], axis=1)
    extra = jnp.concatenate([final, window, features], axis=1)
    heads_ref[FB:] = extra


def pack_weights(weights, vectors):
    return call(
        pack_weights_body,
        (1,),
        [full(w.shape) for w in weights] + [full(v.shape) for v in vectors],
        [full((FB + 16, D)), full((2 * FB, D))],
        [shape((FB + 16, D)), shape((2 * FB, D))],
        micros=3,
    )(*weights, *vectors)


def ffn_out_body(a_ref, b_ref, out_ref, in_ref):
    total = a_ref[...] + b_ref[...].astype(F32)
    out_ref[...] = total[:FB]
    in_ref[...] = total[FB:]


def ffn_out(a, b):
    both = [full((FB, D))] * 2
    return call(ffn_out_body, (1,), [full(a.shape), full(b.shape)], both, [shape((FB, D), F32)] * 2, micros=3)(a, b)


def heads_out_body(a_ref, b_ref, q_ref, k_ref, v_ref, o_ref, fin_ref, inb, qb, vb, ob, outb, g1, s1, g2, s2):
    total = a_ref[...] + b_ref[...].astype(F32)
    k_ref[...] = total[:FB, :HL]
    v_ref[...] = total[:FB, HL:384]
    q_ref[...] = total[:FB, 384:576]
    o_ref[...] = jnp.transpose(total[:FB, 576:])
    tile = total[FB:]
    fin_ref[...] = tile[:, :HL]
    qb[...] = tile[8:9, 256 : 256 + HL].reshape(HL)
    vb[...] = tile[9:10, 320:512].reshape(HL)
    for n, ref in ((5, ob), (2, outb), (3, g1), (4, s1), (0, g2), (1, s2)):
        ref[...] = tile[n : n + 1, 256 : 256 + HL].reshape(HL)
    inb[...] = jnp.concatenate([tile[n : n + 1, 512:] for n in range(3)], axis=1).reshape(D)


def heads_out(a, b):
    dims = [(FB, HL)] * 3 + [(HL, FB), (16, HL), (D,)] + [(HL,)] * 8
    return call(
        heads_out_body, (1,), [full(a.shape), full(b.shape)], [full(d) for d in dims], [shape(d, F32) for d in dims], micros=3
    )(a, b)


def hi_lo(vector):
    high = vector.astype(BF)
    high = lax.optimization_barrier(high)
    return high, (vector - high.astype(F32)).astype(BF)


def extra_rows(final_t, q_bias, v_bias, inner_bias, features):
    q_hi, q_lo = hi_lo(jnp.pad(q_bias, (0, 64)))
    v_hi, v_lo = hi_lo(jnp.pad(v_bias, (64, 0)))
    in_hi, in_lo = hi_lo(inner_bias.reshape(3, 256))
    window = jnp.concatenate([jnp.stack([q_hi, q_lo, v_hi, v_lo]), in_hi, in_lo], axis=0)
    window = jnp.pad(window, ((0, 6), (0, 0)))
    f_hi, f_lo = hi_lo(jnp.pad(jnp.stack(features), ((0, 2), (0, 64))))
    final_t = jnp.pad(final_t, ((0, 16 - final_t.shape[0]), (0, 64)))
    return jnp.concatenate([final_t, window, jnp.concatenate([f_hi, f_lo], axis=0)], axis=1)


def local(
    inputs,
    token_order,
    lengths,
    token_mask,
    cotangent,
    query_weight,
    key_weight,
    value_weight,
    output_weight,
    inner_weight,
    outer_weight,
    final_weight,
    query_bias,
    value_bias,
    output_bias,
    inner_bias,
    outer_bias,
    first_gain,
    first_shift,
    second_gain,
    second_shift,
):
    m, i = lax.axis_index("mp"), lax.axis_index("dp")
    n_dp = lax.axis_size("dp")
    rows = D // n_dp
    by_xor = n_dp == 8
    scal = jnp.concatenate([jnp.stack([i, m]).astype(jnp.int32), lengths[0]])
    features_of = [output_bias, outer_bias, first_gain, first_shift, second_gain, second_shift]

    if by_xor:
        heads_own, ffn_own = pack_weights(
            [key_weight, value_weight, query_weight, output_weight, inner_weight, outer_weight.T, final_weight.T],
            [query_bias, value_bias, inner_bias] + features_of,
        )
    else:
        extra = extra_rows(final_weight.T, query_bias, value_bias, inner_bias, features_of)
        heads_own = jnp.concatenate([key_weight, value_weight, query_weight, output_weight.T], axis=1)
        heads_own = jnp.concatenate([heads_own, extra], axis=0)
        ffn_own = jnp.concatenate([inner_weight, outer_weight.T], axis=0)

    mask_row = token_mask.reshape(1, TOK)
    heads_own, ffn_own, inputs = sync(heads_own, ffn_own, inputs)
    heads_got = [swap(heads_own, "mp", bit) for bit in (2, 1, 3)]
    features, kept, cot, order = pack_in(scal, token_order, inputs, mask_row, cotangent)
    near, away = features[:, :KEYS], features[:, KEYS:]
    ffn_own, near, away = sync(ffn_own, near, away)
    ffn_got = [swap(ffn_own, "mp", bit) for bit in (2, 1, 3)]
    heads_got = sync(*heads_got)
    heads = jnp.stack([h[:rows] for h in (heads_own, *heads_got)])
    extras = jnp.stack([h[rows:] for h in (heads_own, *heads_got)])
    if by_xor:
        heads, near, away = sync(heads, near, away)
        head_x, head_y = over_plane(heads)
        head_x, head_y = sync(head_x, head_y)
        far_a, far_b = sync(*over_corner(head_x, head_y))
        far_a, far_b, ffn_got, near, away, heads, head_x, head_y = sync(
            far_a, far_b, ffn_got, near, away, heads, head_x, head_y
        )
        x1, x2 = swap(near, "mp", 1), swap(away, "mp", 2)
        ffn = jnp.stack([ffn_own, *ffn_got])
        ffn = jnp.concatenate([ffn, extras], axis=1)
        ffn_x, ffn_y = over_plane(ffn)
        far = jnp.concatenate([far_a, far_b], axis=0)
        head_pieces = [heads, head_x, head_y, far]
        head_pieces += [swap(p, "dp", 1) for p in head_pieces]
        x1, x2, *head_pieces = sync(x1, x2, *head_pieces)
        x3 = swap(x2, "mp", 1)
        x3, ffn_x, ffn_y = sync(x3, ffn_x, ffn_y)
        far_a, far_b = over_corner(ffn_x, ffn_y)
        ffn_pieces = [swap(p, "dp", 1) for p in (ffn, ffn_x, ffn_y)]
    else:
        ffn = jnp.concatenate([jnp.stack([ffn_own, *ffn_got]), extras], axis=1)
        x1, x2 = swap(near, "mp", 1), swap(away, "mp", 2)
        x3 = swap(x2, "mp", 1)
        head_pieces, ffn_pieces, final = plain_pieces(heads, ffn)

    packed, fvec, kv, queries, context, context_f, lse, wo = attend(
        scal, kept, (near, x2, x1, x3), extras, head_pieces
    )
    if by_xor:
        context, far_a, far_b, *ffn_pieces = sync(context, far_a, far_b, *ffn_pieces)
        far = jnp.concatenate([far_a, far_b], axis=0)
        ffn_pieces = [ffn, ffn_x, ffn_y, far] + ffn_pieces + [swap(far, "dp", 1)]
        final = jnp.concatenate([p[:, 2 * FB :, :HL] for p in ffn_pieces], axis=1)
    normed, unit, scale, normed_low, act, slope = inner(context, wo, packed, fvec, extras, ffn_pieces)
    grad_two, two_low, vec, fin_grad, sums = outer(scal, act, normed, fvec, final, cot, ffn_pieces)
    vec_got = swap(vec, "mp", 1)
    ffn_keep, ffn_send, pre, hid_sums = outer_back(two_low, act, slope, normed_low, ffn_pieces)
    vec_got, ffn_send, pre = sync(vec_got, ffn_send, pre)
    vec_low = jnp.stack([vec, vec_got])
    vec_high = swap(vec_low, "mp", 2)
    saved = (kept, packed, kv, queries, context, context_f, lse)

    def heads_back(one, low, first, count, held):
        small = (all_sums, fin_grad, hid_sums)
        return attend_back(scal, *saved, one, low, small, head_pieces, first, count, held)

    if by_xor:
        ffn_got = swap(ffn_send, "dp", 1)
        grad_one, one_low, all_sums = inner_back(pre, grad_two, unit, scale, fvec, sums, ffn_pieces)
        ffn_got, one_low = sync(ffn_got, one_low)
        pair = (ffn_keep, ffn_got)
        x_send, y_send = plane_first(*pair)
        one_low, x_send, y_send = sync(one_low, x_send, y_send)
        x_got, y_got = swap(x_send, "dp", 2), swap(y_send, "dp", 4)
        head_keep, head_send, dx0, dx2, dx1, dx3 = heads_back(grad_one, one_low, 0, 4, ())
        dx1, dx3, head_send, x_got, y_got, vec_high = sync(dx1, dx3, head_send, x_got, y_got, vec_high)

        dx3_got = swap(dx3, "mp", 1)
        head_got = swap(head_send, "dp", 1)
        to_y, to_x, upper, lower = plane_second(*pair, x_got, y_got)
        from_y, from_x = swap(to_y, "dp", 4), swap(to_x, "dp", 2)
        vecs = jnp.concatenate([vec_low, vec_high], axis=0)
        dx3_got, head_got, dx1, vecs = sync(dx3_got, head_got, dx1, vecs)
        to_far = (dx2 + dx3_got.astype(F32)).astype(BF)
        far, dx1_got = swap(to_far, "mp", 2), swap(dx1, "mp", 1)
        pair = (head_keep, head_got)
        x_send, y_send = plane_first(*pair)
        x_send, y_send, vecs = sync(x_send, y_send, vecs)
        x_got, y_got = swap(x_send, "dp", 2), swap(y_send, "dp", 4)
        vectors = pack_vec(order, mask_row, vecs)
        from_y, from_x, vectors = sync(from_y, from_x, vectors)
        upper = upper + from_y.astype(F32)
        lower = (lower + from_x.astype(F32)).astype(BF)
        lower_got = swap(lower, "mp", 1)
        x_got, y_got, dx1_got, far = sync(x_got, y_got, dx1_got, far)
        to_y, to_x, h_upper, h_lower = plane_second(*pair, x_got, y_got)
        to_y, to_x, dx1_got = sync(to_y, to_x, dx1_got)
        from_y, from_x = swap(to_y, "dp", 4), swap(to_x, "dp", 2)
        inputs_grad = pack_x(order, dx0, dx1_got, far)
        from_y, from_x, lower_got, inputs_grad = sync(from_y, from_x, lower_got, inputs_grad)
        h_upper = h_upper + from_y.astype(F32)
        h_lower = (h_lower + from_x.astype(F32)).astype(BF)
        h_lower_got = swap(h_lower, "mp", 1)
        upper = upper + lower_got.astype(F32)
        last = swap(upper[1].astype(BF), "mp", 2)
        h_lower_got, last = sync(h_lower_got, last)
        h_upper = h_upper + h_lower_got.astype(F32)
        h_last = swap(h_upper[1].astype(BF), "mp", 2)
        g_out, g_in = ffn_out(upper[0], last)
        g_q, g_k, g_v, g_o, g_fin, g_inb, g_qb, g_vb, g_ob, g_outb, g_g1, g_s1, g_g2, g_s2 = heads_out(h_upper[0], h_last)
        g_out, g_fin = g_out.T, g_fin.T
    else:
        grad_one, one_low, all_sums = inner_back(pre, grad_two, unit, scale, fvec, sums, ffn_pieces)
        head_keep, head_send, dx0, dx2, dx1, dx3 = heads_back(grad_one, one_low, 0, 4, ())
        far = swap((dx2 + swap(dx3, "mp", 1).astype(F32)).astype(BF), "mp", 2)
        inputs_grad = pack_x(order, dx0, swap(dx1, "mp", 1), far)
        vectors = pack_vec(order, mask_row, jnp.concatenate([vec_low, vec_high], axis=0))
        ends = []
        for keep, send in ((ffn_keep, ffn_send), (head_keep, head_send)):
            total = scatter_plain(jnp.concatenate([keep, send], axis=0).transpose(1, 0, 2, 3).astype(F32))
            upper = total[:2] + swap(total[2:].astype(BF), "mp", 1).astype(F32)
            ends.append(upper[0] + swap(upper[1].astype(BF), "mp", 2).astype(F32))
        ffn_sum, head_sum = ends
        tile = head_sum[rows:]
        g_out, g_in, g_fin = ffn_sum[:rows].T, ffn_sum[rows:], tile[: OUT // n_dp, :HL].T
        g_g2, g_s2, g_outb, g_g1, g_s1, g_ob = (tile[n, 256 : 256 + HL] for n in range(6))
        g_inb = tile[:3, 512:].reshape(D)
        g_k, g_v, g_q, g_o = head_sum[:rows, :HL], head_sum[:rows, HL:384], head_sum[:rows, 384:576], head_sum[:rows, 576:].T
        g_qb, g_vb = tile[8, 256 : 256 + HL], tile[9, 320:512]
    return (
        vectors,
        inputs_grad,
        g_q,
        g_k,
        g_v,
        g_o,
        g_in,
        g_out,
        g_fin,
        g_qb,
        g_vb,
        g_ob,
        g_inb,
        g_outb,
        g_g1,
        g_s1,
        g_g2,
        g_s2,
    )


def solution(mesh):
    return jax.shard_map(
        local,
        mesh=mesh,
        in_specs=(
            P("mp", "dp"),
            P("dp", None),
            P("dp", None),
            P("dp"),
            P("dp", None),
            P("dp", "mp"),
            P("dp", "mp"),
            P("dp", "mp"),
            P("mp", "dp"),
            P("dp", "mp"),
            P("mp", "dp"),
            P("mp", "dp"),
            P("mp"),
            P("mp"),
            P("mp"),
            P("mp"),
            P("mp"),
            P("mp"),
            P("mp"),
            P("mp"),
            P("mp"),
        ),
        out_specs=(
            P("dp", None),
            P("mp", "dp"),
            P("dp", "mp"),
            P("dp", "mp"),
            P("dp", "mp"),
            P("mp", "dp"),
            P("dp", "mp"),
            P("mp", "dp"),
            P("mp", "dp"),
            P("mp"),
            P("mp"),
            P("mp"),
            P("mp"),
            P("mp"),
            P("mp"),
            P("mp"),
            P("mp"),
            P("mp"),
        ),
        check_vma=False,
    )
```

profile of v0, /device:TPU:0, one launch (start us, length us, event | category | flops | bytes accessed | tf_op | source)
XLA Modules:
  0.0 298.1 jit_solution(5701433040041307542)
XLA Ops:
  2.7 4.0 %collective-permute-start = (bf16[112,768]{1,0:T(8,128)(2,1)}, bf16[112,768]{1,0:T(8,128)(2,1)S(1)}, u32[]{:S(2)}, u32[]{:S(2)}) collective-permute-start(bf16[112,768]{1,0:T(8,128)(2,1)} %get-tuple-element.158), channel_id=1, source_target_pairs={{0,2},{1,3},{2,0},{3,1},{4,6},{5,7},{6,4},{7,5},{8,10},{9,11},{10,... | collective-permute-start | bytes 516104 | tf_op jit(solution)/shard_map/ppermute | solution.py:42
  8.9 6.1 %shard_map.341 = (bf16[192,2048]{1,0:T(8,128)(2,1)}, f32[8,1024]{1,0:T(8,128)}, f32[512,128]{1,0:T(8,128)}, s32[8,2048]{1,0:T(8,128)}) custom-call(s32[6]{0:T(128)} %pad_add_fusion.scal, s32[1,2048]{1,0:T(1,128)} %order_ref.1, bf16[192,2048]{1,0:T(8,128)(2,1)} %x_ref, s32[1,2048]{1,0:T(1,128)} %bitcast.134, bf16[2048,128]{1,0:T(8,128)(2,1)} %cot_ref.1), custom_call_target="tpu_custom_call" | custom-call | flops 6000000000 | bytes 18000000 | tf_op jit(solution)/shard_map/pallas_call | solution.py:194
  16.6 3.3 %collective-permute-done.2 = bf16[112,768]{1,0:T(8,128)(2,1)S(1)} collective-permute-done((bf16[112,768]{1,0:T(8,128)(2,1)}, bf16[112,768]{1,0:T(8,128)(2,1)S(1)}, u32[]{:S(2)}, u32[]{:S(2)}) %collective-permute-start.2) | collective-permute-done | bytes 172064 | tf_op jit(solution)/shard_map/ppermute | solution.py:42
  23.1 5.1 %collective-permute-start.7 = (bf16[192,768]{1,0:T(8,128)(2,1)S(1)}, bf16[192,768]{1,0:T(8,128)(2,1)S(1)}, u32[]{:S(2)}, u32[]{:S(2)}) collective-permute-start(bf16[192,768]{1,0:T(8,128)(2,1)S(1)} %copy-done.17), channel_id=1, source_target_pairs={{0,2},{1,3},{2,0},{3,1},{4,6},{5,7},{6,4},{7,5},{8,10},{9,11},{10,... | collective-permute-start | bytes 884744 | tf_op jit(solution)/shard_map/ppermute | solution.py:42
  29.7 4.6 %collective-permute-done.3.refs_1_ = bf16[4,96,768]{2,1,0:T(8,128)(2,1)S(1)} collective-permute-done((bf16[4,96,768]{2,1,0:T(8,128)(2,1)S(1)}, bf16[4,96,768]{2,1,0:T(8,128)(2,1)S(1)}, u32[]{:S(2)}, u32[]{:S(2)}) %collective-permute-start.3) | collective-permute-done | bytes 589856 | tf_op jit(solution)/shard_map/ppermute | solution.py:42
  37.7 4.6 %collective-permute-done.5 = bf16[2,96,768]{2,1,0:T(8,128)(2,1)S(1)} collective-permute-done((bf16[2,96,768]{2,1,0:T(8,128)(2,1)S(1)}, bf16[2,96,768]{2,1,0:T(8,128)(2,1)S(1)}, u32[]{:S(2)}, u32[]{:S(2)}) %collective-permute-start.5) | collective-permute-done | bytes 294944 | tf_op jit(solution)/shard_map/ppermute | solution.py:42
  42.9 5.0 %collective-permute-done.7 = bf16[192,768]{1,0:T(8,128)(2,1)S(1)} collective-permute-done((bf16[192,768]{1,0:T(8,128)(2,1)S(1)}, bf16[192,768]{1,0:T(8,128)(2,1)S(1)}, u32[]{:S(2)}, u32[]{:S(2)}) %collective-permute-start.7) | collective-permute-done | bytes 294944 | tf_op jit(solution)/shard_map/ppermute | solution.py:42
  48.8 5.9 %collective-permute-start.10 = (bf16[192,1024]{1,0:T(8,128)(2,1)S(1)}, bf16[192,1024]{1,0:T(8,128)(2,1)S(1)}, u32[]{:S(2)}, u32[]{:S(2)}) collective-permute-start(bf16[192,1024]{1,0:T(8,128)(2,1)S(1)} %get-tuple-element.174.x0), channel_id=1, source_target_pairs={{0,1},{1,0},{2,3},{3,2},{4,5},{5,4},{6,7},{7,6},{8,9},{9,8},{10,11... | collective-permute-start | bytes 1179656 | tf_op jit(solution)/shard_map/ppermute | solution.py:42
  55.9 14.8 %collective-permute-done.10.x1 = bf16[192,1024]{1,0:T(8,128)(2,1)S(1)} collective-permute-done((bf16[192,1024]{1,0:T(8,128)(2,1)S(1)}, bf16[192,1024]{1,0:T(8,128)(2,1)S(1)}, u32[]{:S(2)}, u32[]{:S(2)}) %collective-permute-start.10) | collective-permute-done | bytes 393248 | tf_op jit(solution)/shard_map/ppermute | solution.py:42
  70.7 4.5 %collective-permute-done.11.x2 = bf16[192,1024]{1,0:T(8,128)(2,1)S(1)} collective-permute-done((bf16[192,1024]{1,0:T(8,128)(2,1)S(1)}, bf16[192,1024]{1,0:T(8,128)(2,1)S(1)}, u32[]{:S(2)}, u32[]{:S(2)}) %collective-permute-start.11) | collective-permute-done | bytes 393248 | tf_op jit(solution)/shard_map/ppermute | solution.py:42
  78.3 10.9 %collective-permute-done.16.x3 = bf16[192,1024]{1,0:T(8,128)(2,1)S(1)} collective-permute-done((bf16[192,1024]{1,0:T(8,128)(2,1)S(1)}, bf16[192,1024]{1,0:T(8,128)(2,1)S(1)}, u32[]{:S(2)}, u32[]{:S(2)}) %collective-permute-start.16) | collective-permute-done | bytes 393248 | tf_op jit(solution)/shard_map/ppermute | solution.py:42
  91.1 23.0 %shard_map.342 = (bf16[1024,768]{1,0:T(8,128)(2,1)}, f32[8,768]{1,0:T(8,128)}, bf16[4,1024,384]{2,1,0:T(8,128)(2,1)}, bf16[4,512,256]{2,1,0:T(8,128)(2,1)}, bf16...) custom-call(s32[6]{0:T(128)} %pad_add_fusion.scal, ...), custom_call_target="tpu_custom_call" | custom-call | flops 23000000512 | bytes 69000000 | tf_op jit(solution)/shard_map/pallas_call | solution.py:294
  118.4 12.6 %shard_map.343 = (f32[512,768]{1,0:T(8,128)}, f32[512,768]{1,0:T(8,128)}, f32[512,128]{1,0:T(8,128)}, bf16[512,768]{1,0:T(8,128)(2,1)}, bf16[4,512,768]{2,1,0:T(8,128)(2,1)}, /*index=5*/f32[4,512,768]{2,1,0:T(8,128)}) custom-call(bf16[4,512,256]{2,1,0:T(8,128)(2,1)} %get-tuple-element.198.ctx_ref, bf16[4,768,256]{2,1,0:T(8,128)(2,1)} %get-tuple-element.199.wo_ref, ...), custom_call_target="tpu_custom_call" | custom-call | flops 10000000000 | bytes 30000000 | tf_op jit(solution)/shard_map/pallas_call | solution.py:381
  131.0 12.4 %shard_map.344 = (f32[512,768]{1,0:T(8,128)}, bf16[512,768]{1,0:T(8,128)(2,1)}, bf16[128,512]{1,0:T(8,128)(2,1)}, bf16[4,128,192]{2,1,0:T(8,128)(2,1)}, f32[8,768]{1,0:T(8,128)}) custom-call(s32[6]{0:T(128)} %pad_add_fusion.scal, bf16[4,512,768]{2,1,0:T(8,128)(2,1)} %get-tuple-element.207.act_ref, f32[512,768]{1,0:T(8,128)} %get-tuple-element.208.normed_ref, ...), custom_call_target="tpu_custom_call" | custom-call | flops 10000000000 | bytes 30000000 | tf_op jit(solution)/shard_map/pallas_call | solution.py:467
  143.7 14.3 %shard_map.345 = (bf16[4,4,192,768]{3,2,1,0:T(8,128)(2,1)}, bf16[4,4,192,768]{3,2,1,0:T(8,128)(2,1)}, bf16[4,512,768]{2,1,0:T(8,128)(2,1)}, f32[4,8,768]{2,1,0:T(8,128)}) custom-call(bf16[512,768]{1,0:T(8,128)(2,1)} %get-tuple-element.210.low_ref, bf16[4,512,768]{2,1,0:T(8,128)(2,1)} %get-tuple-element.207.act_ref, ...), custom_call_target="tpu_custom_call" | custom-call | flops 15000000512 | bytes 45000000 | tf_op jit(solution)/shard_map/pallas_call | solution.py:516
  159.1 10.1 %shard_map.346 = (f32[512,768]{1,0:T(8,128)}, bf16[512,768]{1,0:T(8,128)(2,1)}, f32[8,768]{1,0:T(8,128)}) custom-call(bf16[4,512,768]{2,1,0:T(8,128)(2,1)} %get-tuple-element.218.pre_ref, f32[512,768]{1,0:T(8,128)} %get-tuple-element.219.grad_ref, f32[512,768]{1,0:T(8,128)} %get-tuple-element.220.unit_ref, f32[512,128]{1,0:T(8,128)} %get-tuple-element.221.scale_ref, ...), custom_call_target="tpu_custom_call" | custom-call | flops 8999999488 | bytes 27000000 | tf_op jit(solution)/shard_map/pallas_call | solution.py:566
  176.3 37.9 %shard_map.347 = (bf16[4,4,112,768]{3,2,1,0:T(8,128)(2,1)}, bf16[4,4,112,768]{3,2,1,0:T(8,128)(2,1)}, f32[192,1024]{1,0:T(8,128)}, f32[192,1024]{1,0:T(8,128)}, ...) custom-call(s32[6]{0:T(128)} %pad_add_fusion.scal, f32[8,1024]{1,0:T(8,128)} %get-tuple-element.157.kept_ref, ...), custom_call_target="tpu_custom_call" | custom-call | flops 35999997952 | bytes 108000000 | tf_op jit(solution)/shard_map/pallas_call | solution.py:676
  223.3 3.4 %collective-permute-done.32 = bf16[192,1024]{1,0:T(8,128)(2,1)S(1)} collective-permute-done((bf16[192,1024]{1,0:T(8,128)(2,1)}, bf16[192,1024]{1,0:T(8,128)(2,1)S(1)}, u32[]{:S(2)}, u32[]{:S(2)}) %collective-permute-start.32) | collective-permute-done | bytes 393248 | tf_op jit(solution)/shard_map/ppermute | solution.py:42
  237.2 6.1 %shard_map.348 = f32[2048,128]{1,0:T(8,128)} custom-call(s32[8,2048]{1,0:T(8,128)} %get-tuple-element.243.order_ref, s32[1,2048]{1,0:T(1,128)} %bitcast.135, bf16[4,128,512]{2,1,0:T(8,128)(2,1)} %pad_maximum_fusion.1.vec_ref), custom_call_target="tpu_custom_call" | custom-call | flops 5000000000 | bytes 15000000 | tf_op jit(solution)/shard_map/pallas_call | solution.py:723
  249.8 6.6 %collective-permute-done.36.x1_ref = bf16[192,1024]{1,0:T(8,128)(2,1)} collective-permute-done((bf16[192,1024]{1,0:T(8,128)(2,1)}, bf16[192,1024]{1,0:T(8,128)(2,1)}, u32[]{:S(2)}, u32[]{:S(2)}) %collective-permute-start.36) | collective-permute-done | bytes 393248 | tf_op jit(solution)/shard_map/ppermute | solution.py:42
  259.1 6.5 %shard_map.349 = f32[192,2048]{1,0:T(8,128)} custom-call(s32[8,2048]{1,0:T(8,128)} %get-tuple-element.243.order_ref, f32[192,1024]{1,0:T(8,128)} %get-tuple-element.264.x0_ref, bf16[192,1024]{1,0:T(8,128)(2,1)} %collective-permute-done.36.x1_ref, bf16[192,1024]{1,0:T(8,128)(2,1)} %collective-permute-done.37.far_ref), custom_call_target="tpu_custom_call" | custom-call | flops 5000000000 | bytes 15000000 | tf_op jit(solution)/shard_map/pallas_call | solution.py:753
  270.0 3.8 %collective-permute-start.42 = (bf16[192,768]{1,0:T(8,128)(2,1)S(1)}, bf16[192,768]{1,0:T(8,128)(2,1)S(1)}, u32[]{:S(2)}, u32[]{:S(2)}) collective-permute-start(bf16[192,768]{1,0:T(8,128)(2,1)S(1)} %fusion.16), channel_id=1, source_target_pairs={{0,2},{1,3},{2,0},{3,1},{4,6},{5,7},{6,4},{7,5},{8,10},{9,11},{10,... | collective-permute-start | bytes 884744 | tf_op jit(solution)/shard_map/ppermute | solution.py:42
  274.6 11.1 %collective-permute-done.42.b_ref = bf16[192,768]{1,0:T(8,128)(2,1)S(1)} collective-permute-done((bf16[192,768]{1,0:T(8,128)(2,1)S(1)}, bf16[192,768]{1,0:T(8,128)(2,1)S(1)}, u32[]{:S(2)}, u32[]{:S(2)}) %collective-permute-start.42) | collective-permute-done | bytes 294944 | tf_op jit(solution)/shard_map/ppermute | solution.py:42
  290.0 5.3 %collective-permute-done.43.b_ref = bf16[112,768]{1,0:T(8,128)(2,1)S(1)} collective-permute-done((bf16[112,768]{1,0:T(8,128)(2,1)S(1)}, bf16[112,768]{1,0:T(8,128)(2,1)S(1)}, u32[]{:S(2)}, u32[]{:S(2)}) %collective-permute-start.43) | collective-permute-done | bytes 172064 | tf_op jit(solution)/shard_map/ppermute | solution.py:42
  (195 shorter events, 74.5 us)
Async XLA Ops:
  23.1 24.9 %collective-permute-start.7 = (bf16[192,768]{1,0:T(8,128)(2,1)S(1)}, bf16[192,768]{1,0:T(8,128)(2,1)S(1)}, u32[]{:S(2)}, u32[]{:S(2)}) collective-permute-start(bf16[192,768]{1,0:T(8,128)(2,1)S(1)} %copy-done.17), channel_id=1, source_target_pairs={{0,2},{1,3},{2,0},{3,1},{4,6},{5,7},{6,4},{7,5},{8,10},{9,11},{10,... | collective-permute-start | bytes 884744 | tf_op jit(solution)/shard_map/ppermute | solution.py:42
  28.2 20.4 %collective-permute-start.8 = (bf16[192,768]{1,0:T(8,128)(2,1)S(1)}, bf16[192,768]{1,0:T(8,128)(2,1)S(1)}, u32[]{:S(2)}, u32[]{:S(2)}) collective-permute-start(bf16[192,768]{1,0:T(8,128)(2,1)S(1)} %copy-done.17), channel_id=1, source_target_pairs={{0,1},{1,0},{2,3},{3,2},{4,5},{5,4},{6,7},{7,6},{8,9},{9,8},{10,11... | collective-permute-start | bytes 884744 | tf_op jit(solution)/shard_map/ppermute | solution.py:42
  28.2 20.4 %collective-permute-start.9 = (bf16[192,768]{1,0:T(8,128)(2,1)S(1)}, bf16[192,768]{1,0:T(8,128)(2,1)S(1)}, u32[]{:S(2)}, u32[]{:S(2)}) collective-permute-start(bf16[192,768]{1,0:T(8,128)(2,1)S(1)} %copy-done.17), channel_id=1, source_target_pairs={{0,3},{1,2},{2,1},{3,0},{4,7},{5,6},{6,5},{7,4},{8,11},{9,10},{10,... | collective-permute-start | bytes 884744 | tf_op jit(solution)/shard_map/ppermute | solution.py:42
  48.7 26.6 %collective-permute-start.15 = (bf16[4,96,768]{2,1,0:T(8,128)(2,1)S(1)}, bf16[4,96,768]{2,1,0:T(8,128)(2,1)S(1)}, u32[]{:S(2)}, u32[]{:S(2)}) collective-permute-start(bf16[4,96,768]{2,1,0:T(8,128)(2,1)S(1)} %constant_dynamic-update-slice_fusion.refs_3_), channel_id=1, source_target_pairs={{0,4},{4,0},{8,12},{12,8},{16,20},{20,16},{24,28},{28,24},{1,5},{5... | collective-permute-start | bytes 1769480 | tf_op jit(solution)/shard_map/ppermute | solution.py:42
  48.8 21.9 %collective-permute-start.10 = (bf16[192,1024]{1,0:T(8,128)(2,1)S(1)}, bf16[192,1024]{1,0:T(8,128)(2,1)S(1)}, u32[]{:S(2)}, u32[]{:S(2)}) collective-permute-start(bf16[192,1024]{1,0:T(8,128)(2,1)S(1)} %get-tuple-element.174.x0), channel_id=1, source_target_pairs={{0,1},{1,0},{2,3},{3,2},{4,5},{5,4},{6,7},{7,6},{8,9},{9,8},{10,11... | collective-permute-start | bytes 1179656 | tf_op jit(solution)/shard_map/ppermute | solution.py:42
  54.7 20.5 %collective-permute-start.11 = (bf16[192,1024]{1,0:T(8,128)(2,1)S(1)}, bf16[192,1024]{1,0:T(8,128)(2,1)S(1)}, u32[]{:S(2)}, u32[]{:S(2)}) collective-permute-start(bf16[192,1024]{1,0:T(8,128)(2,1)S(1)} %get-tuple-element.175), channel_id=1, source_target_pairs={{0,2},{1,3},{2,0},{3,1},{4,6},{5,7},{6,4},{7,5},{8,10},{9,11},{10,... | collective-permute-start | bytes 1179656 | tf_op jit(solution)/shard_map/ppermute | solution.py:42
  54.8 34.5 %collective-permute-start.17 = (bf16[4,208,768]{2,1,0:T(8,128)(2,1)S(1)}, bf16[4,208,768]{2,1,0:T(8,128)(2,1)S(1)}, u32[]{:S(2)}, u32[]{:S(2)}) collective-permute-start(bf16[4,208,768]{2,1,0:T(8,128)(2,1)S(1)} %maximum_maximum_fusion.refs_0_), channel_id=1, source_target_pairs={{0,8},{4,12},{8,0},{12,4},{16,24},{20,28},{24,16},{28,20},{1,9},{5... | collective-permute-start | bytes 3833864 | tf_op jit(solution)/shard_map/ppermute | solution.py:42
  55.4 33.9 %collective-permute-start.18 = (bf16[4,208,768]{2,1,0:T(8,128)(2,1)S(1)}, bf16[4,208,768]{2,1,0:T(8,128)(2,1)S(1)}, u32[]{:S(2)}, u32[]{:S(2)}) collective-permute-start(bf16[4,208,768]{2,1,0:T(8,128)(2,1)S(1)} %maximum_maximum_fusion.refs_0_), channel_id=1, source_target_pairs={{0,16},{4,20},{8,24},{12,28},{16,0},{20,4},{24,8},{28,12},{1,17},{... | collective-permute-start | bytes 3833864 | tf_op jit(solution)/shard_map/ppermute | solution.py:42
  78.1 36.0 %collective-permute-start.21 = (bf16[4,208,768]{2,1,0:T(8,128)(2,1)S(1)}, bf16[4,208,768]{2,1,0:T(8,128)(2,1)}, u32[]{:S(2)}, u32[]{:S(2)}) collective-permute-start(bf16[4,208,768]{2,1,0:T(8,128)(2,1)S(1)} %maximum_maximum_fusion.refs_0_), channel_id=1, source_target_pairs={{0,4},{4,0},{8,12},{12,8},{16,20},{20,16},{24,28},{28,24},{1,5},{5... | collective-permute-start | bytes 3833864 | tf_op jit(solution)/shard_map/ppermute | solution.py:42
  89.3 24.8 %collective-permute-start.22 = (bf16[4,208,768]{2,1,0:T(8,128)(2,1)S(1)}, bf16[4,208,768]{2,1,0:T(8,128)(2,1)}, u32[]{:S(2)}, u32[]{:S(2)}) collective-permute-start(bf16[4,208,768]{2,1,0:T(8,128)(2,1)S(1)} %collective-permute-done.17.refs_1_), channel_id=1, source_target_pairs={{0,4},{4,0},{8,12},{12,8},{16,20},{20,16},{24,28},{28,24},{1,5},{5... | collective-permute-start | bytes 3833864 | tf_op jit(solution)/shard_map/ppermute | solution.py:42
  89.5 24.7 %collective-permute-start.23 = (bf16[4,208,768]{2,1,0:T(8,128)(2,1)S(1)}, bf16[4,208,768]{2,1,0:T(8,128)(2,1)}, u32[]{:S(2)}, u32[]{:S(2)}) collective-permute-start(bf16[4,208,768]{2,1,0:T(8,128)(2,1)S(1)} %collective-permute-done.18.refs_2_), channel_id=1, source_target_pairs={{0,4},{4,0},{8,12},{12,8},{16,20},{20,16},{24,28},{28,24},{1,5},{5... | collective-permute-start | bytes 3833864 | tf_op jit(solution)/shard_map/ppermute | solution.py:42
  90.0 24.1 %collective-permute-start.19 = (bf16[2,208,768]{2,1,0:T(8,128)(2,1)S(1)}, bf16[2,208,768]{2,1,0:T(8,128)(2,1)S(1)}, u32[]{:S(2)}, u32[]{:S(2)}) collective-permute-start(bf16[2,208,768]{2,1,0:T(8,128)(2,1)S(1)} %slice.188), channel_id=1, source_target_pairs={{0,8},{4,12},{8,0},{12,4},{16,24},{20,28},{24,16},{28,20},{1,9},{5... | collective-permute-start | bytes 1916936 | tf_op jit(solution)/shard_map/ppermute | solution.py:42
  90.6 23.6 %collective-permute-start.20 = (bf16[2,208,768]{2,1,0:T(8,128)(2,1)S(1)}, bf16[2,208,768]{2,1,0:T(8,128)(2,1)S(1)}, u32[]{:S(2)}, u32[]{:S(2)}) collective-permute-start(bf16[2,208,768]{2,1,0:T(8,128)(2,1)S(1)} %slice.189), channel_id=1, source_target_pairs={{0,16},{4,20},{8,24},{12,28},{16,0},{20,4},{24,8},{28,12},{1,17},{... | collective-permute-start | bytes 1916936 | tf_op jit(solution)/shard_map/ppermute | solution.py:42
  158.8 55.5 %collective-permute-start.29 = (bf16[2,128,512]{2,1,0:T(8,128)(2,1)}, bf16[2,128,512]{2,1,0:T(8,128)(2,1)}, u32[]{:S(2)}, u32[]{:S(2)}) collective-permute-start(bf16[2,128,512]{2,1,0:T(8,128)(2,1)} %pad_maximum_fusion.2), channel_id=1, source_target_pairs={{0,2},{1,3},{2,0},{3,1},{4,6},{5,7},{6,4},{7,5},{8,10},{9,11},{10,... | collective-permute-start | bytes 786440 | tf_op jit(solution)/shard_map/ppermute | solution.py:42
  173.3 41.0 %collective-permute-start.27 = (bf16[2,2,192,768]{3,2,1,0:T(8,128)(2,1)}, bf16[2,2,192,768]{3,2,1,0:T(8,128)(2,1)S(1)}, u32[]{:S(2)}, u32[]{:S(2)}) collective-permute-start(bf16[2,2,192,768]{3,2,1,0:T(8,128)(2,1)} %fusion), channel_id=1, source_target_pairs={{0,8},{4,12},{8,0},{12,4},{16,24},{20,28},{24,16},{28,20},{1,9},{5... | collective-permute-start | bytes 3538952 | tf_op jit(solution)/shard_map/ppermute | solution.py:42
  174.8 39.5 %collective-permute-start.28 = (bf16[2,2,192,768]{3,2,1,0:T(8,128)(2,1)S(1)}, bf16[2,2,192,768]{3,2,1,0:T(8,128)(2,1)S(1)}, u32[]{:S(2)}, u32[]{:S(2)}) collective-permute-start(bf16[2,2,192,768]{3,2,1,0:T(8,128)(2,1)S(1)} %fusion.1), channel_id=1, source_target_pairs={{0,16},{4,20},{8,24},{12,28},{16,0},{20,4},{24,8},{28,12},{1,17},{... | collective-permute-start | bytes 3538952 | tf_op jit(solution)/shard_map/ppermute | solution.py:42
  220.4 15.9 %collective-permute-start.30 = (bf16[2,192,768]{2,1,0:T(8,128)(2,1)S(1)}, bf16[2,192,768]{2,1,0:T(8,128)(2,1)S(1)}, u32[]{:S(2)}, u32[]{:S(2)}) collective-permute-start(bf16[2,192,768]{2,1,0:T(8,128)(2,1)S(1)} %get-tuple-element.291), channel_id=1, source_target_pairs={{0,16},{4,20},{8,24},{12,28},{16,0},{20,4},{24,8},{28,12},{1,17},{... | collective-permute-start | bytes 1769480 | tf_op jit(solution)/shard_map/ppermute | solution.py:42
  220.9 22.3 %collective-permute-start.31 = (bf16[2,192,768]{2,1,0:T(8,128)(2,1)}, bf16[2,192,768]{2,1,0:T(8,128)(2,1)}, u32[]{:S(2)}, u32[]{:S(2)}) collective-permute-start(bf16[2,192,768]{2,1,0:T(8,128)(2,1)} %get-tuple-element.290), channel_id=1, source_target_pairs={{0,8},{4,12},{8,0},{12,4},{16,24},{20,28},{24,16},{28,20},{1,9},{5... | collective-permute-start | bytes 1769480 | tf_op jit(solution)/shard_map/ppermute | solution.py:42
  230.1 19.8 %collective-permute-start.37 = (bf16[192,1024]{1,0:T(8,128)(2,1)}, bf16[192,1024]{1,0:T(8,128)(2,1)}, u32[]{:S(2)}, u32[]{:S(2)}) collective-permute-start(bf16[192,1024]{1,0:T(8,128)(2,1)} %add_convert_fusion.4), channel_id=1, source_target_pairs={{0,2},{1,3},{2,0},{3,1},{4,6},{5,7},{6,4},{7,5},{8,10},{9,11},{10,... | collective-permute-start | bytes 1179656 | tf_op jit(solution)/shard_map/ppermute | solution.py:42
  232.3 24.1 %collective-permute-start.34 = (bf16[2,2,112,768]{3,2,1,0:T(8,128)(2,1)}, bf16[2,2,112,768]{3,2,1,0:T(8,128)(2,1)S(1)}, u32[]{:S(2)}, u32[]{:S(2)}) collective-permute-start(bf16[2,2,112,768]{3,2,1,0:T(8,128)(2,1)} %fusion.8), channel_id=1, source_target_pairs={{0,8},{4,12},{8,0},{12,4},{16,24},{20,28},{24,16},{28,20},{1,9},{5... | collective-permute-start | bytes 2064392 | tf_op jit(solution)/shard_map/ppermute | solution.py:42
  232.8 23.6 %collective-permute-start.35 = (bf16[2,2,112,768]{3,2,1,0:T(8,128)(2,1)}, bf16[2,2,112,768]{3,2,1,0:T(8,128)(2,1)}, u32[]{:S(2)}, u32[]{:S(2)}) collective-permute-start(bf16[2,2,112,768]{3,2,1,0:T(8,128)(2,1)} %fusion.9), channel_id=1, source_target_pairs={{0,16},{4,20},{8,24},{12,28},{16,0},{20,4},{24,8},{28,12},{1,17},{... | collective-permute-start | bytes 2064392 | tf_op jit(solution)/shard_map/ppermute | solution.py:42
  237.2 19.3 %collective-permute-start.36 = (bf16[192,1024]{1,0:T(8,128)(2,1)}, bf16[192,1024]{1,0:T(8,128)(2,1)}, u32[]{:S(2)}, u32[]{:S(2)}) collective-permute-start(bf16[192,1024]{1,0:T(8,128)(2,1)} %get-tuple-element.255), channel_id=1, source_target_pairs={{0,1},{1,0},{2,3},{3,2},{4,5},{5,4},{6,7},{7,6},{8,9},{9,8},{10,11... | collective-permute-start | bytes 1179656 | tf_op jit(solution)/shard_map/ppermute | solution.py:42
  245.8 20.0 %collective-permute-start.40 = (bf16[2,192,768]{2,1,0:T(8,128)(2,1)}, bf16[2,192,768]{2,1,0:T(8,128)(2,1)}, u32[]{:S(2)}, u32[]{:S(2)}) collective-permute-start(bf16[2,192,768]{2,1,0:T(8,128)(2,1)} %fusion.5), channel_id=1, source_target_pairs={{0,1},{1,0},{2,3},{3,2},{4,5},{5,4},{6,7},{7,6},{8,9},{9,8},{10,11... | collective-permute-start | bytes 1769480 | tf_op jit(solution)/shard_map/ppermute | solution.py:42
  268.0 17.7 %collective-permute-start.41 = (bf16[2,112,768]{2,1,0:T(8,128)(2,1)S(1)}, bf16[2,112,768]{2,1,0:T(8,128)(2,1)S(1)}, u32[]{:S(2)}, u32[]{:S(2)}) collective-permute-start(bf16[2,112,768]{2,1,0:T(8,128)(2,1)S(1)} %fusion.11), channel_id=1, source_target_pairs={{0,1},{1,0},{2,3},{3,2},{4,5},{5,4},{6,7},{7,6},{8,9},{9,8},{10,11... | collective-permute-start | bytes 1032200 | tf_op jit(solution)/shard_map/ppermute | solution.py:42
  (57 other events, 638.1 us)
where the time goes:
time: 299 us; the launch traced here: 298 us
  Pallas kernels  135 us (45%)
  waiting for transfers between devices  85.9 us (29%)
  starting transfers between devices  43.1 us (14%)
  other arithmetic  22.9 us (8%)
  local copies, waits for them, and re-layouts  9.67 us (3%)
    ppermute x44, waiting for transfers between devices, swap(): return lax.ppermute(array, axis, [(a, a ^ bit) for a in range(size)])  85.9 us
    ppermute x44, starting transfers between devices, swap(): return lax.ppermute(array, axis, [(a, a ^ bit) for a in range(size)])  43.1 us
    pallas_call x1, Pallas kernels, attend_back(): call(functools.partial(attend_back_body, pieces, first, count), (count,),...  37.9 us
    pallas_call x1, Pallas kernels, attend(): call(functools.partial(attend_body, pieces), (4,), [SMEM, full((8, KEYS))...  23 us
    pallas_call x1, Pallas kernels, outer_back(): call(functools.partial(outer_back_body, pieces), (4,), [full((ROWS, D)),...  14.3 us
    pallas_call x1, Pallas kernels, inner(): call(functools.partial(inner_body, pieces), (4,), [full((4, ROWS, 256)),...  12.6 us
    pallas_call x1, Pallas kernels, outer(): call(functools.partial(outer_body, pieces), (4,), [SMEM] + [pl.BlockSpec(...  12.4 us
    pallas_call x1, Pallas kernels, inner_back(): call(functools.partial(inner_back_body, pieces), (4,), [pl.BlockSpec((1,...  10.1 us
  transfers between devices with their start and end apart: 44, of which 23 were waited for; matrix products, arithmetic and copies ran while one was open for 9% of the time, Pallas kernels for 36%

commit v1 on v0

--- a/solution.py
+++ b/solution.py
@@ -18,11 +18,10 @@
 ROWS = 512
 KEYS = 1024
 LONG = 1024
-CHUNK = 256
+CHUNK = 64
 EPS = 1e-06
 F32 = jnp.float32
 BF = jnp.bfloat16
-VMEM_LIMIT = 56 * 1024 * 1024
 
 
 def dot_nn(a, b):
@@ -50,7 +49,7 @@
 SMEM = pl.BlockSpec(memory_space=pltpu.SMEM)
 
 
-def call(body, grid, in_specs, out_specs, out_shape, scratch=(), micros=10, aliases=None):
+def call(body, grid, in_specs, out_specs, out_shape, scratch=(), micros=10, aliases=None, limit=16):
     return pl.pallas_call(
         body,
         grid=grid,
@@ -60,7 +59,7 @@
         scratch_shapes=list(scratch),
         input_output_aliases=aliases or {},
         compiler_params=pltpu.CompilerParams(
-            dimension_semantics=("arbitrary",) * len(grid), vmem_limit_bytes=VMEM_LIMIT
+            dimension_semantics=("arbitrary",) * len(grid), vmem_limit_bytes=limit * 1024 * 1024
         ),
         cost_estimate=pl.CostEstimate(flops=micros * 10**9, transcendentals=0, bytes_accessed=micros * 3 * 10**6),
     )
@@ -237,7 +236,7 @@
 
 def attend_body(pieces, scal, kept_ref, x0, x2, x1, x3, extra_ref, *refs):
     weights = refs[:pieces]
-    xr_ref, fvec_ref, kv_ref, q_ref, ctx_ref, ctx_f_ref, lse_ref, wo_ref, bias_ref = refs[pieces:]
+    xr_ref, fvec_ref, kv_ref, q_ref, ctx_ref, ctx_f_ref, wo_ref, bias_ref = refs[pieces:]
     step = pl.program_id(0)
     rows = D // pieces
 
@@ -276,6 +275,7 @@
     q_ref[0] = queries
     keys, values = kv[:, :256], kv[:, 128:]
     context = jnp.zeros((ROWS, 256), F32)
+    totals = jnp.zeros((ROWS, 256), F32)
     for h in range(3):
         own = jnp.where(lanes_of_head(h, 0), queries, jnp.zeros_like(queries))
         scores = dot_nt(own, keys) + bias_ref[...]
@@ -284,9 +284,9 @@
         total = jnp.sum(weight_h, axis=1, keepdims=True)
         part = dot_nn(weight_h.astype(BF), values) / total
         context = jnp.where(lanes_of_head(h, HD), part, context)
-        lse_ref[0, h] = jnp.broadcast_to(top + jnp.log(total), (ROWS, 128))
+        totals = jnp.where(lane == h, top + jnp.log(total), totals)
     ctx_ref[0] = context.astype(BF)
-    ctx_f_ref[0] = context
+    ctx_f_ref[0] = context + totals
 
 
 def attend(scal, kept, xs, extra, weights):
@@ -305,7 +305,6 @@
             pl.BlockSpec((1, ROWS, 256), lambda j: (j, 0, 0)),
             pl.BlockSpec((1, ROWS, 256), lambda j: (j, 0, 0)),
             pl.BlockSpec((1, ROWS, 256), lambda j: (j, 0, 0)),
-            pl.BlockSpec((1, 3, ROWS, 128), lambda j: (j, 0, 0, 0)),
             pl.BlockSpec((1, D, 256), lambda j: (j, 0, 0)),
         ],
         [
@@ -315,11 +314,11 @@
             shape((4, ROWS, 256)),
             shape((4, ROWS, 256)),
             shape((4, ROWS, 256), F32),
-            shape((4, 3, ROWS, 128), F32),
             shape((4, D, 256)),
         ],
         [pltpu.VMEM((ROWS, KEYS), F32)],
         micros=23,
+        limit=16,
     )(scal, kept, *xs, extra, *weights)
 
 
@@ -345,14 +344,36 @@
     return scale * (scaled - mean - unit * cross)
 
 
-def inner_body(pieces, ctx_ref, wo_ref, xr_ref, fvec_ref, extra_ref, *refs):
-    weights = refs[:pieces]
-    normed_ref, unit_ref, scale_ref, low_ref, act_ref, slope_ref = refs[pieces:]
+def split_out(total, keep_ref, send_ref, first=0):
+    low = total.astype(BF).reshape(PARTS, FB, D)
+    half = PARTS // 2
+    keep_ref[:, 0, first : first + FB] = low[:half]
+    send_ref[:, 0, first : first + FB] = low[half:]
+
+
+ERFC = (-0.82215223, 1.48851587, -1.13520398, 0.27886807, -0.18628806, 0.09678418, 0.37409196, 1.00002368, -1.26551223)
+
+
+def gelu_parts(pre):
+    square = pre * pre * -0.5
+    t = 1.0 / (1.0 + jnp.abs(pre) * (0.5 * math.sqrt(0.5)))
+    poly = 0.17087277 * t
+    for c in ERFC[:-1]:
+        poly = (poly + c) * t
+    tail = 0.5 * t * jnp.exp(square + (poly + ERFC[-1]))
+    half = jnp.where(pre >= 0, 1.0 - tail, tail)
+    return pre * half, half + pre * (jnp.exp(square) * (1.0 / math.sqrt(2.0 * math.pi)))
+
+
+def hidden_body(pieces, scal, ctx_ref, wo_ref, xr_ref, fvec_ref, extra_ref, fin_ref, cot_ref, *refs):
+    inner_w, outer_w, refs = refs[:pieces], refs[pieces : 2 * pieces], refs[2 * pieces :]
+    unit_ref, scale_ref, grad_ref, vec_ref, fin_grad_ref, sums_ref, keep_ref, send_ref, pre_ref, bias_ref = refs[:10]
+    act_ref, slope_ref, normed_ref, first_ref, low_ref, total_ref, unit_two_ref, scale_two_ref = refs[10:]
     step = pl.program_id(0)
+    at = pl.ds(step & 3, 1)
 
     @pl.when(step == 0)
     def _():
-        lane = lax.broadcasted_iota(jnp.int32, (1, 256), 1)
         total = xr_ref[...].astype(F32) + fvec_ref[0:1]
         for n in range(4):
             total = total + dot_nt(ctx_ref[n], wo_ref[n])
@@ -363,67 +384,39 @@
             normed_ref[rows, :] = normed
             unit_ref[rows, :] = unit
             scale_ref[rows, :] = jnp.broadcast_to(scale, (CHUNK, 128))
-            low_ref[rows, :] = normed.astype(BF)
+            first_ref[rows, :] = normed.astype(BF)
             return carried
 
         over_rows(rows_of)
 
-    window = extra_ref[pl.ds(step, 1), :, 256:512][0].astype(F32)
-    bias = jnp.concatenate([window[4 + n : 5 + n] + window[7 + n : 8 + n] for n in range(3)], axis=1)
-    pre = dot_nn(low_ref[...], join(weights, D // pieces)) + bias
-    half = 0.5 + 0.5 * lax.erf(pre * math.sqrt(0.5))
-    act_ref[0] = (pre * half).astype(BF)
-    slope_ref[0] = half + pre * (jnp.exp(pre * pre * -0.5) * (1.0 / math.sqrt(2.0 * math.pi)))
-
-
-def inner(context, wo, packed, fvec, extra, weights):
-    pieces = len(weights)
-    return call(
-        functools.partial(inner_body, pieces),
-        (4,),
-        [full((4, ROWS, 256)), full((4, D, 256)), full((ROWS, D)), full((8, D)), full((4, 16, D))]
-        + [pl.BlockSpec((1, D // pieces, D), lambda j: (j, 0, 0)) for w in weights],
-        [
-            full((ROWS, D)),
-            full((ROWS, D)),
-            full((ROWS, 128)),
-            full((ROWS, D)),
-            pl.BlockSpec((1, ROWS, D), lambda j: (j, 0, 0)),
-            pl.BlockSpec((1, ROWS, D), lambda j: (j, 0, 0)),
-        ],
-        [
-            shape((ROWS, D), F32),
-            shape((ROWS, D), F32),
-            shape((ROWS, 128), F32),
-            shape((ROWS, D)),
-            shape((4, ROWS, D)),
-            shape((4, ROWS, D), F32),
-        ],
-    )(context, wo, packed, fvec, extra, *weights)
-
-
-def outer_body(pieces, scal, act_ref, normed_ref, fvec_ref, fin_ref, cot_ref, *refs):
-    weights = refs[:pieces]
-    grad_ref, low_ref, vec_ref, fin_grad_ref, sums_ref, total_ref, unit_ref, scale_ref = refs[pieces:]
-    step = pl.program_id(0)
-    part = dot_nt(act_ref[0], join(weights, D // pieces))
-
-    @pl.when(step == 0)
-    def _():
-        total_ref[...] = normed_ref[...] + fvec_ref[1:2] + part
-
-    @pl.when(step > 0)
-    def _():
-        total_ref[...] += part
-
-    @pl.when(step == 3)
+    @pl.when(step < 4)
+    def _():
+        window = extra_ref[at, :, 256:512][0].astype(F32)
+        bias = jnp.concatenate([window[4 + n : 5 + n] + window[7 + n : 8 + n] for n in range(3)], axis=1)
+        act, slope = gelu_parts(dot_nn(first_ref[...], join(inner_w, D // pieces)) + bias)
+        act_ref[at] = act.astype(BF)[None]
+        slope_ref[at] = slope[None]
+
+    @pl.when((step >= 4) & (step < 8))
+    def _():
+        part = dot_nt(act_ref[at][0], join(outer_w, D // pieces))
+
+        @pl.when(step == 4)
+        def _():
+            total_ref[...] = normed_ref[...] + fvec_ref[1:2] + part
+
+        @pl.when(step > 4)
+        def _():
+            total_ref[...] += part
+
+    @pl.when(step == 7)
     def _():
         gain = fvec_ref[4:5]
 
         def rows_of(rows, carried):
             normed, unit, scale = norm(total_ref[rows, :], gain, fvec_ref[5:6])
-            unit_ref[rows, :] = unit
-            scale_ref[rows, :] = jnp.broadcast_to(scale, (CHUNK, 128))
+            unit_two_ref[rows, :] = unit
+            scale_two_ref[rows, :] = jnp.broadcast_to(scale, (CHUNK, 128))
             low_ref[rows, :] = normed.astype(BF)
             return carried
 
@@ -449,8 +442,8 @@
         total_ref[...] = dot_nn(grads, final)
 
         def rows_back(rows, carried):
-            grad, unit = total_ref[rows, :], unit_ref[rows, :]
-            back = norm_back(grad, gain, unit, scale_ref[rows, :1])
+            grad, unit = total_ref[rows, :], unit_two_ref[rows, :]
+            back = norm_back(grad, gain, unit, scale_two_ref[rows, :1])
             grad_ref[rows, :] = back
             low_ref[rows, :] = back.astype(BF)
             sums = (grad * unit, grad, back)
@@ -461,72 +454,56 @@
             sums_ref[n : n + 1] = sums[n]
         sums_ref[3:] = jnp.zeros((5, D), F32)
 
-
-def outer(scal, act, normed, fvec, final, cot, weights):
-    pieces = len(weights)
+    @pl.when(step >= 8)
+    def _():
+        low = low_ref[...]
+        grad = dot_nn(low, join(outer_w, D // pieces)) * slope_ref[at][0]
+        split_out(dot_tn(low, act_ref[at][0]), keep_ref, send_ref)
+        grad_low = grad.astype(BF)
+        pre_ref[0] = grad_low
+        bias_ref[0] = jnp.broadcast_to(jnp.sum(grad, axis=0, keepdims=True), (8, D))
+        split_out(dot_tn(first_ref[...], grad_low), keep_ref, send_ref, FB)
+
+
+def hidden(scal, context, wo, packed, fvec, extra, final, cot, inner_w, outer_w):
+    pieces = len(inner_w)
+    half = PARTS // 2
+    late = lambda j: (jnp.maximum(j - 8, 0), 0, 0)
+    wide = pl.BlockSpec((half, 1, 2 * FB, D), lambda j: (0, jnp.maximum(j - 8, 0), 0, 0))
     return call(
-        functools.partial(outer_body, pieces),
-        (4,),
-        [SMEM]
-        + [pl.BlockSpec((1, ROWS, D), lambda j: (j, 0, 0)), full((ROWS, D)), full((8, D))]
+        functools.partial(hidden_body, pieces),
+        (12,),
+        [SMEM, full((4, ROWS, 256)), full((4, D, 256)), full((ROWS, D)), full((8, D)), full((4, 16, D))]
         + [full((4, OUT, HL)), full((ROWS, OUT))]
-        + [pl.BlockSpec((1, D // pieces, D), lambda j: (j, 1, 0)) for w in weights],
-        [
-            full((ROWS, D)),
-            full((ROWS, D)),
-            full((OUT, ROWS)),
-            full((4, OUT, HL)),
-            full((8, D)),
-        ],
+        + [pl.BlockSpec((1, D // pieces, D), lambda j: (jnp.minimum(j, 3), 0, 0)) for _ in inner_w]
+        + [pl.BlockSpec((1, D // pieces, D), lambda j: (jnp.where(j < 4, 0, j & 3), 1, 0)) for _ in outer_w],
+        [full((ROWS, D)), full((ROWS, 128)), full((ROWS, D)), full((OUT, ROWS)), full((4, OUT, HL)), full((8, D))]
+        + [wide, wide, pl.BlockSpec((1, ROWS, D), late), pl.BlockSpec((1, 8, D), late)],
         [
             shape((ROWS, D), F32),
-            shape((ROWS, D)),
+            shape((ROWS, 128), F32),
+            shape((ROWS, D), F32),
             shape((OUT, ROWS)),
             shape((4, OUT, HL)),
             shape((8, D), F32),
-        ],
-        [pltpu.VMEM((ROWS, D), F32), pltpu.VMEM((ROWS, D), F32), pltpu.VMEM((ROWS, 128), F32)],
-    )(scal, act, normed, fvec, final, cot, *weights)
-
-
-def split_out(total, keep_ref, send_ref, first=0):
-    low = total.astype(BF).reshape(PARTS, FB, D)
-    half = PARTS // 2
-    keep_ref[:, 0, first : first + FB] = low[:half]
-    send_ref[:, 0, first : first + FB] = low[half:]
-
-
-def outer_back_body(pieces, low_ref, act_ref, slope_ref, normed_ref, *refs):
-    weights = refs[:pieces]
-    keep_ref, send_ref, pre_ref, bias_ref = refs[pieces:]
-    low = low_ref[...]
-    grad = dot_nn(low, join(weights, D // pieces)) * slope_ref[0]
-    split_out(dot_tn(low, act_ref[0]), keep_ref, send_ref)
-    grad_low = grad.astype(BF)
-    pre_ref[0] = grad_low
-    bias_ref[0] = jnp.broadcast_to(jnp.sum(grad, axis=0, keepdims=True), (8, D))
-    split_out(dot_tn(normed_ref[...], grad_low), keep_ref, send_ref, FB)
-
-
-def outer_back(low, act, slope, normed, weights):
-    pieces = len(weights)
-    half = PARTS // 2
-    wide = pl.BlockSpec((half, 1, 2 * FB, D), lambda j: (0, j, 0, 0))
-    block = pl.BlockSpec((1, ROWS, D), lambda j: (j, 0, 0))
-    return call(
-        functools.partial(outer_back_body, pieces),
-        (4,),
-        [full((ROWS, D)), block, block, full((ROWS, D))]
-        + [pl.BlockSpec((1, D // pieces, D), lambda j: (j, 1, 0)) for w in weights],
-        [wide, wide, block, pl.BlockSpec((1, 8, D), lambda j: (j, 0, 0))],
-        [
             shape((half, 4, 2 * FB, D)),
             shape((half, 4, 2 * FB, D)),
             shape((4, ROWS, D)),
             shape((4, 8, D), F32),
         ],
-        micros=15,
-    )(low, act, slope, normed, *weights)
+        [
+            pltpu.VMEM((4, ROWS, D), BF),
+            pltpu.VMEM((4, ROWS, D), F32),
+            pltpu.VMEM((ROWS, D), F32),
+            pltpu.VMEM((ROWS, D), BF),
+            pltpu.VMEM((ROWS, D), BF),
+            pltpu.VMEM((ROWS, D), F32),
+            pltpu.VMEM((ROWS, D), F32),
+            pltpu.VMEM((ROWS, 128), F32),
+        ],
+        micros=30,
+        limit=24,
+    )(scal, context, wo, packed, fvec, extra, final, cot, *inner_w, *outer_w)
 
 
 def inner_back_body(pieces, pre_ref, grad_ref, unit_ref, scale_ref, fvec_ref, sums_ref, *refs):
@@ -579,6 +556,7 @@
         [shape((ROWS, D), F32), shape((ROWS, D)), shape((8, D), F32)],
         [pltpu.VMEM((ROWS, D), F32)],
         micros=9,
+        limit=10,
     )(pre, grad, unit, scale, fvec, sums, *weights)
 
 
@@ -595,7 +573,7 @@
     return jnp.concatenate([final, jnp.broadcast_to(wide[None], (PARTS, 16, 512))], axis=2)
 
 
-def attend_back_body(pieces, first, count, scal, kept_ref, xr_ref, kv_ref, q_ref, ctx_ref, ctx_f_ref, lse_ref, one_ref, low_ref, all_ref, fin_ref, hid_ref, *refs):
+def attend_back_body(pieces, first, count, scal, kept_ref, xr_ref, kv_ref, q_ref, ctx_ref, ctx_f_ref, one_ref, low_ref, all_ref, fin_ref, hid_ref, *refs):
     weights = refs[:pieces]
     refs = refs[pieces + (2 if first else 0) :]
     keep_ref, send_ref = refs[:2]
@@ -625,7 +603,7 @@
         own_grad = jnp.where(lanes_of_head(h, HD), grad_ctx, zero)
         row_dot = jnp.sum(jnp.where(lanes_of_head(h, HD), products, 0.0), axis=1, keepdims=True)
         scores = dot_nt(own, keys) + bias_ref[...]
-        prob = jnp.exp(scores - lse_ref[0, h][:, :1])
+        prob = jnp.exp(scores - ctx_f_ref[0, :, h : h + 1])
         dv = dv + dot_tn(prob.astype(BF), own_grad)
         grad_scores = (prob * (dot_nt(own_grad, values) - row_dot)).astype(BF)
         dq = jnp.where(lanes_of_head(h, 0), dot_nn(grad_scores, keys), dq)
@@ -666,12 +644,12 @@
             ref[:, ROWS:] = part[:, :ROWS]
 
 
-def attend_back(scal, kept, packed, kv, queries, context, context_f, lse, one, low, small, weights, first, count, held):
+def attend_back(scal, kept, packed, kv, queries, context, context_f, one, low, small, weights, first, count, held):
     pieces = len(weights)
     half = PARTS // 2
     at = lambda j: (j + first, 0, 0)
     wide = pl.BlockSpec((half, 1, FB + 16, D), lambda j: (0, j + first, 0, 0))
-    n_in = 13 + pieces
+    n_in = 12 + pieces
     last = first + count == 4
     return call(
         functools.partial(attend_back_body, pieces, first, count),
@@ -684,7 +662,6 @@
             pl.BlockSpec((1, ROWS, 256), at),
             pl.BlockSpec((1, ROWS, 256), at),
             pl.BlockSpec((1, ROWS, 256), at),
-            pl.BlockSpec((1, 3, ROWS, 128), lambda j: (j + first, 0, 0, 0)),
             full(one.shape),
             full((ROWS, D)),
             full((8, D)),
@@ -698,8 +675,9 @@
         + ([shape((HL, KEYS), F32)] * 2 + [shape((HL, KEYS))] * 2 if last else [shape((KEYS, D), F32)]),
         [pltpu.VMEM((ROWS, KEYS), F32), pltpu.VMEM((KEYS, D), F32)],
         micros=9 * count,
+        limit=24,
         aliases={n_in + n: n for n in range(len(held))},
-    )(scal, kept, packed, kv, queries, context, context_f, lse, one, low, *small, *weights, *held)
+    )(scal, kept, packed, kv, queries, context, context_f, one, low, *small, *weights, *held)
 
 
 def pack_vec_body(order_ref, mask_ref, vec_ref, out_ref, total_ref):
@@ -795,6 +773,7 @@
         [full((FB + 16, D)), full((2 * FB, D))],
         [shape((FB + 16, D)), shape((2 * FB, D))],
         micros=3,
+        limit=56,
     )(*weights, *vectors)
 
 
@@ -925,7 +904,7 @@
         x3 = swap(x2, "mp", 1)
         head_pieces, ffn_pieces, final = plain_pieces(heads, ffn)
 
-    packed, fvec, kv, queries, context, context_f, lse, wo = attend(
+    packed, fvec, kv, queries, context, context_f, wo = attend(
         scal, kept, (near, x2, x1, x3), extras, head_pieces
     )
     if by_xor:
@@ -933,14 +912,11 @@
         far = jnp.concatenate([far_a, far_b], axis=0)
         ffn_pieces = [ffn, ffn_x, ffn_y, far] + ffn_pieces + [swap(far, "dp", 1)]
         final = jnp.concatenate([p[:, 2 * FB :, :HL] for p in ffn_pieces], axis=1)
-    normed, unit, scale, normed_low, act, slope = inner(context, wo, packed, fvec, extras, ffn_pieces)
-    grad_two, two_low, vec, fin_grad, sums = outer(scal, act, normed, fvec, final, cot, ffn_pieces)
+    unit, scale, grad_two, vec, fin_grad, sums, ffn_keep, ffn_send, pre, hid_sums = hidden(
+        scal, context, wo, packed, fvec, extras, final, cot, ffn_pieces, ffn_pieces
+    )
     vec_got = swap(vec, "mp", 1)
-    ffn_keep, ffn_send, pre, hid_sums = outer_back(two_low, act, slope, normed_low, ffn_pieces)
-    vec_got, ffn_send, pre = sync(vec_got, ffn_send, pre)
-    vec_low = jnp.stack([vec, vec_got])
-    vec_high = swap(vec_low, "mp", 2)
-    saved = (kept, packed, kv, queries, context, context_f, lse)
+    saved = (kept, packed, kv, queries, context, context_f)
 
     def heads_back(one, low, first, count, held):
         small = (all_sums, fin_grad, hid_sums)
@@ -949,11 +925,13 @@
     if by_xor:
         ffn_got = swap(ffn_send, "dp", 1)
         grad_one, one_low, all_sums = inner_back(pre, grad_two, unit, scale, fvec, sums, ffn_pieces)
-        ffn_got, one_low = sync(ffn_got, one_low)
+        ffn_got, vec_got, one_low = sync(ffn_got, vec_got, one_low)
         pair = (ffn_keep, ffn_got)
         x_send, y_send = plane_first(*pair)
         one_low, x_send, y_send = sync(one_low, x_send, y_send)
         x_got, y_got = swap(x_send, "dp", 2), swap(y_send, "dp", 4)
+        vec_low = jnp.stack([vec, vec_got])
+        vec_high = swap(vec_low, "mp", 2)
         head_keep, head_send, dx0, dx2, dx1, dx3 = heads_back(grad_one, one_low, 0, 4, ())
         dx1, dx3, head_send, x_got, y_got, vec_high = sync(dx1, dx3, head_send, x_got, y_got, vec_high)
 
@@ -996,7 +974,8 @@
         head_keep, head_send, dx0, dx2, dx1, dx3 = heads_back(grad_one, one_low, 0, 4, ())
         far = swap((dx2 + swap(dx3, "mp", 1).astype(F32)).astype(BF), "mp", 2)
         inputs_grad = pack_x(order, dx0, swap(dx1, "mp", 1), far)
-        vectors = pack_vec(order, mask_row, jnp.concatenate([vec_low, vec_high], axis=0))
+        vec_low = jnp.stack([vec, vec_got])
+        vectors = pack_vec(order, mask_row, jnp.concatenate([vec_low, swap(vec_low, "mp", 2)], axis=0))
         ends = []
         for keep, send in ((ffn_keep, ffn_send), (head_keep, head_send)):
             total = scatter_plain(jnp.concatenate([keep, send], axis=0).transpose(1, 0, 2, 3).astype(F32))

time: 299 us -> 263 us (0.88)
  Pallas kernels: 135 us -> 111 us
  other arithmetic: 22.9 us -> 3.19 us
  waiting for transfers between devices: 85.9 us -> 105 us
  local copies, waits for them, and re-layouts: 9.67 us -> 4.14 us
  starting transfers between devices: 43.1 us -> 39.1 us
    ppermute x44, waiting for transfers between devices: 85.9 us -> 105 us  [swap(): return lax.ppermute(array, axis, [(a, a ^ bit) for a in range(size)])]
    pallas_call x3 -> x1, Pallas kernels: 39.2 us -> 31.8 us  [hidden(): call(functools.partial(hidden_body, pieces), (12,), [SMEM, full((4, ROWS,...]
    pallas_call x1, Pallas kernels: 10.1 us -> 5.3 us  [inner_back(): call(functools.partial(inner_back_body, pieces), (4,), [pl.BlockSpec((1,...]
    convert_element_type x2, other arithmetic: 5.29 us -> 0.74 us  [plane_second(): return (x_part[1].astype(BF), y_part[1].astype(BF), x_part[0], y_part[0])]
    ppermute x44, starting transfers between devices: 43.1 us -> 39.1 us  [swap(): return lax.ppermute(array, axis, [(a, a ^ bit) for a in range(size)])]
    pallas_call x1, Pallas kernels: 37.9 us -> 34.4 us  [attend_back(): call(functools.partial(attend_back_body, pieces, first, count), (count,),...]
    convert_element_type x2, other arithmetic: 3.64 us -> 0.49 us  [plane_first(): added(wide, slice(None), 1, LOW).astype(BF)]
    unnamed x83 -> x43, local copies, waits for them, and re-layouts: 6.55 us -> 3.72 us
  transfers between devices with their start and end apart: 44 -> 44, of which waited for: 23 -> 24; matrix products, arithmetic and copies ran while one was open for 9% -> 1% of each run, Pallas kernels for 36% -> 29%
where the time goes in v1:
time: 263 us
  Pallas kernels  111 us (42%)
  waiting for transfers between devices  105 us (40%)
  starting transfers between devices  39.1 us (15%)
  local copies, waits for them, and re-layouts  4.14 us (2%)
  other arithmetic  3.19 us (1%)
    ppermute x44, waiting for transfers between devices, swap(): return lax.ppermute(array, axis, [(a, a ^ bit) for a in range(size)])  105 us
    ppermute x44, starting transfers between devices, swap(): return lax.ppermute(array, axis, [(a, a ^ bit) for a in range(size)])  39.1 us
    pallas_call x1, Pallas kernels, attend_back(): call(functools.partial(attend_back_body, pieces, first, count), (count,),...  34.4 us
    pallas_call x1, Pallas kernels, hidden(): call(functools.partial(hidden_body, pieces), (12,), [SMEM, full((4, ROWS,...  31.8 us
    pallas_call x1, Pallas kernels, attend(): call(functools.partial(attend_body, pieces), (4,), [SMEM, full((8, KEYS))...  20.3 us
    pallas_call x1, Pallas kernels, pack_x(): call(pack_x_body, (4,), [pl.BlockSpec((8, ROWS), lambda b: (0, b))] + [pl...  5.5 us
    pallas_call x1, Pallas kernels, inner_back(): call(functools.partial(inner_back_body, pieces), (4,), [pl.BlockSpec((1,...  5.3 us
  transfers between devices with their start and end apart: 44, of which 24 were waited for; matrix products, arithmetic and copies ran while one was open for 1% of the time, Pallas kernels for 29%

profile of v1, /device:TPU:0, one launch (start us, length us, event | category | flops | bytes accessed | tf_op | source)
XLA Modules:
  0.0 263.2 jit_solution(5201550088138512257)
XLA Ops:
  2.8 5.0 %collective-permute-start.2 = (bf16[112,768]{1,0:T(8,128)(2,1)}, bf16[112,768]{1,0:T(8,128)(2,1)S(1)}, u32[]{:S(2)}, u32[]{:S(2)}) collective-permute-start(bf16[112,768]{1,0:T(8,128)(2,1)} %get-tuple-element.150), channel_id=1, source_target_pairs={{0,3},{1,2},{2,1},{3,0},{4,7},{5,6},{6,5},{7,4},{8,11},{9,10},{10,... | collective-permute-start | bytes 516104 | tf_op jit(solution)/shard_map/ppermute | solution.py:41
  8.6 4.6 %shard_map.341 = (bf16[192,2048]{1,0:T(8,128)(2,1)S(1)}, f32[8,1024]{1,0:T(8,128)S(1)}, f32[512,128]{1,0:T(8,128)S(1)}, s32[8,2048]{1,0:T(8,128)S(1)}) custom-call(s32[6]{0:T(128)S(1)} %pad_add_fusion.scal, s32[1,2048]{1,0:T(1,128)S(1)} %copy-done.2, bf16[192,2048]{1,0:T(8,128)(2,1)S(1)} %copy-done, s32[1,2048]{1,0:T(1,128)S(1)} %bitcast.118, ...), custom_call_target="tpu_custom_call" | custom-call | flops 6000000000 | bytes 18000000 | tf_op jit(solution)/shard_map/pallas_call | solution.py:193
  14.1 3.1 %collective-permute-done.1 = bf16[112,768]{1,0:T(8,128)(2,1)S(1)} collective-permute-done((bf16[112,768]{1,0:T(8,128)(2,1)}, bf16[112,768]{1,0:T(8,128)(2,1)S(1)}, u32[]{:S(2)}, u32[]{:S(2)}) %collective-permute-start.1) | collective-permute-done | bytes 172064 | tf_op jit(solution)/shard_map/ppermute | solution.py:41
  17.2 5.4 %collective-permute-done = bf16[112,768]{1,0:T(8,128)(2,1)S(1)} collective-permute-done((bf16[112,768]{1,0:T(8,128)(2,1)}, bf16[112,768]{1,0:T(8,128)(2,1)S(1)}, u32[]{:S(2)}, u32[]{:S(2)}) %collective-permute-start) | collective-permute-done | bytes 172064 | tf_op jit(solution)/shard_map/ppermute | solution.py:41
  25.8 2.5 collective-permute-start.9
  30.2 7.0 %collective-permute-done.4.refs_2_ = bf16[4,96,768]{2,1,0:T(8,128)(2,1)S(1)} collective-permute-done((bf16[4,96,768]{2,1,0:T(8,128)(2,1)S(1)}, bf16[4,96,768]{2,1,0:T(8,128)(2,1)S(1)}, u32[]{:S(2)}, u32[]{:S(2)}) %collective-permute-start.4) | collective-permute-done | bytes 589856 | tf_op jit(solution)/shard_map/ppermute | solution.py:41
  40.6 4.9 %collective-permute-done.6 = bf16[2,96,768]{2,1,0:T(8,128)(2,1)S(1)} collective-permute-done((bf16[2,96,768]{2,1,0:T(8,128)(2,1)S(1)}, bf16[2,96,768]{2,1,0:T(8,128)(2,1)S(1)}, u32[]{:S(2)}, u32[]{:S(2)}) %collective-permute-start.6) | collective-permute-done | bytes 294944 | tf_op jit(solution)/shard_map/ppermute | solution.py:41
  45.8 5.4 %collective-permute-done.7 = bf16[192,768]{1,0:T(8,128)(2,1)S(1)} collective-permute-done((bf16[192,768]{1,0:T(8,128)(2,1)S(1)}, bf16[192,768]{1,0:T(8,128)(2,1)S(1)}, u32[]{:S(2)}, u32[]{:S(2)}) %collective-permute-start.7) | collective-permute-done | bytes 294944 | tf_op jit(solution)/shard_map/ppermute | solution.py:41
  51.4 2.3 collective-permute-start.10
  54.9 16.5 %collective-permute-done.11.x2 = bf16[192,1024]{1,0:T(8,128)(2,1)S(1)} collective-permute-done((bf16[192,1024]{1,0:T(8,128)(2,1)S(1)}, bf16[192,1024]{1,0:T(8,128)(2,1)S(1)}, u32[]{:S(2)}, u32[]{:S(2)}) %collective-permute-start.11) | collective-permute-done | bytes 393248 | tf_op jit(solution)/shard_map/ppermute | solution.py:41
  75.3 10.9 %collective-permute-done.16.x3 = bf16[192,1024]{1,0:T(8,128)(2,1)S(1)} collective-permute-done((bf16[192,1024]{1,0:T(8,128)(2,1)S(1)}, bf16[192,1024]{1,0:T(8,128)(2,1)S(1)}, u32[]{:S(2)}, u32[]{:S(2)}) %collective-permute-start.16) | collective-permute-done | bytes 393248 | tf_op jit(solution)/shard_map/ppermute | solution.py:41
  88.0 20.3 %shard_map.342 = (bf16[1024,768]{1,0:T(8,128)(2,1)S(1)}, f32[8,768]{1,0:T(8,128)S(1)}, bf16[4,1024,384]{2,1,0:T(8,128)(2,1)S(1)}, bf16[4,512,256]{2,1,0:T(8,128)...) custom-call(s32[6]{0:T(128)S(1)} %pad_add_fusion.scal, ...), custom_call_target="tpu_custom_call" | custom-call | flops 23000000512 | bytes 69000000 | tf_op jit(solution)/shard_map/pallas_call | solution.py:294
  111.3 2.9 %collective-permute-done.24.refs_7_.refs_15_ = bf16[4,208,768]{2,1,0:T(8,128)(2,1)S(1)} collective-permute-done((bf16[4,208,768]{2,1,0:T(8,128)(2,1)S(1)}, bf16[4,208,768]{2,1,0:T(8,128)(2,1)S(1)}, u32[]{:S(2)}, u32[]{:S(2)}) %collective-permute-start.24) | collective-permute-done | bytes 1277984 | tf_op jit(solution)/shard_map/ppermute | solution.py:41
  114.2 31.8 %shard_map.343 = (f32[512,768]{1,0:T(8,128)S(1)}, f32[512,128]{1,0:T(8,128)S(1)}, f32[512,768]{1,0:T(8,128)S(1)}, bf16[128,512]{1,0:T(8,128)(2,1)S(1)}, bf16[4,1...) custom-call(s32[6]{0:T(128)S(1)} %pad_add_fusion.scal, ...), custom_call_target="tpu_custom_call" | custom-call | flops 30000001024 | bytes 90000000 | tf_op jit(solution)/shard_map/pallas_call | solution.py:473
  146.5 5.3 %shard_map.344 = (f32[512,768]{1,0:T(8,128)S(1)}, bf16[512,768]{1,0:T(8,128)(2,1)S(1)}, f32[8,768]{1,0:T(8,128)S(1)}) custom-call(bf16[4,512,768]{2,1,0:T(8,128)(2,1)S(1)} %get-tuple-element.203.pre_ref, f32[512,768]{1,0:T(8,128)S(1)} %get-tuple-element.204.grad_ref, f32[512,768]{1,0:T(8,128)S(1)} %get-tuple-element.205.unit_ref, ...), custom_call_target="tpu_custom_call" | custom-call | flops 8999999488 | bytes 27000000 | tf_op jit(solution)/shard_map/pallas_call | solution.py:543
  158.8 34.4 %shard_map.345 = (bf16[4,4,112,768]{3,2,1,0:T(8,128)(2,1)S(1)}, bf16[4,4,112,768]{3,2,1,0:T(8,128)(2,1)S(1)}, f32[192,1024]{1,0:T(8,128)S(1)}, f32[192,1024]{1,0...) custom-call(s32[6]{0:T(128)S(1)} %pad_add_fusion.scal, ...), custom_call_target="tpu_custom_call" | custom-call | flops 35999997952 | bytes 108000000 | tf_op jit(solution)/shard_map/pallas_call | solution.py:654
  197.2 7.8 %collective-permute-done.32 = bf16[192,1024]{1,0:T(8,128)(2,1)S(1)} collective-permute-done((bf16[192,1024]{1,0:T(8,128)(2,1)S(1)}, bf16[192,1024]{1,0:T(8,128)(2,1)S(1)}, u32[]{:S(2)}, u32[]{:S(2)}) %collective-permute-start.32) | collective-permute-done | bytes 393248 | tf_op jit(solution)/shard_map/ppermute | solution.py:41
  209.3 2.6 %collective-permute-done.31 = bf16[2,192,768]{2,1,0:T(8,128)(2,1)S(1)} collective-permute-done((bf16[2,192,768]{2,1,0:T(8,128)(2,1)S(1)}, bf16[2,192,768]{2,1,0:T(8,128)(2,1)S(1)}, u32[]{:S(2)}, u32[]{:S(2)}) %collective-permute-start.31) | collective-permute-done | bytes 589856 | tf_op jit(solution)/shard_map/ppermute | solution.py:41
  212.3 5.1 %shard_map.346 = f32[2048,128]{1,0:T(8,128)} custom-call(s32[8,2048]{1,0:T(8,128)S(1)} %get-tuple-element.227.order_ref, s32[1,2048]{1,0:T(1,128)S(1)} %bitcast.119, bf16[4,128,512]{2,1,0:T(8,128)(2,1)S(1)} %pad_maximum_fusion.1.vec_ref), custom_call_target="tpu_custom_call" | custom-call | flops 5000000000 | bytes 15000000 | tf_op jit(solution)/shard_map/pallas_call | solution.py:701
  219.0 5.0 %collective-permute-done.36.x1_ref = bf16[192,1024]{1,0:T(8,128)(2,1)S(1)} collective-permute-done((bf16[192,1024]{1,0:T(8,128)(2,1)S(1)}, bf16[192,1024]{1,0:T(8,128)(2,1)S(1)}, u32[]{:S(2)}, u32[]{:S(2)}) %collective-permute-start.36) | collective-permute-done | bytes 393248 | tf_op jit(solution)/shard_map/ppermute | solution.py:41
  224.1 3.0 %collective-permute-done.37.far_ref = bf16[192,1024]{1,0:T(8,128)(2,1)S(1)} collective-permute-done((bf16[192,1024]{1,0:T(8,128)(2,1)S(1)}, bf16[192,1024]{1,0:T(8,128)(2,1)S(1)}, u32[]{:S(2)}, u32[]{:S(2)}) %collective-permute-start.37) | collective-permute-done | bytes 393248 | tf_op jit(solution)/shard_map/ppermute | solution.py:41
  229.4 5.5 %shard_map.347 = f32[192,2048]{1,0:T(8,128)} custom-call(s32[8,2048]{1,0:T(8,128)S(1)} %get-tuple-element.227.order_ref, f32[192,1024]{1,0:T(8,128)S(1)} %get-tuple-element.248.x0_ref, bf16[192,1024]{1,0:T(8,128)(2,1)S(1)} %collective-permute-done.36.x1_ref, bf16[192,1024]{1,0:T(8,128)(2,1)S(1)} %collective-permute-done.37.far_ref), custom_call_target="tpu_custom_call" | custom-call | flops 5000000000 | bytes 15000000 | tf_op jit(solution)/shard_map/pallas_call | solution.py:731
  239.8 14.2 %collective-permute-done.42.b_ref = bf16[192,768]{1,0:T(8,128)(2,1)S(1)} collective-permute-done((bf16[192,768]{1,0:T(8,128)(2,1)S(1)}, bf16[192,768]{1,0:T(8,128)(2,1)S(1)}, u32[]{:S(2)}, u32[]{:S(2)}) %collective-permute-start.42) | collective-permute-done | bytes 294944 | tf_op jit(solution)/shard_map/ppermute | solution.py:41
  255.9 6.2 %collective-permute-done.43.b_ref = bf16[112,768]{1,0:T(8,128)(2,1)S(1)} collective-permute-done((bf16[112,768]{1,0:T(8,128)(2,1)S(1)}, bf16[112,768]{1,0:T(8,128)(2,1)S(1)}, u32[]{:S(2)}, u32[]{:S(2)}) %collective-permute-start.43) | collective-permute-done | bytes 172064 | tf_op jit(solution)/shard_map/ppermute | solution.py:41
  (152 shorter events, 50.2 us)
Async XLA Ops:
  25.8 20.0 %collective-permute-start.9 = (bf16[192,768]{1,0:T(8,128)(2,1)S(1)}, bf16[192,768]{1,0:T(8,128)(2,1)S(1)}, u32[]{:S(2)}, u32[]{:S(2)}) collective-permute-start(bf16[192,768]{1,0:T(8,128)(2,1)S(1)} %copy-done.14), channel_id=1, source_target_pairs={{0,3},{1,2},{2,1},{3,0},{4,7},{5,6},{6,5},{7,4},{8,11},{9,10},{10,... | collective-permute-start | bytes 884744 | tf_op jit(solution)/shard_map/ppermute | solution.py:41
  28.3 17.5 %collective-permute-start.8 = (bf16[192,768]{1,0:T(8,128)(2,1)S(1)}, bf16[192,768]{1,0:T(8,128)(2,1)S(1)}, u32[]{:S(2)}, u32[]{:S(2)}) collective-permute-start(bf16[192,768]{1,0:T(8,128)(2,1)S(1)} %copy-done.14), channel_id=1, source_target_pairs={{0,1},{1,0},{2,3},{3,2},{4,5},{5,4},{6,7},{7,6},{8,9},{9,8},{10,11... | collective-permute-start | bytes 884744 | tf_op jit(solution)/shard_map/ppermute | solution.py:41
  28.3 22.9 %collective-permute-start.7 = (bf16[192,768]{1,0:T(8,128)(2,1)S(1)}, bf16[192,768]{1,0:T(8,128)(2,1)S(1)}, u32[]{:S(2)}, u32[]{:S(2)}) collective-permute-start(bf16[192,768]{1,0:T(8,128)(2,1)S(1)} %copy-done.14), channel_id=1, source_target_pairs={{0,2},{1,3},{2,0},{3,1},{4,6},{5,7},{6,4},{7,5},{8,10},{9,11},{10,... | collective-permute-start | bytes 884744 | tf_op jit(solution)/shard_map/ppermute | solution.py:41
  51.2 20.7 %collective-permute-start.15 = (bf16[4,96,768]{2,1,0:T(8,128)(2,1)S(1)}, bf16[4,96,768]{2,1,0:T(8,128)(2,1)S(1)}, u32[]{:S(2)}, u32[]{:S(2)}) collective-permute-start(bf16[4,96,768]{2,1,0:T(8,128)(2,1)S(1)} %constant_dynamic-update-slice_fusion.refs_3_), channel_id=1, source_target_pairs={{0,4},{4,0},{8,12},{12,8},{16,20},{20,16},{24,28},{28,24},{1,5},{5... | collective-permute-start | bytes 1769480 | tf_op jit(solution)/shard_map/ppermute | solution.py:41
  51.3 20.1 %collective-permute-start.11 = (bf16[192,1024]{1,0:T(8,128)(2,1)S(1)}, bf16[192,1024]{1,0:T(8,128)(2,1)S(1)}, u32[]{:S(2)}, u32[]{:S(2)}) collective-permute-start(bf16[192,1024]{1,0:T(8,128)(2,1)S(1)} %get-tuple-element.167), channel_id=1, source_target_pairs={{0,2},{1,3},{2,0},{3,1},{4,6},{5,7},{6,4},{7,5},{8,10},{9,11},{10,... | collective-permute-start | bytes 1179656 | tf_op jit(solution)/shard_map/ppermute | solution.py:41
  51.4 20.2 %collective-permute-start.10 = (bf16[192,1024]{1,0:T(8,128)(2,1)S(1)}, bf16[192,1024]{1,0:T(8,128)(2,1)S(1)}, u32[]{:S(2)}, u32[]{:S(2)}) collective-permute-start(bf16[192,1024]{1,0:T(8,128)(2,1)S(1)} %get-tuple-element.166.x0), channel_id=1, source_target_pairs={{0,1},{1,0},{2,3},{3,2},{4,5},{5,4},{6,7},{7,6},{8,9},{9,8},{10,11... | collective-permute-start | bytes 1179656 | tf_op jit(solution)/shard_map/ppermute | solution.py:41
  53.8 32.4 %collective-permute-start.18 = (bf16[4,208,768]{2,1,0:T(8,128)(2,1)S(1)}, bf16[4,208,768]{2,1,0:T(8,128)(2,1)S(1)}, u32[]{:S(2)}, u32[]{:S(2)}) collective-permute-start(bf16[4,208,768]{2,1,0:T(8,128)(2,1)S(1)} %maximum_maximum_fusion.refs_0_.refs_8_), channel_id=1, source_target_pairs={{0,16},{4,20},{8,24},{12,28},{16,0},{20,4},{24,8},{28,12},{1,17},{... | collective-permute-start | bytes 3833864 | tf_op jit(solution)/shard_map/ppermute | solution.py:41
  54.4 31.9 %collective-permute-start.17 = (bf16[4,208,768]{2,1,0:T(8,128)(2,1)S(1)}, bf16[4,208,768]{2,1,0:T(8,128)(2,1)S(1)}, u32[]{:S(2)}, u32[]{:S(2)}) collective-permute-start(bf16[4,208,768]{2,1,0:T(8,128)(2,1)S(1)} %maximum_maximum_fusion.refs_0_.refs_8_), channel_id=1, source_target_pairs={{0,8},{4,12},{8,0},{12,4},{16,24},{20,28},{24,16},{28,20},{1,9},{5... | collective-permute-start | bytes 3833864 | tf_op jit(solution)/shard_map/ppermute | solution.py:41
  75.1 35.9 %collective-permute-start.21 = (bf16[4,208,768]{2,1,0:T(8,128)(2,1)S(1)}, bf16[4,208,768]{2,1,0:T(8,128)(2,1)S(1)}, u32[]{:S(2)}, u32[]{:S(2)}) collective-permute-start(bf16[4,208,768]{2,1,0:T(8,128)(2,1)S(1)} %maximum_maximum_fusion.refs_0_.refs_8_), channel_id=1, source_target_pairs={{0,4},{4,0},{8,12},{12,8},{16,20},{20,16},{24,28},{28,24},{1,5},{5... | collective-permute-start | bytes 3833864 | tf_op jit(solution)/shard_map/ppermute | solution.py:41
  86.3 24.7 %collective-permute-start.23 = (bf16[4,208,768]{2,1,0:T(8,128)(2,1)S(1)}, bf16[4,208,768]{2,1,0:T(8,128)(2,1)S(1)}, u32[]{:S(2)}, u32[]{:S(2)}) collective-permute-start(bf16[4,208,768]{2,1,0:T(8,128)(2,1)S(1)} %collective-permute-done.18.refs_2_.refs_10_), channel_id=1, source_target_pairs={{0,4},{4,0},{8,12},{12,8},{16,20},{20,16},{24,28},{28,24},{1,5},{5... | collective-permute-start | bytes 3833864 | tf_op jit(solution)/shard_map/ppermute | solution.py:41
  86.4 24.6 %collective-permute-start.22 = (bf16[4,208,768]{2,1,0:T(8,128)(2,1)S(1)}, bf16[4,208,768]{2,1,0:T(8,128)(2,1)S(1)}, u32[]{:S(2)}, u32[]{:S(2)}) collective-permute-start(bf16[4,208,768]{2,1,0:T(8,128)(2,1)S(1)} %collective-permute-done.17.refs_1_.refs_9_), channel_id=1, source_target_pairs={{0,4},{4,0},{8,12},{12,8},{16,20},{20,16},{24,28},{28,24},{1,5},{5... | collective-permute-start | bytes 3833864 | tf_op jit(solution)/shard_map/ppermute | solution.py:41
  87.0 24.0 %collective-permute-start.20 = (bf16[2,208,768]{2,1,0:T(8,128)(2,1)S(1)}, bf16[2,208,768]{2,1,0:T(8,128)(2,1)S(1)}, u32[]{:S(2)}, u32[]{:S(2)}) collective-permute-start(bf16[2,208,768]{2,1,0:T(8,128)(2,1)S(1)} %slice.189), channel_id=1, source_target_pairs={{0,16},{4,20},{8,24},{12,28},{16,0},{20,4},{24,8},{28,12},{1,17},{... | collective-permute-start | bytes 1916936 | tf_op jit(solution)/shard_map/ppermute | solution.py:41
  87.5 23.5 %collective-permute-start.19 = (bf16[2,208,768]{2,1,0:T(8,128)(2,1)S(1)}, bf16[2,208,768]{2,1,0:T(8,128)(2,1)S(1)}, u32[]{:S(2)}, u32[]{:S(2)}) collective-permute-start(bf16[2,208,768]{2,1,0:T(8,128)(2,1)S(1)} %slice.188), channel_id=1, source_target_pairs={{0,8},{4,12},{8,0},{12,4},{16,24},{20,28},{24,16},{28,20},{1,9},{5... | collective-permute-start | bytes 1916936 | tf_op jit(solution)/shard_map/ppermute | solution.py:41
  154.9 38.4 %collective-permute-start.29 = (bf16[2,128,512]{2,1,0:T(8,128)(2,1)S(1)}, bf16[2,128,512]{2,1,0:T(8,128)(2,1)S(1)}, u32[]{:S(2)}, u32[]{:S(2)}) collective-permute-start(bf16[2,128,512]{2,1,0:T(8,128)(2,1)S(1)} %pad_maximum_fusion.2), channel_id=1, source_target_pairs={{0,2},{1,3},{2,0},{3,1},{4,6},{5,7},{6,4},{7,5},{8,10},{9,11},{10,... | collective-permute-start | bytes 786440 | tf_op jit(solution)/shard_map/ppermute | solution.py:41
  155.8 37.5 %collective-permute-start.27 = (bf16[2,2,192,768]{3,2,1,0:T(8,128)(2,1)S(1)}, bf16[2,2,192,768]{3,2,1,0:T(8,128)(2,1)S(1)}, u32[]{:S(2)}, u32[]{:S(2)}) collective-permute-start(bf16[2,2,192,768]{3,2,1,0:T(8,128)(2,1)S(1)} %fusion), channel_id=1, source_target_pairs={{0,8},{4,12},{8,0},{12,4},{16,24},{20,28},{24,16},{28,20},{1,9},{5... | collective-permute-start | bytes 3538952 | tf_op jit(solution)/shard_map/ppermute | solution.py:41
  157.3 36.0 %collective-permute-start.28 = (bf16[2,2,192,768]{3,2,1,0:T(8,128)(2,1)S(1)}, bf16[2,2,192,768]{3,2,1,0:T(8,128)(2,1)S(1)}, u32[]{:S(2)}, u32[]{:S(2)}) collective-permute-start(bf16[2,2,192,768]{3,2,1,0:T(8,128)(2,1)S(1)} %fusion.1), channel_id=1, source_target_pairs={{0,16},{4,20},{8,24},{12,28},{16,0},{20,4},{24,8},{28,12},{1,17},{... | collective-permute-start | bytes 3538952 | tf_op jit(solution)/shard_map/ppermute | solution.py:41
  195.7 16.2 %collective-permute-start.31 = (bf16[2,192,768]{2,1,0:T(8,128)(2,1)S(1)}, bf16[2,192,768]{2,1,0:T(8,128)(2,1)S(1)}, u32[]{:S(2)}, u32[]{:S(2)}) collective-permute-start(bf16[2,192,768]{2,1,0:T(8,128)(2,1)S(1)} %get-tuple-element.274), channel_id=1, source_target_pairs={{0,8},{4,12},{8,0},{12,4},{16,24},{20,28},{24,16},{28,20},{1,9},{5... | collective-permute-start | bytes 1769480 | tf_op jit(solution)/shard_map/ppermute | solution.py:41
  196.3 21.2 %collective-permute-start.30 = (bf16[2,192,768]{2,1,0:T(8,128)(2,1)S(1)}, bf16[2,192,768]{2,1,0:T(8,128)(2,1)S(1)}, u32[]{:S(2)}, u32[]{:S(2)}) collective-permute-start(bf16[2,192,768]{2,1,0:T(8,128)(2,1)S(1)} %get-tuple-element.275), channel_id=1, source_target_pairs={{0,16},{4,20},{8,24},{12,28},{16,0},{20,4},{24,8},{28,12},{1,17},{... | collective-permute-start | bytes 1769480 | tf_op jit(solution)/shard_map/ppermute | solution.py:41
  204.9 19.1 %collective-permute-start.36 = (bf16[192,1024]{1,0:T(8,128)(2,1)S(1)}, bf16[192,1024]{1,0:T(8,128)(2,1)S(1)}, u32[]{:S(2)}, u32[]{:S(2)}) collective-permute-start(bf16[192,1024]{1,0:T(8,128)(2,1)S(1)} %get-tuple-element.239), channel_id=1, source_target_pairs={{0,1},{1,0},{2,3},{3,2},{4,5},{5,4},{6,7},{7,6},{8,9},{9,8},{10,11... | collective-permute-start | bytes 1179656 | tf_op jit(solution)/shard_map/ppermute | solution.py:41
  207.1 19.9 %collective-permute-start.37 = (bf16[192,1024]{1,0:T(8,128)(2,1)S(1)}, bf16[192,1024]{1,0:T(8,128)(2,1)S(1)}, u32[]{:S(2)}, u32[]{:S(2)}) collective-permute-start(bf16[192,1024]{1,0:T(8,128)(2,1)S(1)} %add_convert_fusion.4), channel_id=1, source_target_pairs={{0,2},{1,3},{2,0},{3,1},{4,6},{5,7},{6,4},{7,5},{8,10},{9,11},{10,... | collective-permute-start | bytes 1179656 | tf_op jit(solution)/shard_map/ppermute | solution.py:41
  207.8 19.3 %collective-permute-start.34 = (bf16[2,2,112,768]{3,2,1,0:T(8,128)(2,1)S(1)}, bf16[2,2,112,768]{3,2,1,0:T(8,128)(2,1)S(1)}, u32[]{:S(2)}, u32[]{:S(2)}) collective-permute-start(bf16[2,2,112,768]{3,2,1,0:T(8,128)(2,1)S(1)} %fusion.8), channel_id=1, source_target_pairs={{0,8},{4,12},{8,0},{12,4},{16,24},{20,28},{24,16},{28,20},{1,9},{5... | collective-permute-start | bytes 2064392 | tf_op jit(solution)/shard_map/ppermute | solution.py:41
  211.9 15.9 %collective-permute-start.35 = (bf16[2,2,112,768]{3,2,1,0:T(8,128)(2,1)S(1)}, bf16[2,2,112,768]{3,2,1,0:T(8,128)(2,1)S(1)}, u32[]{:S(2)}, u32[]{:S(2)}) collective-permute-start(bf16[2,2,112,768]{3,2,1,0:T(8,128)(2,1)S(1)} %fusion.9), channel_id=1, source_target_pairs={{0,16},{4,20},{8,24},{12,28},{16,0},{20,4},{24,8},{28,12},{1,17},{... | collective-permute-start | bytes 2064392 | tf_op jit(solution)/shard_map/ppermute | solution.py:41
  217.8 18.9 %collective-permute-start.40 = (bf16[2,192,768]{2,1,0:T(8,128)(2,1)S(1)}, bf16[2,192,768]{2,1,0:T(8,128)(2,1)S(1)}, u32[]{:S(2)}, u32[]{:S(2)}) collective-permute-start(bf16[2,192,768]{2,1,0:T(8,128)(2,1)S(1)} %fusion.5), channel_id=1, source_target_pairs={{0,1},{1,0},{2,3},{3,2},{4,5},{5,4},{6,7},{7,6},{8,9},{9,8},{10,11... | collective-permute-start | bytes 1769480 | tf_op jit(solution)/shard_map/ppermute | solution.py:41
  236.9 17.1 %collective-permute-start.41 = (bf16[2,112,768]{2,1,0:T(8,128)(2,1)S(1)}, bf16[2,112,768]{2,1,0:T(8,128)(2,1)S(1)}, u32[]{:S(2)}, u32[]{:S(2)}) collective-permute-start(bf16[2,112,768]{2,1,0:T(8,128)(2,1)S(1)} %fusion.11), channel_id=1, source_target_pairs={{0,1},{1,0},{2,3},{3,2},{4,5},{5,4},{6,7},{7,6},{8,9},{9,8},{10,11... | collective-permute-start | bytes 1032200 | tf_op jit(solution)/shard_map/ppermute | solution.py:41
  (37 other events, 297.3 us)

commit v2 on v1

--- a/solution.py
+++ b/solution.py
@@ -49,7 +49,7 @@
 SMEM = pl.BlockSpec(memory_space=pltpu.SMEM)
 
 
-def call(body, grid, in_specs, out_specs, out_shape, scratch=(), micros=10, aliases=None, limit=16):
+def call(body, grid, in_specs, out_specs, out_shape, scratch=(), micros=10, aliases=None, limit=12):
     return pl.pallas_call(
         body,
         grid=grid,
@@ -61,7 +61,7 @@
         compiler_params=pltpu.CompilerParams(
             dimension_semantics=("arbitrary",) * len(grid), vmem_limit_bytes=limit * 1024 * 1024
         ),
-        cost_estimate=pl.CostEstimate(flops=micros * 10**9, transcendentals=0, bytes_accessed=micros * 3 * 10**6),
+        cost_estimate=pl.CostEstimate(flops=micros * 4 * 10**9, transcendentals=0, bytes_accessed=micros * 12 * 10**6),
     )
 
 
@@ -234,30 +234,48 @@
     return jnp.where((q_seg == k_seg) | (q_pos == k_pos), 0.0, -1e30)
 
 
-def attend_body(pieces, scal, kept_ref, x0, x2, x1, x3, extra_ref, *refs):
+def prepare_body(by_xor, scal, kept_ref, x0, x2, x1, extra_ref, part_ref, fvec_ref, bias_ref):
+    frow = feature_row(scal, by_xor)
+    upper = jnp.zeros((ROWS, D), F32)
+    lower = jnp.zeros((ROWS, D), F32)
+    fvec = jnp.zeros((16, D), F32)
+    for n in range(4):
+        chosen = pick(scal, frow, n)
+        fvec = fvec + dot_nn(extra_ref[n, :, 512 : 512 + HL], chosen)
+        if n < 3:
+            ref = (x0, x2, x1)[n]
+            near, away = (ref[:, ROWS:], ref[:, :ROWS]) if n == 2 else (ref[:, :ROWS], ref[:, ROWS:])
+            upper = upper + dot_tn(near, chosen)
+            lower = lower + dot_tn(away, chosen)
+    part_ref[:ROWS] = upper.astype(BF)
+    part_ref[ROWS:] = lower.astype(BF)
+    fvec_ref[...] = fvec[:8] + fvec[8:]
+    bias_ref[...] = allowed_bias(scal, kept_ref[:1])
+
+
+def prepare(by_xor, scal, kept, x0, x2, x1, extra):
+    dims = [(KEYS, D), (8, D), (ROWS, KEYS)]
+    return call(
+        functools.partial(prepare_body, by_xor),
+        (1,),
+        [SMEM, full((8, KEYS))] + [full((HL, KEYS))] * 3 + [full((4, 16, D))],
+        [full(d) for d in dims],
+        [shape(dims[0]), shape(dims[1], F32), shape(dims[2], F32)],
+        micros=0,
+    )(scal, kept, x0, x2, x1, extra)
+
+
+def attend_body(pieces, scal, part_ref, bias_ref, x3, extra_ref, *refs):
     weights = refs[:pieces]
-    xr_ref, fvec_ref, kv_ref, q_ref, ctx_ref, ctx_f_ref, wo_ref, bias_ref = refs[pieces:]
+    xr_ref, kv_ref, q_ref, ctx_ref, lse_ref, wo_ref = refs[pieces:]
     step = pl.program_id(0)
     rows = D // pieces
 
     @pl.when(step == 0)
     def _():
-        frow = feature_row(scal, pieces > 1)
-        upper = jnp.zeros((ROWS, D), F32)
-        lower = jnp.zeros((ROWS, D), F32)
-        fvec = jnp.zeros((16, D), F32)
-        for n, (ref, crossed) in enumerate(((x0, False), (x2, False), (x1, True), (x3, True))):
-            chosen = pick(scal, frow, n)
-            near, away = ref[:, :ROWS], ref[:, ROWS:]
-            if crossed:
-                near, away = away, near
-            upper = upper + dot_tn(near, chosen)
-            lower = lower + dot_tn(away, chosen)
-            fvec = fvec + dot_nn(extra_ref[n, :, 512 : 512 + HL], chosen)
-        xr_ref[:ROWS] = upper.astype(BF)
-        xr_ref[ROWS:] = lower.astype(BF)
-        fvec_ref[...] = fvec[:8] + fvec[8:]
-        bias_ref[...] = allowed_bias(scal, kept_ref[:1])
+        chosen = pick(scal, feature_row(scal, pieces > 1), 3)
+        xr_ref[:ROWS] = (part_ref[:ROWS].astype(F32) + dot_tn(x3[:, ROWS:], chosen)).astype(BF)
+        xr_ref[ROWS:] = (part_ref[ROWS:].astype(F32) + dot_tn(x3[:, :ROWS], chosen)).astype(BF)
 
     weight = join(weights, rows)
     wo_ref[0] = weight[:, 512:]
@@ -275,7 +293,7 @@
     q_ref[0] = queries
     keys, values = kv[:, :256], kv[:, 128:]
     context = jnp.zeros((ROWS, 256), F32)
-    totals = jnp.zeros((ROWS, 256), F32)
+    totals = jnp.zeros((ROWS, 128), F32)
     for h in range(3):
         own = jnp.where(lanes_of_head(h, 0), queries, jnp.zeros_like(queries))
         scores = dot_nt(own, keys) + bias_ref[...]
@@ -284,42 +302,37 @@
         total = jnp.sum(weight_h, axis=1, keepdims=True)
         part = dot_nn(weight_h.astype(BF), values) / total
         context = jnp.where(lanes_of_head(h, HD), part, context)
-        totals = jnp.where(lane == h, top + jnp.log(total), totals)
+        totals = jnp.where(lane[:, :128] == h, top + jnp.log(total), totals)
     ctx_ref[0] = context.astype(BF)
-    ctx_f_ref[0] = context + totals
-
-
-def attend(scal, kept, xs, extra, weights):
+    lse_ref[0] = jnp.transpose(totals)[:8]
+
+
+def attend(scal, part, bias, x3, extra, weights):
     pieces = len(weights)
     return call(
         functools.partial(attend_body, pieces),
         (4,),
-        [SMEM, full((8, KEYS))]
-        + [full((HL, KEYS))] * 4
-        + [full((4, 16, D))]
+        [SMEM, full((KEYS, D)), full((ROWS, KEYS)), full((HL, KEYS)), full((4, 16, D))]
         + [pl.BlockSpec((1,) + w.shape[1:], lambda j: (j, 0, 0)) for w in weights],
         [
             full((KEYS, D)),
-            full((8, D)),
             pl.BlockSpec((1, KEYS, 384), lambda j: (j, 0, 0)),
             pl.BlockSpec((1, ROWS, 256), lambda j: (j, 0, 0)),
             pl.BlockSpec((1, ROWS, 256), lambda j: (j, 0, 0)),
-            pl.BlockSpec((1, ROWS, 256), lambda j: (j, 0, 0)),
+            pl.BlockSpec((1, 8, ROWS), lambda j: (j, 0, 0)),
             pl.BlockSpec((1, D, 256), lambda j: (j, 0, 0)),
         ],
         [
             shape((KEYS, D)),
-            shape((8, D), F32),
             shape((4, KEYS, 384)),
             shape((4, ROWS, 256)),
             shape((4, ROWS, 256)),
-            shape((4, ROWS, 256), F32),
+            shape((4, 8, ROWS), F32),
             shape((4, D, 256)),
         ],
-        [pltpu.VMEM((ROWS, KEYS), F32)],
         micros=23,
-        limit=16,
-    )(scal, kept, *xs, extra, *weights)
+        limit=14,
+    )(scal, part, bias, x3, extra, *weights)
 
 
 def over_rows(body, carried=()):
@@ -365,29 +378,40 @@
     return pre * half, half + pre * (jnp.exp(square) * (1.0 / math.sqrt(2.0 * math.pi)))
 
 
-def hidden_body(pieces, scal, ctx_ref, wo_ref, xr_ref, fvec_ref, extra_ref, fin_ref, cot_ref, *refs):
+def first_norm_body(ctx_ref, wo_ref, xr_ref, fvec_ref, unit_ref, scale_ref, low_ref):
+    total = xr_ref[...].astype(F32) + fvec_ref[0:1]
+    for n in range(4):
+        total = total + dot_nt(ctx_ref[n], wo_ref[n])
+    unit_ref[...] = total
+
+    def rows_of(rows, carried):
+        normed, unit, scale = norm(unit_ref[rows, :], fvec_ref[2:3], fvec_ref[3:4])
+        unit_ref[rows, :] = unit
+        scale_ref[rows, :] = jnp.broadcast_to(scale, (CHUNK, 128))
+        low_ref[rows, :] = normed.astype(BF)
+        return carried
+
+    over_rows(rows_of)
+
+
+def first_norm(context, wo, packed, fvec):
+    dims = [(ROWS, D), (ROWS, 128), (ROWS, D)]
+    return call(
+        first_norm_body,
+        (1,),
+        [full((4, ROWS, 256)), full((4, D, 256)), full((ROWS, D)), full((8, D))],
+        [full(d) for d in dims],
+        [shape(d, F32) for d in dims[:2]] + [shape(dims[2])],
+        micros=3,
+    )(context, wo, packed, fvec)
+
+
+def hidden_body(pieces, scal, unit_ref, first_ref, fvec_ref, extra_ref, fin_ref, cot_ref, *refs):
     inner_w, outer_w, refs = refs[:pieces], refs[pieces : 2 * pieces], refs[2 * pieces :]
-    unit_ref, scale_ref, grad_ref, vec_ref, fin_grad_ref, sums_ref, keep_ref, send_ref, pre_ref, bias_ref = refs[:10]
-    act_ref, slope_ref, normed_ref, first_ref, low_ref, total_ref, unit_two_ref, scale_two_ref = refs[10:]
+    grad_ref, vec_ref, fin_grad_ref, sums_ref, keep_ref, send_ref, pre_ref, bias_ref = refs[:8]
+    act_ref, slope_ref, low_ref, total_ref, unit_two_ref, scale_two_ref = refs[8:]
     step = pl.program_id(0)
     at = pl.ds(step & 3, 1)
-
-    @pl.when(step == 0)
-    def _():
-        total = xr_ref[...].astype(F32) + fvec_ref[0:1]
-        for n in range(4):
-            total = total + dot_nt(ctx_ref[n], wo_ref[n])
-        normed_ref[...] = total
-
-        def rows_of(rows, carried):
-            normed, unit, scale = norm(normed_ref[rows, :], fvec_ref[2:3], fvec_ref[3:4])
-            normed_ref[rows, :] = normed
-            unit_ref[rows, :] = unit
-            scale_ref[rows, :] = jnp.broadcast_to(scale, (CHUNK, 128))
-            first_ref[rows, :] = normed.astype(BF)
-            return carried
-
-        over_rows(rows_of)
 
     @pl.when(step < 4)
     def _():
@@ -395,7 +419,7 @@
         bias = jnp.concatenate([window[4 + n : 5 + n] + window[7 + n : 8 + n] for n in range(3)], axis=1)
         act, slope = gelu_parts(dot_nn(first_ref[...], join(inner_w, D // pieces)) + bias)
         act_ref[at] = act.astype(BF)[None]
-        slope_ref[at] = slope[None]
+        slope_ref[at] = slope.astype(BF)[None]
 
     @pl.when((step >= 4) & (step < 8))
     def _():
@@ -403,7 +427,7 @@
 
         @pl.when(step == 4)
         def _():
-            total_ref[...] = normed_ref[...] + fvec_ref[1:2] + part
+            total_ref[...] = unit_ref[...] * fvec_ref[2:3] + fvec_ref[3:4] + fvec_ref[1:2] + part
 
         @pl.when(step > 4)
         def _():
@@ -457,7 +481,7 @@
     @pl.when(step >= 8)
     def _():
         low = low_ref[...]
-        grad = dot_nn(low, join(outer_w, D // pieces)) * slope_ref[at][0]
+        grad = dot_nn(low, join(outer_w, D // pieces)) * slope_ref[at][0].astype(F32)
         split_out(dot_tn(low, act_ref[at][0]), keep_ref, send_ref)
         grad_low = grad.astype(BF)
         pre_ref[0] = grad_low
@@ -465,7 +489,7 @@
         split_out(dot_tn(first_ref[...], grad_low), keep_ref, send_ref, FB)
 
 
-def hidden(scal, context, wo, packed, fvec, extra, final, cot, inner_w, outer_w):
+def hidden(scal, unit, low, fvec, extra, final, cot, inner_w, outer_w):
     pieces = len(inner_w)
     half = PARTS // 2
     late = lambda j: (jnp.maximum(j - 8, 0), 0, 0)
@@ -473,15 +497,13 @@
     return call(
         functools.partial(hidden_body, pieces),
         (12,),
-        [SMEM, full((4, ROWS, 256)), full((4, D, 256)), full((ROWS, D)), full((8, D)), full((4, 16, D))]
+        [SMEM, full((ROWS, D)), full((ROWS, D)), full((8, D)), full((4, 16, D))]
         + [full((4, OUT, HL)), full((ROWS, OUT))]
         + [pl.BlockSpec((1, D // pieces, D), lambda j: (jnp.minimum(j, 3), 0, 0)) for _ in inner_w]
         + [pl.BlockSpec((1, D // pieces, D), lambda j: (jnp.where(j < 4, 0, j & 3), 1, 0)) for _ in outer_w],
-        [full((ROWS, D)), full((ROWS, 128)), full((ROWS, D)), full((OUT, ROWS)), full((4, OUT, HL)), full((8, D))]
+        [full((ROWS, D)), full((OUT, ROWS)), full((4, OUT, HL)), full((8, D))]
         + [wide, wide, pl.BlockSpec((1, ROWS, D), late), pl.BlockSpec((1, 8, D), late)],
         [
-            shape((ROWS, D), F32),
-            shape((ROWS, 128), F32),
             shape((ROWS, D), F32),
             shape((OUT, ROWS)),
             shape((4, OUT, HL)),
@@ -493,17 +515,15 @@
         ],
         [
             pltpu.VMEM((4, ROWS, D), BF),
-            pltpu.VMEM((4, ROWS, D), F32),
-            pltpu.VMEM((ROWS, D), F32),
-            pltpu.VMEM((ROWS, D), BF),
+            pltpu.VMEM((4, ROWS, D), BF),
             pltpu.VMEM((ROWS, D), BF),
             pltpu.VMEM((ROWS, D), F32),
             pltpu.VMEM((ROWS, D), F32),
             pltpu.VMEM((ROWS, 128), F32),
         ],
         micros=30,
-        limit=24,
-    )(scal, context, wo, packed, fvec, extra, final, cot, *inner_w, *outer_w)
+        limit=18,
+    )(scal, unit, low, fvec, extra, final, cot, *inner_w, *outer_w)
 
 
 def inner_back_body(pieces, pre_ref, grad_ref, unit_ref, scale_ref, fvec_ref, sums_ref, *refs):
@@ -573,7 +593,7 @@
     return jnp.concatenate([final, jnp.broadcast_to(wide[None], (PARTS, 16, 512))], axis=2)
 
 
-def attend_back_body(pieces, first, count, scal, kept_ref, xr_ref, kv_ref, q_ref, ctx_ref, ctx_f_ref, one_ref, low_ref, all_ref, fin_ref, hid_ref, *refs):
+def attend_back_body(pieces, first, count, scal, kept_ref, xr_ref, kv_ref, q_ref, ctx_ref, lse_ref, one_ref, low_ref, all_ref, fin_ref, hid_ref, *refs):
     weights = refs[:pieces]
     refs = refs[pieces + (2 if first else 0) :]
     keep_ref, send_ref = refs[:2]
@@ -593,7 +613,8 @@
     grad_ctx = jnp.where(lane >= HD, grad_ctx, 0.0).astype(BF)
     keys, values = kv_ref[0, :, :256], kv_ref[0, :, 128:]
     queries = q_ref[0]
-    products = grad_ctx.astype(F32) * ctx_f_ref[0]
+    products = grad_ctx.astype(F32) * ctx_ref[0].astype(F32)
+    totals = jnp.transpose(lse_ref[0])
     dq = jnp.zeros((ROWS, 256), F32)
     dk = jnp.zeros((KEYS, 256), F32)
     dv = jnp.zeros((KEYS, 256), F32)
@@ -603,7 +624,7 @@
         own_grad = jnp.where(lanes_of_head(h, HD), grad_ctx, zero)
         row_dot = jnp.sum(jnp.where(lanes_of_head(h, HD), products, 0.0), axis=1, keepdims=True)
         scores = dot_nt(own, keys) + bias_ref[...]
-        prob = jnp.exp(scores - ctx_f_ref[0, :, h : h + 1])
+        prob = jnp.exp(scores - totals[:, h : h + 1])
         dv = dv + dot_tn(prob.astype(BF), own_grad)
         grad_scores = (prob * (dot_nt(own_grad, values) - row_dot)).astype(BF)
         dq = jnp.where(lanes_of_head(h, 0), dot_nn(grad_scores, keys), dq)
@@ -644,7 +665,7 @@
             ref[:, ROWS:] = part[:, :ROWS]
 
 
-def attend_back(scal, kept, packed, kv, queries, context, context_f, one, low, small, weights, first, count, held):
+def attend_back(scal, kept, packed, kv, queries, context, log_total, one, low, small, weights, first, count, held):
     pieces = len(weights)
     half = PARTS // 2
     at = lambda j: (j + first, 0, 0)
@@ -661,7 +682,7 @@
             pl.BlockSpec((1, KEYS, 384), at),
             pl.BlockSpec((1, ROWS, 256), at),
             pl.BlockSpec((1, ROWS, 256), at),
-            pl.BlockSpec((1, ROWS, 256), at),
+            pl.BlockSpec((1, 8, ROWS), at),
             full(one.shape),
             full((ROWS, D)),
             full((8, D)),
@@ -675,9 +696,9 @@
         + ([shape((HL, KEYS), F32)] * 2 + [shape((HL, KEYS))] * 2 if last else [shape((KEYS, D), F32)]),
         [pltpu.VMEM((ROWS, KEYS), F32), pltpu.VMEM((KEYS, D), F32)],
         micros=9 * count,
-        limit=24,
+        limit=22,
         aliases={n_in + n: n for n in range(len(held))},
-    )(scal, kept, packed, kv, queries, context, context_f, one, low, *small, *weights, *held)
+    )(scal, kept, packed, kv, queries, context, log_total, one, low, *small, *weights, *held)
 
 
 def pack_vec_body(order_ref, mask_ref, vec_ref, out_ref, total_ref):
@@ -883,9 +904,7 @@
         head_x, head_y = over_plane(heads)
         head_x, head_y = sync(head_x, head_y)
         far_a, far_b = sync(*over_corner(head_x, head_y))
-        far_a, far_b, ffn_got, near, away, heads, head_x, head_y = sync(
-            far_a, far_b, ffn_got, near, away, heads, head_x, head_y
-        )
+        far_a, far_b, ffn_got, near, away, heads, head_x, head_y = sync(far_a, far_b, ffn_got, near, away, heads, head_x, head_y)
         x1, x2 = swap(near, "mp", 1), swap(away, "mp", 2)
         ffn = jnp.stack([ffn_own, *ffn_got])
         ffn = jnp.concatenate([ffn, extras], axis=1)
@@ -893,30 +912,35 @@
         far = jnp.concatenate([far_a, far_b], axis=0)
         head_pieces = [heads, head_x, head_y, far]
         head_pieces += [swap(p, "dp", 1) for p in head_pieces]
-        x1, x2, *head_pieces = sync(x1, x2, *head_pieces)
+        x1, x2 = sync(x1, x2)
         x3 = swap(x2, "mp", 1)
-        x3, ffn_x, ffn_y = sync(x3, ffn_x, ffn_y)
+        part, fvec, bias = prepare(by_xor, scal, kept, near, x2, x1, extras)
+        x3, ffn_x, ffn_y, part, *head_pieces = sync(x3, ffn_x, ffn_y, part, *head_pieces)
         far_a, far_b = over_corner(ffn_x, ffn_y)
         ffn_pieces = [swap(p, "dp", 1) for p in (ffn, ffn_x, ffn_y)]
     else:
         ffn = jnp.concatenate([jnp.stack([ffn_own, *ffn_got]), extras], axis=1)
         x1, x2 = swap(near, "mp", 1), swap(away, "mp", 2)
         x3 = swap(x2, "mp", 1)
+        part, fvec, bias = prepare(by_xor, scal, kept, near, x2, x1, extras)
         head_pieces, ffn_pieces, final = plain_pieces(heads, ffn)
 
-    packed, fvec, kv, queries, context, context_f, wo = attend(
-        scal, kept, (near, x2, x1, x3), extras, head_pieces
-    )
+    packed, kv, queries, context, log_total, wo = attend(scal, part, bias, x3, extras, head_pieces)
     if by_xor:
         context, far_a, far_b, *ffn_pieces = sync(context, far_a, far_b, *ffn_pieces)
         far = jnp.concatenate([far_a, far_b], axis=0)
         ffn_pieces = [ffn, ffn_x, ffn_y, far] + ffn_pieces + [swap(far, "dp", 1)]
+        unit, scale, normed_low = first_norm(context, wo, packed, fvec)
+        unit, last = sync(unit, ffn_pieces[-1])
+        ffn_pieces[-1] = last
         final = jnp.concatenate([p[:, 2 * FB :, :HL] for p in ffn_pieces], axis=1)
-    unit, scale, grad_two, vec, fin_grad, sums, ffn_keep, ffn_send, pre, hid_sums = hidden(
-        scal, context, wo, packed, fvec, extras, final, cot, ffn_pieces, ffn_pieces
+    if not by_xor:
+        unit, scale, normed_low = first_norm(context, wo, packed, fvec)
+    grad_two, vec, fin_grad, sums, ffn_keep, ffn_send, pre, hid_sums = hidden(
+        scal, unit, normed_low, fvec, extras, final, cot, ffn_pieces, ffn_pieces
     )
     vec_got = swap(vec, "mp", 1)
-    saved = (kept, packed, kv, queries, context, context_f)
+    saved = (kept, packed, kv, queries, context, log_total)
 
     def heads_back(one, low, first, count, held):
         small = (all_sums, fin_grad, hid_sums)
@@ -954,7 +978,6 @@
         lower_got = swap(lower, "mp", 1)
         x_got, y_got, dx1_got, far = sync(x_got, y_got, dx1_got, far)
         to_y, to_x, h_upper, h_lower = plane_second(*pair, x_got, y_got)
-        to_y, to_x, dx1_got = sync(to_y, to_x, dx1_got)
         from_y, from_x = swap(to_y, "dp", 4), swap(to_x, "dp", 2)
         inputs_grad = pack_x(order, dx0, dx1_got, far)
         from_y, from_x, lower_got, inputs_grad = sync(from_y, from_x, lower_got, inputs_grad)

time: 263 us -> 256 us (0.973)
  waiting for transfers between devices: 105 us -> 93.9 us
  starting transfers between devices: 39.1 us -> 42.4 us
    ppermute x44, waiting for transfers between devices: 105 us -> 93.9 us  [swap(): return lax.ppermute(array, axis, [(a, a ^ bit) for a in range(size)])]
    ppermute x44, starting transfers between devices: 39.1 us -> 42.4 us  [swap(): return lax.ppermute(array, axis, [(a, a ^ bit) for a in range(size)])]
    pallas_call x2 -> x4, Pallas kernels: 52.1 us -> 53.2 us  [the longest x1 29.1 us: hidden(): call(functools.partial(hidden_body, pieces), (12,), [SMEM, full((ROWS, D)...]
  transfers between devices with their start and end apart: 44 -> 44, of which waited for: 24 -> 20; matrix products, arithmetic and copies ran while one was open for 1% -> 1% of each run, Pallas kernels for 29% -> 31%
where the time goes in v2:
time: 256 us
  Pallas kernels  112 us (44%)
  waiting for transfers between devices  93.9 us (37%)
  starting transfers between devices  42.4 us (17%)
  other arithmetic  3.17 us (1%)
  local copies, waits for them, and re-layouts  3.03 us (1%)
    ppermute x44, waiting for transfers between devices, swap(): return lax.ppermute(array, axis, [(a, a ^ bit) for a in range(size)])  93.9 us
    ppermute x44, starting transfers between devices, swap(): return lax.ppermute(array, axis, [(a, a ^ bit) for a in range(size)])  42.4 us
    pallas_call x1, Pallas kernels, attend_back(): call(functools.partial(attend_back_body, pieces, first, count), (count,),...  34.5 us
    pallas_call x1, Pallas kernels, hidden(): call(functools.partial(hidden_body, pieces), (12,), [SMEM, full((ROWS, D)...  29.1 us
    pallas_call x1, Pallas kernels, attend(): call(functools.partial(attend_body, pieces), (4,), [SMEM, full((KEYS, D))...  19.6 us
    pallas_call x1, Pallas kernels, pack_x(): call(pack_x_body, (4,), [pl.BlockSpec((8, ROWS), lambda b: (0, b))] + [pl...  5.5 us
    pallas_call x1, Pallas kernels, inner_back(): call(functools.partial(inner_back_body, pieces), (4,), [pl.BlockSpec((1,...  5.3 us
    pallas_call x1, Pallas kernels, pack_vec(): call(pack_vec_body, (4,), [pl.BlockSpec((8, ROWS), lambda b: (0, b)), ful...  5.14 us
  transfers between devices with their start and end apart: 44, of which 20 were waited for; matrix products, arithmetic and copies ran while one was open for 1% of the time, Pallas kernels for 31%

profile of v2, /device:TPU:0, one launch (start us, length us, event | category | flops | bytes accessed | tf_op | source)
XLA Modules:
  0.0 256.1 jit_solution(10137483010980752188)
XLA Ops:
  2.8 5.0 %collective-permute-start.2 = (bf16[112,768]{1,0:T(8,128)(2,1)}, bf16[112,768]{1,0:T(8,128)(2,1)S(1)}, u32[]{:S(2)}, u32[]{:S(2)}) collective-permute-start(bf16[112,768]{1,0:T(8,128)(2,1)} %get-tuple-element.151), channel_id=1, source_target_pairs={{0,3},{1,2},{2,1},{3,0},{4,7},{5,6},{6,5},{7,4},{8,11},{9,10},{10,... | collective-permute-start | bytes 516104 | tf_op jit(solution)/shard_map/ppermute | solution.py:41
  8.6 4.6 %shard_map.341 = (bf16[192,2048]{1,0:T(8,128)(2,1)S(1)}, f32[8,1024]{1,0:T(8,128)S(1)}, f32[512,128]{1,0:T(8,128)S(1)}, s32[8,2048]{1,0:T(8,128)S(1)}) custom-call(s32[6]{0:T(128)S(1)} %pad_add_fusion.scal, s32[1,2048]{1,0:T(1,128)S(1)} %copy-done.22, bf16[192,2048]{1,0:T(8,128)(2,1)S(1)} %copy-done.12, s32[1,2048]{1,0:T(1,128)S(1)} %bitcast.118, ...), custom_call_target="tpu_custom_call" | custom-call | flops 24000000000 | bytes 72000000 | tf_op jit(solution)/shard_map/pallas_call | solution.py:193
  14.1 3.1 %collective-permute-done.1 = bf16[112,768]{1,0:T(8,128)(2,1)S(1)} collective-permute-done((bf16[112,768]{1,0:T(8,128)(2,1)}, bf16[112,768]{1,0:T(8,128)(2,1)S(1)}, u32[]{:S(2)}, u32[]{:S(2)}) %collective-permute-start.1) | collective-permute-done | bytes 172064 | tf_op jit(solution)/shard_map/ppermute | solution.py:41
  17.2 5.4 %collective-permute-done = bf16[112,768]{1,0:T(8,128)(2,1)S(1)} collective-permute-done((bf16[112,768]{1,0:T(8,128)(2,1)}, bf16[112,768]{1,0:T(8,128)(2,1)S(1)}, u32[]{:S(2)}, u32[]{:S(2)}) %collective-permute-start) | collective-permute-done | bytes 172064 | tf_op jit(solution)/shard_map/ppermute | solution.py:41
  25.8 2.5 collective-permute-start.9
  30.2 7.0 %collective-permute-done.4.refs_2_ = bf16[4,96,768]{2,1,0:T(8,128)(2,1)S(1)} collective-permute-done((bf16[4,96,768]{2,1,0:T(8,128)(2,1)S(1)}, bf16[4,96,768]{2,1,0:T(8,128)(2,1)S(1)}, u32[]{:S(2)}, u32[]{:S(2)}) %collective-permute-start.4) | collective-permute-done | bytes 589856 | tf_op jit(solution)/shard_map/ppermute | solution.py:41
  40.6 4.9 %collective-permute-done.6 = bf16[2,96,768]{2,1,0:T(8,128)(2,1)S(1)} collective-permute-done((bf16[2,96,768]{2,1,0:T(8,128)(2,1)S(1)}, bf16[2,96,768]{2,1,0:T(8,128)(2,1)S(1)}, u32[]{:S(2)}, u32[]{:S(2)}) %collective-permute-start.6) | collective-permute-done | bytes 294944 | tf_op jit(solution)/shard_map/ppermute | solution.py:41
  45.8 5.4 %collective-permute-done.7 = bf16[192,768]{1,0:T(8,128)(2,1)S(1)} collective-permute-done((bf16[192,768]{1,0:T(8,128)(2,1)S(1)}, bf16[192,768]{1,0:T(8,128)(2,1)S(1)}, u32[]{:S(2)}, u32[]{:S(2)}) %collective-permute-start.7) | collective-permute-done | bytes 294944 | tf_op jit(solution)/shard_map/ppermute | solution.py:41
  52.5 2.4 collective-permute-start.10
  54.9 13.9 %collective-permute-done.11.x2 = bf16[192,1024]{1,0:T(8,128)(2,1)S(1)} collective-permute-done((bf16[192,1024]{1,0:T(8,128)(2,1)S(1)}, bf16[192,1024]{1,0:T(8,128)(2,1)S(1)}, u32[]{:S(2)}, u32[]{:S(2)}) %collective-permute-start.11) | collective-permute-done | bytes 393248 | tf_op jit(solution)/shard_map/ppermute | solution.py:41
  68.9 4.1 %collective-permute-done.10.x1 = bf16[192,1024]{1,0:T(8,128)(2,1)S(1)} collective-permute-done((bf16[192,1024]{1,0:T(8,128)(2,1)S(1)}, bf16[192,1024]{1,0:T(8,128)(2,1)S(1)}, u32[]{:S(2)}, u32[]{:S(2)}) %collective-permute-start.10) | collective-permute-done | bytes 393248 | tf_op jit(solution)/shard_map/ppermute | solution.py:41
  73.5 2.5 shard_map.342
  76.2 8.4 %collective-permute-done.12.x3 = bf16[192,1024]{1,0:T(8,128)(2,1)S(1)} collective-permute-done((bf16[192,1024]{1,0:T(8,128)(2,1)S(1)}, bf16[192,1024]{1,0:T(8,128)(2,1)S(1)}, u32[]{:S(2)}, u32[]{:S(2)}) %collective-permute-start.12) | collective-permute-done | bytes 393248 | tf_op jit(solution)/shard_map/ppermute | solution.py:41
  88.4 19.6 %shard_map.343 = (bf16[1024,768]{1,0:T(8,128)(2,1)S(1)}, bf16[4,1024,384]{2,1,0:T(8,128)(2,1)S(1)}, bf16[4,512,256]{2,1,0:T(8,128)(2,1)S(1)}, bf16[4,512,256]{2,...) custom-call(s32[6]{0:T(128)S(1)} %pad_add_fusion.scal, ...), custom_call_target="tpu_custom_call" | custom-call | flops 92000002048 | bytes 276000000 | tf_op jit(solution)/shard_map/pallas_call | solution.py:312
  111.5 29.1 %shard_map.345 = (f32[512,768]{1,0:T(8,128)S(1)}, bf16[128,512]{1,0:T(8,128)(2,1)S(1)}, bf16[4,128,192]{2,1,0:T(8,128)(2,1)S(1)}, f32[8,768]{1,0:T(8,128)S(1)}, ...) custom-call(s32[6]{0:T(128)S(1)} %pad_add_fusion.scal, ...), custom_call_target="tpu_custom_call" | custom-call | flops 120000004096 | bytes 360000000 | tf_op jit(solution)/shard_map/pallas_call | solution.py:497
  141.1 5.3 %shard_map.346 = (f32[512,768]{1,0:T(8,128)S(1)}, bf16[512,768]{1,0:T(8,128)(2,1)S(1)}, f32[8,768]{1,0:T(8,128)S(1)}) custom-call(bf16[4,512,768]{2,1,0:T(8,128)(2,1)S(1)} %get-tuple-element.213.pre_ref, f32[512,768]{1,0:T(8,128)S(1)} %get-tuple-element.214.grad_ref, f32[512,768]{1,0:T(8,128)S(1)} %get-tuple-element.203.unit_ref, ...), custom_call_target="tpu_custom_call" | custom-call | flops 35999997952 | bytes 108000000 | tf_op jit(solution)/shard_map/pallas_call | solution.py:563
  151.8 34.5 %shard_map.347 = (bf16[4,4,112,768]{3,2,1,0:T(8,128)(2,1)S(1)}, bf16[4,4,112,768]{3,2,1,0:T(8,128)(2,1)S(1)}, f32[192,1024]{1,0:T(8,128)S(1)}, f32[192,1024]{1,0...) custom-call(s32[6]{0:T(128)S(1)} %pad_add_fusion.scal, f32[8,1024]{1,0:T(8,128)S(1)} %copy-done.11, ...), custom_call_target="tpu_custom_call" | custom-call | flops 143999991808 | bytes 432000000 | tf_op jit(solution)/shard_map/pallas_call | solution.py:675
  191.8 6.2 %collective-permute-done.32 = bf16[192,1024]{1,0:T(8,128)(2,1)S(1)} collective-permute-done((bf16[192,1024]{1,0:T(8,128)(2,1)S(1)}, bf16[192,1024]{1,0:T(8,128)(2,1)S(1)}, u32[]{:S(2)}, u32[]{:S(2)}) %collective-permute-start.32) | collective-permute-done | bytes 393248 | tf_op jit(solution)/shard_map/ppermute | solution.py:41
  202.3 2.6 %collective-permute-done.31 = bf16[2,192,768]{2,1,0:T(8,128)(2,1)S(1)} collective-permute-done((bf16[2,192,768]{2,1,0:T(8,128)(2,1)S(1)}, bf16[2,192,768]{2,1,0:T(8,128)(2,1)S(1)}, u32[]{:S(2)}, u32[]{:S(2)}) %collective-permute-start.31) | collective-permute-done | bytes 589856 | tf_op jit(solution)/shard_map/ppermute | solution.py:41
  206.4 5.1 %shard_map.348 = f32[2048,128]{1,0:T(8,128)} custom-call(s32[8,2048]{1,0:T(8,128)S(1)} %get-tuple-element.236.order_ref, s32[1,2048]{1,0:T(1,128)S(1)} %bitcast.119, bf16[4,128,512]{2,1,0:T(8,128)(2,1)S(1)} %pad_maximum_fusion.1.vec_ref), custom_call_target="tpu_custom_call" | custom-call | flops 20000000000 | bytes 60000000 | tf_op jit(solution)/shard_map/pallas_call | solution.py:722
  211.9 5.6 %collective-permute-done.36.x1_ref = bf16[192,1024]{1,0:T(8,128)(2,1)S(1)} collective-permute-done((bf16[192,1024]{1,0:T(8,128)(2,1)S(1)}, bf16[192,1024]{1,0:T(8,128)(2,1)S(1)}, u32[]{:S(2)}, u32[]{:S(2)}) %collective-permute-start.36) | collective-permute-done | bytes 393248 | tf_op jit(solution)/shard_map/ppermute | solution.py:41
  224.1 5.5 %shard_map.349 = f32[192,2048]{1,0:T(8,128)} custom-call(s32[8,2048]{1,0:T(8,128)S(1)} %get-tuple-element.236.order_ref, f32[192,1024]{1,0:T(8,128)S(1)} %get-tuple-element.254.x0_ref, bf16[192,1024]{1,0:T(8,128)(2,1)S(1)} %collective-permute-done.36.x1_ref, bf16[192,1024]{1,0:T(8,128)(2,1)S(1)} %collective-permute-done.37.far_ref), custom_call_target="tpu_custom_call" | custom-call | flops 20000000000 | bytes 60000000 | tf_op jit(solution)/shard_map/pallas_call | solution.py:752
  233.1 13.9 %collective-permute-done.42.b_ref = bf16[192,768]{1,0:T(8,128)(2,1)S(1)} collective-permute-done((bf16[192,768]{1,0:T(8,128)(2,1)S(1)}, bf16[192,768]{1,0:T(8,128)(2,1)S(1)}, u32[]{:S(2)}, u32[]{:S(2)}) %collective-permute-start.42) | collective-permute-done | bytes 294944 | tf_op jit(solution)/shard_map/ppermute | solution.py:41
  248.9 6.1 %collective-permute-done.43.b_ref = bf16[112,768]{1,0:T(8,128)(2,1)S(1)} collective-permute-done((bf16[112,768]{1,0:T(8,128)(2,1)S(1)}, bf16[112,768]{1,0:T(8,128)(2,1)S(1)}, u32[]{:S(2)}, u32[]{:S(2)}) %collective-permute-start.43) | collective-permute-done | bytes 172064 | tf_op jit(solution)/shard_map/ppermute | solution.py:41
  (186 shorter events, 51.9 us)
Async XLA Ops:
  25.8 20.0 %collective-permute-start.9 = (bf16[192,768]{1,0:T(8,128)(2,1)S(1)}, bf16[192,768]{1,0:T(8,128)(2,1)S(1)}, u32[]{:S(2)}, u32[]{:S(2)}) collective-permute-start(bf16[192,768]{1,0:T(8,128)(2,1)S(1)} %copy-done.30), channel_id=1, source_target_pairs={{0,3},{1,2},{2,1},{3,0},{4,7},{5,6},{6,5},{7,4},{8,11},{9,10},{10,... | collective-permute-start | bytes 884744 | tf_op jit(solution)/shard_map/ppermute | solution.py:41
  28.3 17.5 %collective-permute-start.8 = (bf16[192,768]{1,0:T(8,128)(2,1)S(1)}, bf16[192,768]{1,0:T(8,128)(2,1)S(1)}, u32[]{:S(2)}, u32[]{:S(2)}) collective-permute-start(bf16[192,768]{1,0:T(8,128)(2,1)S(1)} %copy-done.30), channel_id=1, source_target_pairs={{0,1},{1,0},{2,3},{3,2},{4,5},{5,4},{6,7},{7,6},{8,9},{9,8},{10,11... | collective-permute-start | bytes 884744 | tf_op jit(solution)/shard_map/ppermute | solution.py:41
  28.3 22.9 %collective-permute-start.7 = (bf16[192,768]{1,0:T(8,128)(2,1)S(1)}, bf16[192,768]{1,0:T(8,128)(2,1)S(1)}, u32[]{:S(2)}, u32[]{:S(2)}) collective-permute-start(bf16[192,768]{1,0:T(8,128)(2,1)S(1)} %copy-done.30), channel_id=1, source_target_pairs={{0,2},{1,3},{2,0},{3,1},{4,6},{5,7},{6,4},{7,5},{8,10},{9,11},{10,... | collective-permute-start | bytes 884744 | tf_op jit(solution)/shard_map/ppermute | solution.py:41
  51.3 33.3 %collective-permute-start.14 = (bf16[4,208,768]{2,1,0:T(8,128)(2,1)S(1)}, bf16[4,208,768]{2,1,0:T(8,128)(2,1)S(1)}, u32[]{:S(2)}, u32[]{:S(2)}) collective-permute-start(bf16[4,208,768]{2,1,0:T(8,128)(2,1)S(1)} %maximum_maximum_fusion.refs_0_.refs_8_), channel_id=1, source_target_pairs={{0,16},{4,20},{8,24},{12,28},{16,0},{20,4},{24,8},{28,12},{1,17},{... | collective-permute-start | bytes 3833864 | tf_op jit(solution)/shard_map/ppermute | solution.py:41
  51.8 32.8 %collective-permute-start.13 = (bf16[4,208,768]{2,1,0:T(8,128)(2,1)S(1)}, bf16[4,208,768]{2,1,0:T(8,128)(2,1)S(1)}, u32[]{:S(2)}, u32[]{:S(2)}) collective-permute-start(bf16[4,208,768]{2,1,0:T(8,128)(2,1)S(1)} %maximum_maximum_fusion.refs_0_.refs_8_), channel_id=1, source_target_pairs={{0,8},{4,12},{8,0},{12,4},{16,24},{20,28},{24,16},{28,20},{1,9},{5... | collective-permute-start | bytes 3833864 | tf_op jit(solution)/shard_map/ppermute | solution.py:41
  52.4 16.5 %collective-permute-start.11 = (bf16[192,1024]{1,0:T(8,128)(2,1)S(1)}, bf16[192,1024]{1,0:T(8,128)(2,1)S(1)}, u32[]{:S(2)}, u32[]{:S(2)}) collective-permute-start(bf16[192,1024]{1,0:T(8,128)(2,1)S(1)} %get-tuple-element.169), channel_id=1, source_target_pairs={{0,2},{1,3},{2,0},{3,1},{4,6},{5,7},{6,4},{7,5},{8,10},{9,11},{10,... | collective-permute-start | bytes 1179656 | tf_op jit(solution)/shard_map/ppermute | solution.py:41
  52.4 20.5 %collective-permute-start.18 = (bf16[4,96,768]{2,1,0:T(8,128)(2,1)S(1)}, bf16[4,96,768]{2,1,0:T(8,128)(2,1)S(1)}, u32[]{:S(2)}, u32[]{:S(2)}) collective-permute-start(bf16[4,96,768]{2,1,0:T(8,128)(2,1)S(1)} %constant_dynamic-update-slice_fusion.refs_3_), channel_id=1, source_target_pairs={{0,4},{4,0},{8,12},{12,8},{16,20},{20,16},{24,28},{28,24},{1,5},{5... | collective-permute-start | bytes 1769480 | tf_op jit(solution)/shard_map/ppermute | solution.py:41
  52.5 20.4 %collective-permute-start.10 = (bf16[192,1024]{1,0:T(8,128)(2,1)S(1)}, bf16[192,1024]{1,0:T(8,128)(2,1)S(1)}, u32[]{:S(2)}, u32[]{:S(2)}) collective-permute-start(bf16[192,1024]{1,0:T(8,128)(2,1)S(1)} %get-tuple-element.168.x0), channel_id=1, source_target_pairs={{0,1},{1,0},{2,3},{3,2},{4,5},{5,4},{6,7},{7,6},{8,9},{9,8},{10,11... | collective-permute-start | bytes 1179656 | tf_op jit(solution)/shard_map/ppermute | solution.py:41
  76.0 32.0 %collective-permute-start.21 = (bf16[4,208,768]{2,1,0:T(8,128)(2,1)S(1)}, bf16[4,208,768]{2,1,0:T(8,128)(2,1)S(1)}, u32[]{:S(2)}, u32[]{:S(2)}) collective-permute-start(bf16[4,208,768]{2,1,0:T(8,128)(2,1)S(1)} %maximum_maximum_fusion.refs_0_.refs_8_), channel_id=1, source_target_pairs={{0,4},{4,0},{8,12},{12,8},{16,20},{20,16},{24,28},{28,24},{1,5},{5... | collective-permute-start | bytes 3833864 | tf_op jit(solution)/shard_map/ppermute | solution.py:41
  84.6 23.4 %collective-permute-start.23 = (bf16[4,208,768]{2,1,0:T(8,128)(2,1)S(1)}, bf16[4,208,768]{2,1,0:T(8,128)(2,1)S(1)}, u32[]{:S(2)}, u32[]{:S(2)}) collective-permute-start(bf16[4,208,768]{2,1,0:T(8,128)(2,1)S(1)} %collective-permute-done.14.refs_2_.refs_10_), channel_id=1, source_target_pairs={{0,4},{4,0},{8,12},{12,8},{16,20},{20,16},{24,28},{28,24},{1,5},{5... | collective-permute-start | bytes 3833864 | tf_op jit(solution)/shard_map/ppermute | solution.py:41
  84.8 23.3 %collective-permute-start.22 = (bf16[4,208,768]{2,1,0:T(8,128)(2,1)S(1)}, bf16[4,208,768]{2,1,0:T(8,128)(2,1)S(1)}, u32[]{:S(2)}, u32[]{:S(2)}) collective-permute-start(bf16[4,208,768]{2,1,0:T(8,128)(2,1)S(1)} %collective-permute-done.13.refs_1_.refs_9_), channel_id=1, source_target_pairs={{0,4},{4,0},{8,12},{12,8},{16,20},{20,16},{24,28},{28,24},{1,5},{5... | collective-permute-start | bytes 3833864 | tf_op jit(solution)/shard_map/ppermute | solution.py:41
  85.3 22.7 %collective-permute-start.20 = (bf16[2,208,768]{2,1,0:T(8,128)(2,1)S(1)}, bf16[2,208,768]{2,1,0:T(8,128)(2,1)S(1)}, u32[]{:S(2)}, u32[]{:S(2)}) collective-permute-start(bf16[2,208,768]{2,1,0:T(8,128)(2,1)S(1)} %slice.189), channel_id=1, source_target_pairs={{0,16},{4,20},{8,24},{12,28},{16,0},{20,4},{24,8},{28,12},{1,17},{... | collective-permute-start | bytes 1916936 | tf_op jit(solution)/shard_map/ppermute | solution.py:41
  86.8 21.2 %collective-permute-start.19 = (bf16[2,208,768]{2,1,0:T(8,128)(2,1)S(1)}, bf16[2,208,768]{2,1,0:T(8,128)(2,1)S(1)}, u32[]{:S(2)}, u32[]{:S(2)}) collective-permute-start(bf16[2,208,768]{2,1,0:T(8,128)(2,1)S(1)} %slice.188), channel_id=1, source_target_pairs={{0,8},{4,12},{8,0},{12,4},{16,24},{20,28},{24,16},{28,20},{1,9},{5... | collective-permute-start | bytes 1916936 | tf_op jit(solution)/shard_map/ppermute | solution.py:41
  149.4 36.9 %collective-permute-start.29 = (bf16[2,128,512]{2,1,0:T(8,128)(2,1)S(1)}, bf16[2,128,512]{2,1,0:T(8,128)(2,1)S(1)}, u32[]{:S(2)}, u32[]{:S(2)}) collective-permute-start(bf16[2,128,512]{2,1,0:T(8,128)(2,1)S(1)} %pad_maximum_fusion.2), channel_id=1, source_target_pairs={{0,2},{1,3},{2,0},{3,1},{4,6},{5,7},{6,4},{7,5},{8,10},{9,11},{10,... | collective-permute-start | bytes 786440 | tf_op jit(solution)/shard_map/ppermute | solution.py:41
  150.4 36.0 %collective-permute-start.27 = (bf16[2,2,192,768]{3,2,1,0:T(8,128)(2,1)S(1)}, bf16[2,2,192,768]{3,2,1,0:T(8,128)(2,1)S(1)}, u32[]{:S(2)}, u32[]{:S(2)}) collective-permute-start(bf16[2,2,192,768]{3,2,1,0:T(8,128)(2,1)S(1)} %fusion), channel_id=1, source_target_pairs={{0,8},{4,12},{8,0},{12,4},{16,24},{20,28},{24,16},{28,20},{1,9},{5... | collective-permute-start | bytes 3538952 | tf_op jit(solution)/shard_map/ppermute | solution.py:41
  150.9 35.4 %collective-permute-start.28 = (bf16[2,2,192,768]{3,2,1,0:T(8,128)(2,1)S(1)}, bf16[2,2,192,768]{3,2,1,0:T(8,128)(2,1)S(1)}, u32[]{:S(2)}, u32[]{:S(2)}) collective-permute-start(bf16[2,2,192,768]{3,2,1,0:T(8,128)(2,1)S(1)} %fusion.1), channel_id=1, source_target_pairs={{0,16},{4,20},{8,24},{12,28},{16,0},{20,4},{24,8},{28,12},{1,17},{... | collective-permute-start | bytes 3538952 | tf_op jit(solution)/shard_map/ppermute | solution.py:41
  188.7 16.2 %collective-permute-start.31 = (bf16[2,192,768]{2,1,0:T(8,128)(2,1)S(1)}, bf16[2,192,768]{2,1,0:T(8,128)(2,1)S(1)}, u32[]{:S(2)}, u32[]{:S(2)}) collective-permute-start(bf16[2,192,768]{2,1,0:T(8,128)(2,1)S(1)} %get-tuple-element.280), channel_id=1, source_target_pairs={{0,8},{4,12},{8,0},{12,4},{16,24},{20,28},{24,16},{28,20},{1,9},{5... | collective-permute-start | bytes 1769480 | tf_op jit(solution)/shard_map/ppermute | solution.py:41
  190.2 21.3 %collective-permute-start.30 = (bf16[2,192,768]{2,1,0:T(8,128)(2,1)S(1)}, bf16[2,192,768]{2,1,0:T(8,128)(2,1)S(1)}, u32[]{:S(2)}, u32[]{:S(2)}) collective-permute-start(bf16[2,192,768]{2,1,0:T(8,128)(2,1)S(1)} %get-tuple-element.281), channel_id=1, source_target_pairs={{0,16},{4,20},{8,24},{12,28},{16,0},{20,4},{24,8},{28,12},{1,17},{... | collective-permute-start | bytes 1769480 | tf_op jit(solution)/shard_map/ppermute | solution.py:41
  198.0 19.6 %collective-permute-start.36 = (bf16[192,1024]{1,0:T(8,128)(2,1)S(1)}, bf16[192,1024]{1,0:T(8,128)(2,1)S(1)}, u32[]{:S(2)}, u32[]{:S(2)}) collective-permute-start(bf16[192,1024]{1,0:T(8,128)(2,1)S(1)} %get-tuple-element.248), channel_id=1, source_target_pairs={{0,1},{1,0},{2,3},{3,2},{4,5},{5,4},{6,7},{7,6},{8,9},{9,8},{10,11... | collective-permute-start | bytes 1179656 | tf_op jit(solution)/shard_map/ppermute | solution.py:41
  199.7 19.5 %collective-permute-start.37 = (bf16[192,1024]{1,0:T(8,128)(2,1)S(1)}, bf16[192,1024]{1,0:T(8,128)(2,1)S(1)}, u32[]{:S(2)}, u32[]{:S(2)}) collective-permute-start(bf16[192,1024]{1,0:T(8,128)(2,1)S(1)} %add_convert_fusion.4), channel_id=1, source_target_pairs={{0,2},{1,3},{2,0},{3,1},{4,6},{5,7},{6,4},{7,5},{8,10},{9,11},{10,... | collective-permute-start | bytes 1179656 | tf_op jit(solution)/shard_map/ppermute | solution.py:41
  201.1 18.2 %collective-permute-start.34 = (bf16[2,2,112,768]{3,2,1,0:T(8,128)(2,1)S(1)}, bf16[2,2,112,768]{3,2,1,0:T(8,128)(2,1)S(1)}, u32[]{:S(2)}, u32[]{:S(2)}) collective-permute-start(bf16[2,2,112,768]{3,2,1,0:T(8,128)(2,1)S(1)} %fusion.8), channel_id=1, source_target_pairs={{0,8},{4,12},{8,0},{12,4},{16,24},{20,28},{24,16},{28,20},{1,9},{5... | collective-permute-start | bytes 2064392 | tf_op jit(solution)/shard_map/ppermute | solution.py:41
  204.9 15.9 %collective-permute-start.35 = (bf16[2,2,112,768]{3,2,1,0:T(8,128)(2,1)S(1)}, bf16[2,2,112,768]{3,2,1,0:T(8,128)(2,1)S(1)}, u32[]{:S(2)}, u32[]{:S(2)}) collective-permute-start(bf16[2,2,112,768]{3,2,1,0:T(8,128)(2,1)S(1)} %fusion.9), channel_id=1, source_target_pairs={{0,16},{4,20},{8,24},{12,28},{16,0},{20,4},{24,8},{28,12},{1,17},{... | collective-permute-start | bytes 2064392 | tf_op jit(solution)/shard_map/ppermute | solution.py:41
  211.9 17.8 %collective-permute-start.40 = (bf16[2,192,768]{2,1,0:T(8,128)(2,1)S(1)}, bf16[2,192,768]{2,1,0:T(8,128)(2,1)S(1)}, u32[]{:S(2)}, u32[]{:S(2)}) collective-permute-start(bf16[2,192,768]{2,1,0:T(8,128)(2,1)S(1)} %fusion.5), channel_id=1, source_target_pairs={{0,1},{1,0},{2,3},{3,2},{4,5},{5,4},{6,7},{7,6},{8,9},{9,8},{10,11... | collective-permute-start | bytes 1769480 | tf_op jit(solution)/shard_map/ppermute | solution.py:41
  230.1 16.8 %collective-permute-start.41 = (bf16[2,112,768]{2,1,0:T(8,128)(2,1)S(1)}, bf16[2,112,768]{2,1,0:T(8,128)(2,1)S(1)}, u32[]{:S(2)}, u32[]{:S(2)}) collective-permute-start(bf16[2,112,768]{2,1,0:T(8,128)(2,1)S(1)} %fusion.11), channel_id=1, source_target_pairs={{0,1},{1,0},{2,3},{3,2},{4,5},{5,4},{6,7},{7,6},{8,9},{9,8},{10,11... | collective-permute-start | bytes 1032200 | tf_op jit(solution)/shard_map/ppermute | solution.py:41
  (53 other events, 602.5 us)

commit v3 on v2

--- a/solution.py
+++ b/solution.py
@@ -335,11 +335,11 @@
     )(scal, part, bias, x3, extra, *weights)
 
 
-def over_rows(body, carried=()):
+def over_rows(body, carried=(), chunk=CHUNK):
     def step(r, carried):
-        return body(pl.ds(pl.multiple_of(r * CHUNK, CHUNK), CHUNK), carried)
-
-    return lax.fori_loop(0, ROWS // CHUNK, step, carried)
+        return body(pl.ds(pl.multiple_of(r * chunk, chunk), chunk), carried)
+
+    return lax.fori_loop(0, ROWS // chunk, step, carried)
 
 
 def norm(residual, gain, shift):
@@ -387,11 +387,11 @@
     def rows_of(rows, carried):
         normed, unit, scale = norm(unit_ref[rows, :], fvec_ref[2:3], fvec_ref[3:4])
         unit_ref[rows, :] = unit
-        scale_ref[rows, :] = jnp.broadcast_to(scale, (CHUNK, 128))
+        scale_ref[rows, :] = jnp.broadcast_to(scale, (128, 128))
         low_ref[rows, :] = normed.astype(BF)
         return carried
 
-    over_rows(rows_of)
+    over_rows(rows_of, (), 128)
 
 
 def first_norm(context, wo, packed, fvec):
@@ -551,7 +551,7 @@
             return tuple(c + jnp.sum(t, axis=0, keepdims=True) for c, t in zip(carried, sums))
 
         all_ref[0:3] = sums_ref[0:3]
-        sums = over_rows(rows_back, (jnp.zeros((1, D), F32),) * 3)
+        sums = over_rows(rows_back, (jnp.zeros((1, D), F32),) * 3, 128)
         for n in range(3):
             all_ref[3 + n : 4 + n] = sums[n]
         all_ref[6:] = jnp.zeros((2, D), F32)
@@ -903,8 +903,8 @@
         heads, near, away = sync(heads, near, away)
         head_x, head_y = over_plane(heads)
         head_x, head_y = sync(head_x, head_y)
-        far_a, far_b = sync(*over_corner(head_x, head_y))
-        far_a, far_b, ffn_got, near, away, heads, head_x, head_y = sync(far_a, far_b, ffn_got, near, away, heads, head_x, head_y)
+        far_a, far_b, near, away = sync(*over_corner(head_x, head_y), near, away)
+        far_a, far_b, ffn_got, heads, head_x, head_y = sync(far_a, far_b, ffn_got, heads, head_x, head_y)
         x1, x2 = swap(near, "mp", 1), swap(away, "mp", 2)
         ffn = jnp.stack([ffn_own, *ffn_got])
         ffn = jnp.concatenate([ffn, extras], axis=1)

time: 256 us -> 256 us (level)
  transfers between devices with their start and end apart: 44 -> 44, of which waited for: 20 -> 21; matrix products, arithmetic and copies ran while one was open for 1% -> 1% of each run, Pallas kernels for 31% -> 31%
where the time goes in v3:
time: 256 us
  Pallas kernels  111 us (43%)
  waiting for transfers between devices  94.3 us (37%)
  starting transfers between devices  42.4 us (17%)
  other arithmetic  3.17 us (1%)
  local copies, waits for them, and re-layouts  3.02 us (1%)
    ppermute x44, waiting for transfers between devices, swap(): return lax.ppermute(array, axis, [(a, a ^ bit) for a in range(size)])  94.3 us
    ppermute x44, starting transfers between devices, swap(): return lax.ppermute(array, axis, [(a, a ^ bit) for a in range(size)])  42.4 us
    pallas_call x1, Pallas kernels, attend_back(): call(functools.partial(attend_back_body, pieces, first, count), (count,),...  34.5 us
    pallas_call x1, Pallas kernels, hidden(): call(functools.partial(hidden_body, pieces), (12,), [SMEM, full((ROWS, D)...  29.1 us
    pallas_call x1, Pallas kernels, attend(): call(functools.partial(attend_body, pieces), (4,), [SMEM, full((KEYS, D))...  19.6 us
    pallas_call x1, Pallas kernels, pack_x(): call(pack_x_body, (4,), [pl.BlockSpec((8, ROWS), lambda b: (0, b))] + [pl...  5.5 us
    pallas_call x1, Pallas kernels, pack_vec(): call(pack_vec_body, (4,), [pl.BlockSpec((8, ROWS), lambda b: (0, b)), ful...  5.14 us
  transfers between devices with their start and end apart: 44, of which 21 were waited for; matrix products, arithmetic and copies ran while one was open for 1% of the time, Pallas kernels for 31%

profile of v3, /device:TPU:0, one launch (start us, length us, event | category | flops | bytes accessed | tf_op | source)
XLA Modules:
  0.0 255.8 jit_solution(17816456365850667410)
XLA Ops:
  2.8 5.0 %collective-permute-start.2 = (bf16[112,768]{1,0:T(8,128)(2,1)}, bf16[112,768]{1,0:T(8,128)(2,1)S(1)}, u32[]{:S(2)}, u32[]{:S(2)}) collective-permute-start(bf16[112,768]{1,0:T(8,128)(2,1)} %get-tuple-element.151), channel_id=1, source_target_pairs={{0,3},{1,2},{2,1},{3,0},{4,7},{5,6},{6,5},{7,4},{8,11},{9,10},{10,... | collective-permute-start | bytes 516104 | tf_op jit(solution)/shard_map/ppermute | solution.py:41
  8.6 4.6 %shard_map.341 = (bf16[192,2048]{1,0:T(8,128)(2,1)S(1)}, f32[8,1024]{1,0:T(8,128)S(1)}, f32[512,128]{1,0:T(8,128)S(1)}, s32[8,2048]{1,0:T(8,128)S(1)}) custom-call(s32[6]{0:T(128)S(1)} %pad_add_fusion.scal, s32[1,2048]{1,0:T(1,128)S(1)} %copy-done.22, bf16[192,2048]{1,0:T(8,128)(2,1)S(1)} %copy-done.12, s32[1,2048]{1,0:T(1,128)S(1)} %bitcast.118, ...), custom_call_target="tpu_custom_call" | custom-call | flops 24000000000 | bytes 72000000 | tf_op jit(solution)/shard_map/pallas_call | solution.py:193
  14.1 3.1 %collective-permute-done.1 = bf16[112,768]{1,0:T(8,128)(2,1)S(1)} collective-permute-done((bf16[112,768]{1,0:T(8,128)(2,1)}, bf16[112,768]{1,0:T(8,128)(2,1)S(1)}, u32[]{:S(2)}, u32[]{:S(2)}) %collective-permute-start.1) | collective-permute-done | bytes 172064 | tf_op jit(solution)/shard_map/ppermute | solution.py:41
  17.2 5.4 %collective-permute-done = bf16[112,768]{1,0:T(8,128)(2,1)S(1)} collective-permute-done((bf16[112,768]{1,0:T(8,128)(2,1)}, bf16[112,768]{1,0:T(8,128)(2,1)S(1)}, u32[]{:S(2)}, u32[]{:S(2)}) %collective-permute-start) | collective-permute-done | bytes 172064 | tf_op jit(solution)/shard_map/ppermute | solution.py:41
  25.8 2.5 collective-permute-start.12
  30.2 7.0 %collective-permute-done.4.refs_2_ = bf16[4,96,768]{2,1,0:T(8,128)(2,1)S(1)} collective-permute-done((bf16[4,96,768]{2,1,0:T(8,128)(2,1)S(1)}, bf16[4,96,768]{2,1,0:T(8,128)(2,1)S(1)}, u32[]{:S(2)}, u32[]{:S(2)}) %collective-permute-start.4) | collective-permute-done | bytes 589856 | tf_op jit(solution)/shard_map/ppermute | solution.py:41
  40.6 4.9 %collective-permute-done.6 = bf16[2,96,768]{2,1,0:T(8,128)(2,1)S(1)} collective-permute-done((bf16[2,96,768]{2,1,0:T(8,128)(2,1)S(1)}, bf16[2,96,768]{2,1,0:T(8,128)(2,1)S(1)}, u32[]{:S(2)}, u32[]{:S(2)}) %collective-permute-start.6) | collective-permute-done | bytes 294944 | tf_op jit(solution)/shard_map/ppermute | solution.py:41
  45.8 5.4 %collective-permute-done.10 = bf16[192,768]{1,0:T(8,128)(2,1)S(1)} collective-permute-done((bf16[192,768]{1,0:T(8,128)(2,1)S(1)}, bf16[192,768]{1,0:T(8,128)(2,1)S(1)}, u32[]{:S(2)}, u32[]{:S(2)}) %collective-permute-start.10) | collective-permute-done | bytes 294944 | tf_op jit(solution)/shard_map/ppermute | solution.py:41
  52.5 2.4 collective-permute-start.7
  54.9 13.9 %collective-permute-done.8.x2 = bf16[192,1024]{1,0:T(8,128)(2,1)S(1)} collective-permute-done((bf16[192,1024]{1,0:T(8,128)(2,1)S(1)}, bf16[192,1024]{1,0:T(8,128)(2,1)S(1)}, u32[]{:S(2)}, u32[]{:S(2)}) %collective-permute-start.8) | collective-permute-done | bytes 393248 | tf_op jit(solution)/shard_map/ppermute | solution.py:41
  68.9 4.1 %collective-permute-done.7.x1 = bf16[192,1024]{1,0:T(8,128)(2,1)S(1)} collective-permute-done((bf16[192,1024]{1,0:T(8,128)(2,1)S(1)}, bf16[192,1024]{1,0:T(8,128)(2,1)S(1)}, u32[]{:S(2)}, u32[]{:S(2)}) %collective-permute-start.7) | collective-permute-done | bytes 393248 | tf_op jit(solution)/shard_map/ppermute | solution.py:41
  73.5 2.5 shard_map.342
  76.2 8.4 %collective-permute-done.9.x3 = bf16[192,1024]{1,0:T(8,128)(2,1)S(1)} collective-permute-done((bf16[192,1024]{1,0:T(8,128)(2,1)S(1)}, bf16[192,1024]{1,0:T(8,128)(2,1)S(1)}, u32[]{:S(2)}, u32[]{:S(2)}) %collective-permute-start.9) | collective-permute-done | bytes 393248 | tf_op jit(solution)/shard_map/ppermute | solution.py:41
  88.4 19.6 %shard_map.343 = (bf16[1024,768]{1,0:T(8,128)(2,1)S(1)}, bf16[4,1024,384]{2,1,0:T(8,128)(2,1)S(1)}, bf16[4,512,256]{2,1,0:T(8,128)(2,1)S(1)}, bf16[4,512,256]{2,...) custom-call(s32[6]{0:T(128)S(1)} %pad_add_fusion.scal, ...), custom_call_target="tpu_custom_call" | custom-call | flops 92000002048 | bytes 276000000 | tf_op jit(solution)/shard_map/pallas_call | solution.py:312
  111.2 29.1 %shard_map.345 = (f32[512,768]{1,0:T(8,128)S(1)}, bf16[128,512]{1,0:T(8,128)(2,1)S(1)}, bf16[4,128,192]{2,1,0:T(8,128)(2,1)S(1)}, f32[8,768]{1,0:T(8,128)S(1)}, ...) custom-call(s32[6]{0:T(128)S(1)} %pad_add_fusion.scal, ...), custom_call_target="tpu_custom_call" | custom-call | flops 120000004096 | bytes 360000000 | tf_op jit(solution)/shard_map/pallas_call | solution.py:497
  140.8 5.0 %shard_map.346 = (f32[512,768]{1,0:T(8,128)S(1)}, bf16[512,768]{1,0:T(8,128)(2,1)S(1)}, f32[8,768]{1,0:T(8,128)S(1)}) custom-call(bf16[4,512,768]{2,1,0:T(8,128)(2,1)S(1)} %get-tuple-element.213.pre_ref, f32[512,768]{1,0:T(8,128)S(1)} %get-tuple-element.214.grad_ref, f32[512,768]{1,0:T(8,128)S(1)} %get-tuple-element.203.unit_ref, ...), custom_call_target="tpu_custom_call" | custom-call | flops 35999997952 | bytes 108000000 | tf_op jit(solution)/shard_map/pallas_call | solution.py:563
  151.5 34.5 %shard_map.347 = (bf16[4,4,112,768]{3,2,1,0:T(8,128)(2,1)S(1)}, bf16[4,4,112,768]{3,2,1,0:T(8,128)(2,1)S(1)}, f32[192,1024]{1,0:T(8,128)S(1)}, f32[192,1024]{1,0...) custom-call(s32[6]{0:T(128)S(1)} %pad_add_fusion.scal, f32[8,1024]{1,0:T(8,128)S(1)} %copy-done.11, ...), custom_call_target="tpu_custom_call" | custom-call | flops 143999991808 | bytes 432000000 | tf_op jit(solution)/shard_map/pallas_call | solution.py:675
  191.5 6.2 %collective-permute-done.32 = bf16[192,1024]{1,0:T(8,128)(2,1)S(1)} collective-permute-done((bf16[192,1024]{1,0:T(8,128)(2,1)S(1)}, bf16[192,1024]{1,0:T(8,128)(2,1)S(1)}, u32[]{:S(2)}, u32[]{:S(2)}) %collective-permute-start.32) | collective-permute-done | bytes 393248 | tf_op jit(solution)/shard_map/ppermute | solution.py:41
  202.0 2.6 %collective-permute-done.31 = bf16[2,192,768]{2,1,0:T(8,128)(2,1)S(1)} collective-permute-done((bf16[2,192,768]{2,1,0:T(8,128)(2,1)S(1)}, bf16[2,192,768]{2,1,0:T(8,128)(2,1)S(1)}, u32[]{:S(2)}, u32[]{:S(2)}) %collective-permute-start.31) | collective-permute-done | bytes 589856 | tf_op jit(solution)/shard_map/ppermute | solution.py:41
  206.1 5.1 %shard_map.348 = f32[2048,128]{1,0:T(8,128)} custom-call(s32[8,2048]{1,0:T(8,128)S(1)} %get-tuple-element.236.order_ref, s32[1,2048]{1,0:T(1,128)S(1)} %bitcast.119, bf16[4,128,512]{2,1,0:T(8,128)(2,1)S(1)} %pad_maximum_fusion.1.vec_ref), custom_call_target="tpu_custom_call" | custom-call | flops 20000000000 | bytes 60000000 | tf_op jit(solution)/shard_map/pallas_call | solution.py:722
  211.6 5.6 %collective-permute-done.36.x1_ref = bf16[192,1024]{1,0:T(8,128)(2,1)S(1)} collective-permute-done((bf16[192,1024]{1,0:T(8,128)(2,1)S(1)}, bf16[192,1024]{1,0:T(8,128)(2,1)S(1)}, u32[]{:S(2)}, u32[]{:S(2)}) %collective-permute-start.36) | collective-permute-done | bytes 393248 | tf_op jit(solution)/shard_map/ppermute | solution.py:41
  223.8 5.5 %shard_map.349 = f32[192,2048]{1,0:T(8,128)} custom-call(s32[8,2048]{1,0:T(8,128)S(1)} %get-tuple-element.236.order_ref, f32[192,1024]{1,0:T(8,128)S(1)} %get-tuple-element.254.x0_ref, bf16[192,1024]{1,0:T(8,128)(2,1)S(1)} %collective-permute-done.36.x1_ref, bf16[192,1024]{1,0:T(8,128)(2,1)S(1)} %collective-permute-done.37.far_ref), custom_call_target="tpu_custom_call" | custom-call | flops 20000000000 | bytes 60000000 | tf_op jit(solution)/shard_map/pallas_call | solution.py:752
  232.7 13.9 %collective-permute-done.42.b_ref = bf16[192,768]{1,0:T(8,128)(2,1)S(1)} collective-permute-done((bf16[192,768]{1,0:T(8,128)(2,1)S(1)}, bf16[192,768]{1,0:T(8,128)(2,1)S(1)}, u32[]{:S(2)}, u32[]{:S(2)}) %collective-permute-start.42) | collective-permute-done | bytes 294944 | tf_op jit(solution)/shard_map/ppermute | solution.py:41
  248.6 6.1 %collective-permute-done.43.b_ref = bf16[112,768]{1,0:T(8,128)(2,1)S(1)} collective-permute-done((bf16[112,768]{1,0:T(8,128)(2,1)S(1)}, bf16[112,768]{1,0:T(8,128)(2,1)S(1)}, u32[]{:S(2)}, u32[]{:S(2)}) %collective-permute-start.43) | collective-permute-done | bytes 172064 | tf_op jit(solution)/shard_map/ppermute | solution.py:41
  (186 shorter events, 51.9 us)
Async XLA Ops:
  25.8 20.0 %collective-permute-start.12 = (bf16[192,768]{1,0:T(8,128)(2,1)S(1)}, bf16[192,768]{1,0:T(8,128)(2,1)S(1)}, u32[]{:S(2)}, u32[]{:S(2)}) collective-permute-start(bf16[192,768]{1,0:T(8,128)(2,1)S(1)} %copy-done.30), channel_id=1, source_target_pairs={{0,3},{1,2},{2,1},{3,0},{4,7},{5,6},{6,5},{7,4},{8,11},{9,10},{10,... | collective-permute-start | bytes 884744 | tf_op jit(solution)/shard_map/ppermute | solution.py:41
  28.3 17.5 %collective-permute-start.11 = (bf16[192,768]{1,0:T(8,128)(2,1)S(1)}, bf16[192,768]{1,0:T(8,128)(2,1)S(1)}, u32[]{:S(2)}, u32[]{:S(2)}) collective-permute-start(bf16[192,768]{1,0:T(8,128)(2,1)S(1)} %copy-done.30), channel_id=1, source_target_pairs={{0,1},{1,0},{2,3},{3,2},{4,5},{5,4},{6,7},{7,6},{8,9},{9,8},{10,11... | collective-permute-start | bytes 884744 | tf_op jit(solution)/shard_map/ppermute | solution.py:41
  28.3 22.9 %collective-permute-start.10 = (bf16[192,768]{1,0:T(8,128)(2,1)S(1)}, bf16[192,768]{1,0:T(8,128)(2,1)S(1)}, u32[]{:S(2)}, u32[]{:S(2)}) collective-permute-start(bf16[192,768]{1,0:T(8,128)(2,1)S(1)} %copy-done.30), channel_id=1, source_target_pairs={{0,2},{1,3},{2,0},{3,1},{4,6},{5,7},{6,4},{7,5},{8,10},{9,11},{10,... | collective-permute-start | bytes 884744 | tf_op jit(solution)/shard_map/ppermute | solution.py:41
  51.3 33.3 %collective-permute-start.14 = (bf16[4,208,768]{2,1,0:T(8,128)(2,1)S(1)}, bf16[4,208,768]{2,1,0:T(8,128)(2,1)S(1)}, u32[]{:S(2)}, u32[]{:S(2)}) collective-permute-start(bf16[4,208,768]{2,1,0:T(8,128)(2,1)S(1)} %maximum_maximum_fusion.refs_0_.refs_8_), channel_id=1, source_target_pairs={{0,16},{4,20},{8,24},{12,28},{16,0},{20,4},{24,8},{28,12},{1,17},{... | collective-permute-start | bytes 3833864 | tf_op jit(solution)/shard_map/ppermute | solution.py:41
  51.8 32.8 %collective-permute-start.13 = (bf16[4,208,768]{2,1,0:T(8,128)(2,1)S(1)}, bf16[4,208,768]{2,1,0:T(8,128)(2,1)S(1)}, u32[]{:S(2)}, u32[]{:S(2)}) collective-permute-start(bf16[4,208,768]{2,1,0:T(8,128)(2,1)S(1)} %maximum_maximum_fusion.refs_0_.refs_8_), channel_id=1, source_target_pairs={{0,8},{4,12},{8,0},{12,4},{16,24},{20,28},{24,16},{28,20},{1,9},{5... | collective-permute-start | bytes 3833864 | tf_op jit(solution)/shard_map/ppermute | solution.py:41
  52.4 16.5 %collective-permute-start.8 = (bf16[192,1024]{1,0:T(8,128)(2,1)S(1)}, bf16[192,1024]{1,0:T(8,128)(2,1)S(1)}, u32[]{:S(2)}, u32[]{:S(2)}) collective-permute-start(bf16[192,1024]{1,0:T(8,128)(2,1)S(1)} %get-tuple-element.166), channel_id=1, source_target_pairs={{0,2},{1,3},{2,0},{3,1},{4,6},{5,7},{6,4},{7,5},{8,10},{9,11},{10,... | collective-permute-start | bytes 1179656 | tf_op jit(solution)/shard_map/ppermute | solution.py:41
  52.4 20.5 %collective-permute-start.18 = (bf16[4,96,768]{2,1,0:T(8,128)(2,1)S(1)}, bf16[4,96,768]{2,1,0:T(8,128)(2,1)S(1)}, u32[]{:S(2)}, u32[]{:S(2)}) collective-permute-start(bf16[4,96,768]{2,1,0:T(8,128)(2,1)S(1)} %constant_dynamic-update-slice_fusion.refs_3_), channel_id=1, source_target_pairs={{0,4},{4,0},{8,12},{12,8},{16,20},{20,16},{24,28},{28,24},{1,5},{5... | collective-permute-start | bytes 1769480 | tf_op jit(solution)/shard_map/ppermute | solution.py:41
  52.5 20.4 %collective-permute-start.7 = (bf16[192,1024]{1,0:T(8,128)(2,1)S(1)}, bf16[192,1024]{1,0:T(8,128)(2,1)S(1)}, u32[]{:S(2)}, u32[]{:S(2)}) collective-permute-start(bf16[192,1024]{1,0:T(8,128)(2,1)S(1)} %get-tuple-element.165.x0), channel_id=1, source_target_pairs={{0,1},{1,0},{2,3},{3,2},{4,5},{5,4},{6,7},{7,6},{8,9},{9,8},{10,11... | collective-permute-start | bytes 1179656 | tf_op jit(solution)/shard_map/ppermute | solution.py:41
  76.0 32.0 %collective-permute-start.21 = (bf16[4,208,768]{2,1,0:T(8,128)(2,1)S(1)}, bf16[4,208,768]{2,1,0:T(8,128)(2,1)S(1)}, u32[]{:S(2)}, u32[]{:S(2)}) collective-permute-start(bf16[4,208,768]{2,1,0:T(8,128)(2,1)S(1)} %maximum_maximum_fusion.refs_0_.refs_8_), channel_id=1, source_target_pairs={{0,4},{4,0},{8,12},{12,8},{16,20},{20,16},{24,28},{28,24},{1,5},{5... | collective-permute-start | bytes 3833864 | tf_op jit(solution)/shard_map/ppermute | solution.py:41
  84.6 23.4 %collective-permute-start.23 = (bf16[4,208,768]{2,1,0:T(8,128)(2,1)S(1)}, bf16[4,208,768]{2,1,0:T(8,128)(2,1)S(1)}, u32[]{:S(2)}, u32[]{:S(2)}) collective-permute-start(bf16[4,208,768]{2,1,0:T(8,128)(2,1)S(1)} %collective-permute-done.14.refs_2_.refs_10_), channel_id=1, source_target_pairs={{0,4},{4,0},{8,12},{12,8},{16,20},{20,16},{24,28},{28,24},{1,5},{5... | collective-permute-start | bytes 3833864 | tf_op jit(solution)/shard_map/ppermute | solution.py:41
  84.8 23.3 %collective-permute-start.22 = (bf16[4,208,768]{2,1,0:T(8,128)(2,1)S(1)}, bf16[4,208,768]{2,1,0:T(8,128)(2,1)S(1)}, u32[]{:S(2)}, u32[]{:S(2)}) collective-permute-start(bf16[4,208,768]{2,1,0:T(8,128)(2,1)S(1)} %collective-permute-done.13.refs_1_.refs_9_), channel_id=1, source_target_pairs={{0,4},{4,0},{8,12},{12,8},{16,20},{20,16},{24,28},{28,24},{1,5},{5... | collective-permute-start | bytes 3833864 | tf_op jit(solution)/shard_map/ppermute | solution.py:41
  85.3 22.7 %collective-permute-start.20 = (bf16[2,208,768]{2,1,0:T(8,128)(2,1)S(1)}, bf16[2,208,768]{2,1,0:T(8,128)(2,1)S(1)}, u32[]{:S(2)}, u32[]{:S(2)}) collective-permute-start(bf16[2,208,768]{2,1,0:T(8,128)(2,1)S(1)} %slice.189), channel_id=1, source_target_pairs={{0,16},{4,20},{8,24},{12,28},{16,0},{20,4},{24,8},{28,12},{1,17},{... | collective-permute-start | bytes 1916936 | tf_op jit(solution)/shard_map/ppermute | solution.py:41
  86.8 21.2 %collective-permute-start.19 = (bf16[2,208,768]{2,1,0:T(8,128)(2,1)S(1)}, bf16[2,208,768]{2,1,0:T(8,128)(2,1)S(1)}, u32[]{:S(2)}, u32[]{:S(2)}) collective-permute-start(bf16[2,208,768]{2,1,0:T(8,128)(2,1)S(1)} %slice.188), channel_id=1, source_target_pairs={{0,8},{4,12},{8,0},{12,4},{16,24},{20,28},{24,16},{28,20},{1,9},{5... | collective-permute-start | bytes 1916936 | tf_op jit(solution)/shard_map/ppermute | solution.py:41
  149.1 36.9 %collective-permute-start.29 = (bf16[2,128,512]{2,1,0:T(8,128)(2,1)S(1)}, bf16[2,128,512]{2,1,0:T(8,128)(2,1)S(1)}, u32[]{:S(2)}, u32[]{:S(2)}) collective-permute-start(bf16[2,128,512]{2,1,0:T(8,128)(2,1)S(1)} %pad_maximum_fusion.2), channel_id=1, source_target_pairs={{0,2},{1,3},{2,0},{3,1},{4,6},{5,7},{6,4},{7,5},{8,10},{9,11},{10,... | collective-permute-start | bytes 786440 | tf_op jit(solution)/shard_map/ppermute | solution.py:41
  150.0 36.0 %collective-permute-start.27 = (bf16[2,2,192,768]{3,2,1,0:T(8,128)(2,1)S(1)}, bf16[2,2,192,768]{3,2,1,0:T(8,128)(2,1)S(1)}, u32[]{:S(2)}, u32[]{:S(2)}) collective-permute-start(bf16[2,2,192,768]{3,2,1,0:T(8,128)(2,1)S(1)} %fusion), channel_id=1, source_target_pairs={{0,8},{4,12},{8,0},{12,4},{16,24},{20,28},{24,16},{28,20},{1,9},{5... | collective-permute-start | bytes 3538952 | tf_op jit(solution)/shard_map/ppermute | solution.py:41
  150.6 35.4 %collective-permute-start.28 = (bf16[2,2,192,768]{3,2,1,0:T(8,128)(2,1)S(1)}, bf16[2,2,192,768]{3,2,1,0:T(8,128)(2,1)S(1)}, u32[]{:S(2)}, u32[]{:S(2)}) collective-permute-start(bf16[2,2,192,768]{3,2,1,0:T(8,128)(2,1)S(1)} %fusion.1), channel_id=1, source_target_pairs={{0,16},{4,20},{8,24},{12,28},{16,0},{20,4},{24,8},{28,12},{1,17},{... | collective-permute-start | bytes 3538952 | tf_op jit(solution)/shard_map/ppermute | solution.py:41
  188.3 16.2 %collective-permute-start.31 = (bf16[2,192,768]{2,1,0:T(8,128)(2,1)S(1)}, bf16[2,192,768]{2,1,0:T(8,128)(2,1)S(1)}, u32[]{:S(2)}, u32[]{:S(2)}) collective-permute-start(bf16[2,192,768]{2,1,0:T(8,128)(2,1)S(1)} %get-tuple-element.280), channel_id=1, source_target_pairs={{0,8},{4,12},{8,0},{12,4},{16,24},{20,28},{24,16},{28,20},{1,9},{5... | collective-permute-start | bytes 1769480 | tf_op jit(solution)/shard_map/ppermute | solution.py:41
  189.9 21.3 %collective-permute-start.30 = (bf16[2,192,768]{2,1,0:T(8,128)(2,1)S(1)}, bf16[2,192,768]{2,1,0:T(8,128)(2,1)S(1)}, u32[]{:S(2)}, u32[]{:S(2)}) collective-permute-start(bf16[2,192,768]{2,1,0:T(8,128)(2,1)S(1)} %get-tuple-element.281), channel_id=1, source_target_pairs={{0,16},{4,20},{8,24},{12,28},{16,0},{20,4},{24,8},{28,12},{1,17},{... | collective-permute-start | bytes 1769480 | tf_op jit(solution)/shard_map/ppermute | solution.py:41
  197.6 19.6 %collective-permute-start.36 = (bf16[192,1024]{1,0:T(8,128)(2,1)S(1)}, bf16[192,1024]{1,0:T(8,128)(2,1)S(1)}, u32[]{:S(2)}, u32[]{:S(2)}) collective-permute-start(bf16[192,1024]{1,0:T(8,128)(2,1)S(1)} %get-tuple-element.248), channel_id=1, source_target_pairs={{0,1},{1,0},{2,3},{3,2},{4,5},{5,4},{6,7},{7,6},{8,9},{9,8},{10,11... | collective-permute-start | bytes 1179656 | tf_op jit(solution)/shard_map/ppermute | solution.py:41
  199.4 19.5 %collective-permute-start.37 = (bf16[192,1024]{1,0:T(8,128)(2,1)S(1)}, bf16[192,1024]{1,0:T(8,128)(2,1)S(1)}, u32[]{:S(2)}, u32[]{:S(2)}) collective-permute-start(bf16[192,1024]{1,0:T(8,128)(2,1)S(1)} %add_convert_fusion.4), channel_id=1, source_target_pairs={{0,2},{1,3},{2,0},{3,1},{4,6},{5,7},{6,4},{7,5},{8,10},{9,11},{10,... | collective-permute-start | bytes 1179656 | tf_op jit(solution)/shard_map/ppermute | solution.py:41
  200.7 18.2 %collective-permute-start.34 = (bf16[2,2,112,768]{3,2,1,0:T(8,128)(2,1)S(1)}, bf16[2,2,112,768]{3,2,1,0:T(8,128)(2,1)S(1)}, u32[]{:S(2)}, u32[]{:S(2)}) collective-permute-start(bf16[2,2,112,768]{3,2,1,0:T(8,128)(2,1)S(1)} %fusion.8), channel_id=1, source_target_pairs={{0,8},{4,12},{8,0},{12,4},{16,24},{20,28},{24,16},{28,20},{1,9},{5... | collective-permute-start | bytes 2064392 | tf_op jit(solution)/shard_map/ppermute | solution.py:41
  204.6 15.9 %collective-permute-start.35 = (bf16[2,2,112,768]{3,2,1,0:T(8,128)(2,1)S(1)}, bf16[2,2,112,768]{3,2,1,0:T(8,128)(2,1)S(1)}, u32[]{:S(2)}, u32[]{:S(2)}) collective-permute-start(bf16[2,2,112,768]{3,2,1,0:T(8,128)(2,1)S(1)} %fusion.9), channel_id=1, source_target_pairs={{0,16},{4,20},{8,24},{12,28},{16,0},{20,4},{24,8},{28,12},{1,17},{... | collective-permute-start | bytes 2064392 | tf_op jit(solution)/shard_map/ppermute | solution.py:41
  211.5 17.8 %collective-permute-start.40 = (bf16[2,192,768]{2,1,0:T(8,128)(2,1)S(1)}, bf16[2,192,768]{2,1,0:T(8,128)(2,1)S(1)}, u32[]{:S(2)}, u32[]{:S(2)}) collective-permute-start(bf16[2,192,768]{2,1,0:T(8,128)(2,1)S(1)} %fusion.5), channel_id=1, source_target_pairs={{0,1},{1,0},{2,3},{3,2},{4,5},{5,4},{6,7},{7,6},{8,9},{9,8},{10,11... | collective-permute-start | bytes 1769480 | tf_op jit(solution)/shard_map/ppermute | solution.py:41
  229.8 16.8 %collective-permute-start.41 = (bf16[2,112,768]{2,1,0:T(8,128)(2,1)S(1)}, bf16[2,112,768]{2,1,0:T(8,128)(2,1)S(1)}, u32[]{:S(2)}, u32[]{:S(2)}) collective-permute-start(bf16[2,112,768]{2,1,0:T(8,128)(2,1)S(1)} %fusion.11), channel_id=1, source_target_pairs={{0,1},{1,0},{2,3},{3,2},{4,5},{5,4},{6,7},{7,6},{8,9},{9,8},{10,11... | collective-permute-start | bytes 1032200 | tf_op jit(solution)/shard_map/ppermute | solution.py:41
  (53 other events, 602.3 us)
